TPU v7x, 32 devices: a whole 2x2x4 slice. The times are simulated.
32 devices in a mesh: grp: 2 (over x), line: 16 (over z, y, core).
Axes of the slice: x: 2, y: 2, z: 4, core: 2. Of those that a mesh axis runs over, the one named last changes fastest.
Arguments:
- ptdf: bfloat16 [4096, 13824], P('line'), may hold values from -0.109375 to 0.109375
- load: bfloat16 [13824, 256], P('line', 'grp'), parts along dimension 1, may hold values from 0 to 0.29882812
- unit_bus: int32 [1024], replicated, may hold values from 0 to 13823
- min_up: int32 [1024], P('line'), may hold values from 2 to 31
- gen_max: float32 [1024], P('line'), may hold values from 0.5 to 2
- cost_gen: float32 [1024], P('line'), may hold values from 0.5 to 5
- cost_commit: float32 [1024], P('line'), may hold values from 0.5 to 5
- cost_start: float32 [1024], P('line'), may hold values from 0.5 to 5
- init_commit: float32 [1024], P('line'), may hold values from 0 to 1
- line_limit: float32 [4096], P('line'), may hold values from 0.1 to 1
- gen: float32 [1024, 256], P('line', 'grp'), parts along dimension 1, may hold values from 0 to 1
- commit: float32 [1024, 256], P('line', 'grp'), parts along dimension 1, may hold values from 0 to 1
- startup: float32 [1024, 256], P('line', 'grp'), parts along dimension 1, may hold values from 0 to 0.5
- line_dual: float32 [4096, 256], P('line', 'grp'), parts along dimension 1, may hold values from -6 to 6
- balance_dual: float32 [256], P(('grp', 'line')), parts along dimension 0, may hold values from -6 to 6
- cap_dual: float32 [1024, 256], P('line', 'grp'), parts along dimension 1, may hold values from 0 to 1
- start_dual: float32 [1024, 256], P('line', 'grp'), parts along dimension 1, may hold values from 0 to 1
- window_dual: float32 [1024, 256], P('line', 'grp'), parts along dimension 1, may hold values from 0 to 1
Outputs:
- gen_out: float32 [1024, 256], P('line', 'grp'), parts along dimension 1
- commit_out: float32 [1024, 256], P('line', 'grp'), parts along dimension 1
- startup_out: float32 [1024, 256], P('line', 'grp'), parts along dimension 1
- line_dual_out: float32 [4096, 256], P('line', 'grp'), parts along dimension 1
- balance_dual_out: float32 [256], P(('grp', 'line')), parts along dimension 0
- cap_dual_out: float32 [1024, 256], P('line', 'grp'), parts along dimension 1
- start_dual_out: float32 [1024, 256], P('line', 'grp'), parts along dimension 1
- window_dual_out: float32 [1024, 256], P('line', 'grp'), parts along dimension 1
There are 2 independent parts, one for each index of `grp`. A program takes and returns all parts, laid end to end along the dimension named above; an argument that names none is the same for every part. Nothing has to cross between parts.
All inputs are finite; a program needn't handle non-finite values.
Results may differ from a plain program's by a relative error of at most 0.00054.
Values may be sent and summed in bfloat16 or wider, within the bound.
No kernel may reach another device: no remote copies, remote signals or barrier semaphores. Data moves between devices by JAX's collectives and lax.ppermute only.
A program may use at most 64 MiB of HBM per device.

v0:
```python
import jax
import jax.numpy as jnp
from jax import lax
from jax.sharding import PartitionSpec as P

ITERS = 2


TAU_STEP = 0.05
SIGMA_STEP = 0.5


def prefix_sums(values):
    zeros_column = jnp.zeros((values.shape[0], 1), jnp.float32)
    return jnp.concatenate([zeros_column, jnp.cumsum(values, axis=1)], axis=1)


def window_indices(min_up, periods):
    positions = jnp.broadcast_to(
        jnp.arange(periods, dtype=jnp.int32)[None, :], (min_up.shape[0], periods)
    )
    spans = min_up[:, None]
    lower_end = jnp.maximum(positions + 1 - spans, 0)
    upper_end = jnp.minimum(positions + spans, periods)
    return (positions, lower_end, upper_end)


def window_forward(values, positions, lower_end):
    sums = prefix_sums(values)
    return jnp.take_along_axis(sums, positions + 1, axis=1) - jnp.take_along_axis(
        sums, lower_end, axis=1
    )


def window_backward(values, positions, upper_end):
    sums = prefix_sums(values)
    return jnp.take_along_axis(sums, upper_end, axis=1) - jnp.take_along_axis(
        sums, positions, axis=1
    )


def primal_update(
    gen,
    commit,
    startup,
    adjoint_gen,
    start_dual,
    window_dual,
    gen_max,
    cost_gen,
    cost_commit,
    cost_start,
    cap_dual,
    positions,
    upper_end,
):
    zeros_column = jnp.zeros((start_dual.shape[0], 1), jnp.float32)
    later_start = jnp.concatenate([start_dual[:, 1:], zeros_column], axis=1)
    grad_gen = cost_gen[:, None] + adjoint_gen
    grad_commit = (
        cost_commit[:, None] - gen_max[:, None] * cap_dual + start_dual - later_start - window_dual
    )
    grad_start = (
        cost_start[:, None] - start_dual + window_backward(window_dual, positions, upper_end)
    )
    new_gen = jnp.clip(gen - TAU_STEP * grad_gen, 0.0, gen_max[:, None])
    new_commit = jnp.clip(commit - TAU_STEP * grad_commit, 0.0, 1.0)
    new_start = jnp.clip(startup - TAU_STEP * grad_start, 0.0, 1.0)
    return (new_gen, new_commit, new_start)


def unit_dual_update(
    bar_gen,
    bar_commit,
    bar_start,
    cap_dual,
    start_dual,
    window_dual,
    gen_max,
    init_commit,
    positions,
    lower_end,
):
    new_cap = jnp.maximum(0.0, cap_dual + SIGMA_STEP * (bar_gen - gen_max[:, None] * bar_commit))
    previous = jnp.concatenate([init_commit[:, None], bar_commit[:, :-1]], axis=1)
    new_start = jnp.maximum(0.0, start_dual + SIGMA_STEP * (bar_commit - previous - bar_start))
    new_window = jnp.maximum(
        0.0,
        window_dual + SIGMA_STEP * (window_forward(bar_start, positions, lower_end) - bar_commit),
    )
    return (new_cap, new_start, new_window)


def line_update(line_dual, flows, line_limit):
    shifted = line_dual + SIGMA_STEP * flows
    limits = line_limit[:, None]
    return shifted - SIGMA_STEP * jnp.clip(shifted / SIGMA_STEP, -limits, limits)


def on_device(
    ptdf,
    load,
    unit_bus,
    min_up,
    gen_max,
    cost_gen,
    cost_commit,
    cost_start,
    init_commit,
    line_limit,
    gen,
    commit,
    startup,
    line_dual,
    balance_dual,
    cap_dual,
    start_dual,
    window_dual,
):
    unit_dev, periods = gen.shape
    devices = lax.axis_size("line")
    unit_count = unit_dev * devices
    period_dev = periods // devices
    unit_cols = jnp.take(ptdf, unit_bus, axis=1)
    add_piece = lax.all_gather(load, "line", axis=0, tiled=True)
    add_flow_part = jnp.dot(ptdf, add_piece, preferred_element_type=jnp.float32)
    demand_part = jnp.sum(add_piece.astype(jnp.float32), axis=0)
    own_demand = lax.dynamic_slice_in_dim(
        demand_part, lax.axis_index("line") * period_dev, period_dev
    )
    positions, lower_end, upper_end = window_indices(min_up, periods)
    own_columns = lax.all_to_all(unit_cols, "line", split_axis=1, concat_axis=0, tiled=True)
    for step in range(ITERS):
        dual_half = line_dual.astype(jnp.bfloat16)
        weighted = lax.dot_general(
            own_columns,
            lax.all_gather(dual_half, "line", axis=0, tiled=True),
            (((0,), (0,)), ((), ())),
            preferred_element_type=jnp.float32,
        )
        balance_all = lax.all_gather(balance_dual, "line", axis=0, tiled=True)
        adjoint_gen = weighted + balance_all[None, :] + cap_dual
        new_gen, new_commit, new_start = primal_update(
            gen,
            commit,
            startup,
            adjoint_gen,
            start_dual,
            window_dual,
            gen_max,
            cost_gen,
            cost_commit,
            cost_start,
            cap_dual,
            positions,
            upper_end,
        )
        bar_gen = 2.0 * new_gen - gen
        bar_commit = 2.0 * new_commit - commit
        bar_start = 2.0 * new_start - startup
        bar_half = bar_gen.astype(jnp.bfloat16)
        piece = lax.all_gather(bar_half, "line", axis=0, tiled=True)
        flow_part = jnp.dot(unit_cols, piece, preferred_element_type=jnp.float32)
        total_part = jnp.sum(piece.astype(jnp.float32), axis=0)
        own_totals = lax.dynamic_slice_in_dim(
            total_part, lax.axis_index("line") * period_dev, period_dev
        )
        flows = flow_part - add_flow_part
        line_dual = line_update(line_dual, flows, line_limit)
        balance_dual = balance_dual + (own_totals - own_demand) / unit_count
        cap_dual, start_dual, window_dual = unit_dual_update(
            bar_gen,
            bar_commit,
            bar_start,
            cap_dual,
            start_dual,
            window_dual,
            gen_max,
            init_commit,
            positions,
            lower_end,
        )
        gen, commit, startup = (new_gen, new_commit, new_start)
    return (gen, commit, startup, line_dual, balance_dual, cap_dual, start_dual, window_dual)


def solution(mesh):
    in_specs = (
        P("line", None),
        P("line", "grp"),
        P(),
        P("line"),
        P("line"),
        P("line"),
        P("line"),
        P("line"),
        P("line"),
        P("line"),
        P("line", "grp"),
        P("line", "grp"),
        P("line", "grp"),
        P("line", "grp"),
        P(("grp", "line")),
        P("line", "grp"),
        P("line", "grp"),
        P("line", "grp"),
    )
    out_specs = (
        P("line", "grp"),
        P("line", "grp"),
        P("line", "grp"),
        P("line", "grp"),
        P(("grp", "line")),
        P("line", "grp"),
        P("line", "grp"),
        P("line", "grp"),
    )
    return jax.shard_map(
        on_device, mesh=mesh, in_specs=in_specs, out_specs=out_specs, check_vma=False
    )
```

profile of v0, /device:TPU:0, one launch (start us, length us, event | category | flops | bytes accessed | tf_op | source)
XLA Modules:
  0.0 693.9 jit_solution(9594438777631026581)
XLA Ops:
  7.2 0.0 all-gather.4.cloned.1.call-start
  7.2 1.5 convert_element_type.21
  8.8 0.0 all-gather.4.cloned.1.call-update
  8.8 0.0 all-gather.6.cloned.1.call-start
  8.8 0.7 all-gather.6.cloned.1.call-update
  9.5 0.0 copy-start.16
  9.5 10.3 %copy.38 = bf16[256,13824]{0,1:T(8,128)(2,1)} copy(bf16[256,13824]{1,0:T(8,128)(2,1)} %param.20) | data formatting | bytes 14155776 | tf_op args[0]
  19.9 0.1 broadcast_in_dim.58
  19.9 7.4 %gather_fusion = bf16[1024,256]{1,0:T(8,128)(2,1)S(1)} fusion(bf16[256,13824]{0,1:T(8,128)(2,1)} %copy.38, s32[1024]{0:T(1024)S(1)} %fusion.63), kind=kCustom, calls=%fused_computation.8 | custom fusion | bytes 1052672 | tf_op jit(solution)/shard_map/jit(_take)/gather | solution.py:124
  27.4 1.0 broadcast_select_fusion
  28.4 7.4 %all-to-all-start = ((bf16[256,16,64]{0,2,1:T(8,128)(2,1)}), bf16[256,16,64]{0,2,1:T(8,128)(2,1)S(1)}, u32[]{:S(2)}, u32[]{:S(2)}) async-start(bf16[256,16,64]{0,2,1:T(8,128)(2,1)} %broadcast_select_fusion), calls=%async_computation | async-start | bytes 1048576 | tf_op jit(solution)/shard_map/all_to_all | solution.py:132
  35.8 0.0 all-gather.8.cloned.1.call-start
  35.8 0.3 reduce_window_sum.22
  36.1 0.1 concatenate.26
  36.3 0.1 fusion.35
  36.4 65.0 %gather_fusion.1 = f32[8192]{0:T(1024)S(1)} fusion(f32[64,129]{1,0:T(8,128)S(1)} %concatenate.26, s32[8192]{0:T(1024)S(1)} %get-tuple-element.29), kind=kCustom, calls=%fused_computation.clone | custom fusion | bytes 131072 | tf_op jit(solution)/shard_map/jit(take_along_axis)/gather | solution.py:37
  101.4 0.0 copy-start.19
  101.4 65.0 %gather_fusion.2 = f32[8192]{0:T(1024)S(1)} fusion(f32[64,129]{1,0:T(8,128)S(1)} %concatenate.26, s32[8192]{0:T(1024)S(1)} %fusion.31), kind=kCustom, calls=%fused_computation.1.clone | custom fusion | bytes 131072 | tf_op jit(solution)/shard_map/jit(take_along_axis)/gather | solution.py:37
  166.4 0.1 slice.12
  166.5 0.1 multiply_subtract_fusion.5
  166.6 0.3 reduce_window_sum.23
  166.9 0.1 concatenate.28
  167.0 65.0 %gather_fusion.3 = f32[8192]{0:T(1024)S(1)} fusion(f32[64,129]{1,0:T(8,128)S(1)} %concatenate.28, s32[8192]{0:T(1024)S(1)} %get-tuple-element.27), kind=kCustom, calls=%fused_computation.2.clone | custom fusion | bytes 131072 | tf_op jit(solution)/shard_map/jit(take_along_axis)/gather | solution.py:30
  232.0 0.0 copy-start.10
  232.0 0.0 copy-start.20
  232.1 65.0 %gather_fusion.4 = f32[8192]{0:T(1024)S(1)} fusion(f32[64,129]{1,0:T(8,128)S(1)} %concatenate.28, s32[8192]{0:T(1024)S(1)} %get-tuple-element.28), kind=kCustom, calls=%fused_computation.3.clone | custom fusion | bytes 131072 | tf_op jit(solution)/shard_map/jit(take_along_axis)/gather | solution.py:30
  297.1 0.1 fusion.53
  297.2 0.3 reduce_window_sum.27
  297.5 0.1 concatenate.29
  297.6 65.0 %gather_fusion.5 = f32[8192]{0:T(1024)S(1)} fusion(f32[64,129]{1,0:T(8,128)S(1)} %concatenate.29, s32[8192]{0:T(1024)S(1)} %get-tuple-element.29), kind=kCustom, calls=%fused_computation.4.clone | custom fusion | bytes 131072 | tf_op jit(solution)/shard_map/jit(take_along_axis)/gather | solution.py:37
  362.6 0.0 copy-start.24
  362.6 65.0 %gather_fusion.6 = f32[8192]{0:T(1024)S(1)} fusion(f32[64,129]{1,0:T(8,128)S(1)} %concatenate.29, s32[8192]{0:T(1024)S(1)} %fusion.31), kind=kCustom, calls=%fused_computation.5.clone | custom fusion | bytes 131072 | tf_op jit(solution)/shard_map/jit(take_along_axis)/gather | solution.py:37
  427.6 0.1 copy.40
  427.7 0.7 multiply_subtract_fusion.2
  428.5 0.6 copy-done.8
  429.1 0.3 reduce_window_sum.32
  429.4 0.1 concatenate.31
  429.4 65.0 %gather_fusion.7 = f32[8192]{0:T(1024)S(1)} fusion(f32[64,129]{1,0:T(8,128)S(1)} %concatenate.31, s32[8192]{0:T(1024)S(1)} %get-tuple-element.27), kind=kCustom, calls=%fused_computation.6.clone | custom fusion | bytes 131072 | tf_op jit(solution)/shard_map/jit(take_along_axis)/gather | solution.py:30
  494.5 0.0 copy-start.22
  494.5 0.0 copy-start.26
  494.5 0.0 copy-start.25
  494.5 0.0 copy-start.13
  494.5 65.0 %gather_fusion.8 = f32[8192]{0:T(1024)S(1)} fusion(f32[64,129]{1,0:T(8,128)S(1)} %concatenate.31, s32[8192]{0:T(1024)S(1)} %get-tuple-element.28), kind=kCustom, calls=%fused_computation.7.clone | custom fusion | bytes 131072 | tf_op jit(solution)/shard_map/jit(take_along_axis)/gather | solution.py:30
  559.5 0.1 slice.35
  559.6 0.5 neg.5
  560.1 0.6 dynamic-slice
  561.4 0.2 dynamic-update-slice
  561.6 33.8 %all-reduce.6 = f32[128]{0:T(128)S(1)} all-reduce(f32[128]{0:T(128)S(1)} %dynamic-update-slice), channel_id=1, replica_groups=mesh['grp'=2,'line'=16] {'line'}, use_global_device_ids=true, to_apply=%add.6 | all-reduce | flops 128 | bytes 1024
  595.5 0.0 all-gather.4.cloned.1.call-done
  595.6 2.4 fusion.48
  597.9 19.4 %all_gather.23 = bf16[1024,128]{1,0:T(8,128)(2,1)} all-gather(bf16[64,128]{1,0:T(8,128)(2,1)S(1)} %get-tuple-element.25), channel_id=1, replica_groups=mesh['grp'=2,'line'=16] {'line'}, dimensions={0}, use_global_device_ids=true | all-gather | bytes 278528 | tf_op jit(solution)/shard_map/all_gather | solution.py:162
  617.4 6.3 fusion.71
  623.7 1.2 fusion.70
  625.0 0.0 all-gather.8.cloned.1.call-update
  625.0 1.1 convert_reduce_fusion.2
  626.1 1.9 convert_reduce_fusion
  628.0 0.8 fusion.69
  628.8 31.5 %all-reduce.7 = f32[128]{0:T(128)S(1)} all-reduce(f32[128]{0:T(128)S(1)} %get-tuple-element.21), channel_id=1, replica_groups=mesh['grp'=2,'line'=16] {'line'}, use_global_device_ids=true, to_apply=%add.7 | all-reduce | flops 128 | bytes 1024
  660.3 1.4 all-gather.8.cloned.1.call-done
  661.7 2.4 add_maximum_fusion
  664.1 20.2 %all_gather.27 = bf16[1024,128]{1,0:T(8,128)(2,1)S(1)} all-gather(bf16[64,128]{1,0:T(8,128)(2,1)S(1)} %get-tuple-element.24), channel_id=1, replica_groups=mesh['grp'=2,'line'=16] {'line'}, dimensions={0}, use_global_device_ids=true | all-gather | bytes 278528 | tf_op jit(solution)/shard_map/all_gather | solution.py:162
  684.3 0.1 convert_reduce_fusion.1
  684.4 2.3 multiply_subtract_fusion
  686.8 0.6 multiply_add_fusion
  (54 shorter events, 0.2 us)
Async XLA Ops:
  7.2 588.4 %all-gather.4.cloned.1.call-start = ((), (), s32[]{:S(2)}) async-start(), calls=%async_computation.1 | async-start | bytes 1114112 | tf_op jit(solution)/shard_map/all_gather | solution.py:137
  8.8 608.5 %all-gather.6.cloned.1.call-start = ((), (), s32[]{:S(2)}) async-start(), calls=%async_computation.2 | async-start | bytes 3760128 | tf_op jit(solution)/shard_map/all_gather | solution.py:125
  9.5 10.3 %copy-start.16 = (s32[1024]{0:T(1024)S(1)}, s32[1024]{0:T(1024)}, u32[]{:S(2)}) copy-start(s32[1024]{0:T(1024)} %param.22) | copy-start | bytes 12292
  19.8 16.0 %copy-start.11 = (f32[64,128]{1,0:T(8,128)S(1)}, f32[64,128]{1,0:T(8,128)}, u32[]{:S(2)}) copy-start(f32[64,128]{1,0:T(8,128)} %param.37) | copy-start | bytes 98308
  19.8 16.4 %copy-start.17 = (s32[64]{0:T(128)S(1)}, s32[64]{0:T(128)}, u32[]{:S(2)}) copy-start(s32[64]{0:T(128)} %param.23) | copy-start | bytes 772
  27.4 8.4 %copy-start.2 = (bf16[1024,256]{1,0:T(8,128)(2,1)}, bf16[1024,256]{1,0:T(8,128)(2,1)S(1)}, u32[]{:S(2)}) copy-start(bf16[1024,256]{1,0:T(8,128)(2,1)S(1)} %gather_fusion) | copy-start | bytes 1572868
  28.4 567.0 %all-to-all-start = ((bf16[256,16,64]{0,2,1:T(8,128)(2,1)}), bf16[256,16,64]{0,2,1:T(8,128)(2,1)S(1)}, u32[]{:S(2)}, u32[]{:S(2)}) async-start(bf16[256,16,64]{0,2,1:T(8,128)(2,1)} %broadcast_select_fusion), calls=%async_computation | async-start | bytes 1048576 | tf_op jit(solution)/shard_map/all_to_all | solution.py:132
  35.8 625.9 %all-gather.8.cloned.1.call-start = ((), (), s32[]{:S(2)}) async-start(), calls=%async_computation.3 | async-start | bytes 1114112 | tf_op jit(solution)/shard_map/all_gather | solution.py:137
  101.4 65.0 %copy-start.6 = (f32[64,128]{1,0:T(8,128)S(1)}, f32[64,128]{1,0:T(8,128)}, u32[]{:S(2)}) copy-start(f32[64,128]{1,0:T(8,128)} %param.36) | copy-start | bytes 98308
  101.4 65.1 %copy-start.15 = (f32[64,128]{1,0:T(8,128)S(1)}, f32[64,128]{1,0:T(8,128)}, u32[]{:S(2)}) copy-start(f32[64,128]{1,0:T(8,128)} %param.32) | copy-start | bytes 98308
  101.4 65.1 %copy-start.19 = (f32[64]{0:T(128)S(1)}, f32[64]{0:T(128)}, u32[]{:S(2)}) copy-start(f32[64]{0:T(128)} %param.27) | copy-start | bytes 772
  232.0 65.1 %copy-start.10 = (f32[64,128]{1,0:T(8,128)S(1)}, f32[64,128]{1,0:T(8,128)}, u32[]{:S(2)}) copy-start(f32[64,128]{1,0:T(8,128)} %param.35) | copy-start | bytes 98308
  232.0 65.1 %copy-start.14 = (f32[64,128]{1,0:T(8,128)S(1)}, f32[64,128]{1,0:T(8,128)}, u32[]{:S(2)}) copy-start(f32[64,128]{1,0:T(8,128)} %param.31) | copy-start | bytes 98308
  232.0 65.1 %copy-start.18 = (f32[64]{0:T(128)S(1)}, f32[64]{0:T(128)}, u32[]{:S(2)}) copy-start(f32[64]{0:T(128)} %param.24) | copy-start | bytes 772
  232.0 65.1 %copy-start.20 = (f32[64]{0:T(128)S(1)}, f32[64]{0:T(128)}, u32[]{:S(2)}) copy-start(f32[64]{0:T(128)} %param.26) | copy-start | bytes 772
  362.6 65.0 %copy-start.24 = (f32[64]{0:T(128)S(1)}, f32[64]{0:T(128)}, u32[]{:S(2)}) copy-start(f32[64]{0:T(128)} %param.28) | copy-start | bytes 772
  427.7 0.7 copy-start.7
  428.5 0.6 copy-start.8
  428.5 167.1 %copy-start.5 = (f32[64,128]{1,0:T(8,128)}, f32[64,128]{1,0:T(8,128)S(1)}, u32[]{:S(2)}) copy-start(f32[64,128]{1,0:T(8,128)S(1)} %get-tuple-element.15) | copy-start | bytes 98308
  494.5 65.2 %copy-start.22 = (f32[256]{0:T(256)S(1)}, f32[256]{0:T(256)}, u32[]{:S(2)}) copy-start(f32[256]{0:T(256)} %param.29) | copy-start | bytes 3076
  494.5 65.7 %copy-start.26 = (u32[32]{0:T(128)S(1)}, u32[32]{0:T(128)}, u32[]{:S(2)}) copy-start(u32[32]{0:T(128)} %constant.183) | copy-start | bytes 388
  494.5 66.9 %copy-start.25 = (f32[8]{0:T(128)S(1)}, f32[8]{0:T(128)}, u32[]{:S(2)}) copy-start(f32[8]{0:T(128)} %param.34) | copy-start | bytes 100
  494.5 101.0 %copy-start.13 = (f32[64,128]{1,0:T(8,128)S(1)}, f32[64,128]{1,0:T(8,128)}, u32[]{:S(2)}) copy-start(f32[64,128]{1,0:T(8,128)} %param.30) | copy-start | bytes 98308
  494.5 101.0 %copy-start.21 = (f32[64]{0:T(128)S(1)}, f32[64]{0:T(128)}, u32[]{:S(2)}) copy-start(f32[64]{0:T(128)} %param.25) | copy-start | bytes 772
  595.5 21.8 %copy-start.1 = (bf16[16,8,8,256]{3,2,0,1:T(8,128)(2,1)}, bf16[16,8,8,256]{3,2,0,1:T(8,128)(2,1)S(1)}, u32[]{:S(2)}) copy-start(bf16[16,8,8,256]{3,2,0,1:T(8,128)(2,1)S(1)} %copy.42) | copy-start | bytes 1572868
  617.3 6.4 copy-start.3
  617.3 6.4 copy-start.4
  617.3 6.4 copy-start.12
  617.3 6.4 copy-start.23
  617.4 8.7 %copy-start = (bf16[13824,128]{1,0:T(8,128)(2,1)S(1)}, bf16[13824,128]{1,0:T(8,128)(2,1)}, u32[]{:S(2)}) copy-start(bf16[13824,128]{1,0:T(8,128)(2,1)} %all-gather.6.cloned.1.call-done) | copy-start | bytes 10616836
  623.7 1.3 copy-start.9
Sparse Core Ops, SparseCore 0:
  10.7 43.6 all-gather.3
  56.7 45.7 all-gather.5
  625.1 36.5 all-gather.7
where the time goes:
time: 695 us; the launch traced here: 694 us
  local copies, waits for them, and re-layouts  540 us (78%)
  blocking collectives  105 us (15%)
  between operations  14.9 us (2%)
  matrix products  14.6 us (2%)
  other arithmetic  9.8 us (1%)
  starting transfers between devices  7.48 us (1%)
    gather x2, local copies, waits for them, and re-layouts, window_forward(): jnp.take_along_axis(sums, positions + 1, axis=1)  130 us
    gather x2, local copies, waits for them, and re-layouts, window_backward(): jnp.take_along_axis(sums, upper_end, axis=1)  130 us
    gather x2, local copies, waits for them, and re-layouts, window_backward(): jnp.take_along_axis(sums, positions, axis=1)  130 us
    gather x2, local copies, waits for them, and re-layouts, window_forward(): jnp.take_along_axis(sums, lower_end, axis=1)  130 us
    unnamed x2, blocking collectives  65.3 us
    all_gather x2, blocking collectives, on_device(): piece = lax.all_gather(bar_half, 'line', axis=0, tiled=True)  39.6 us
  transfers between devices with their start and end apart: 4, of which 1 were waited for; matrix products, arithmetic and copies ran while one was open for 79% of the time, Pallas kernels for 0%

commit v1 on v0

v1 whole, which is shorter than its diff:
```python
import functools

import jax
import jax.numpy as jnp
from jax import lax
from jax.experimental import pallas as pl
from jax.experimental.pallas import tpu as pltpu
from jax.sharding import PartitionSpec as P

ITERS = 2
TAU = 0.05
SIGMA = 0.5
SPAN_BITS = 5

F32 = jnp.float32
BF16 = jnp.bfloat16
VMEM = pl.BlockSpec(memory_space=pltpu.VMEM)


def shift_right(values, amount):
    lanes = lax.broadcasted_iota(jnp.int32, values.shape, 1)
    return jnp.where(lanes >= amount, pltpu.roll(values, amount, 1), 0.0)


def shift_left(values, amount):
    periods = values.shape[1]
    lanes = lax.broadcasted_iota(jnp.int32, values.shape, 1)
    return jnp.where(lanes < periods - amount, pltpu.roll(values, periods - amount, 1), 0.0)


def window_sum(values, spans, shift):
    block = values
    total = jnp.zeros_like(values)
    for bit in range(SPAN_BITS):
        chosen = (lax.shift_right_logical(spans, bit) & 1) == 1
        total = jnp.where(chosen, block + shift(total, 1 << bit), total)
        if bit + 1 < SPAN_BITS:
            block = block + shift(block, 1 << bit)
    return total


def ahead_kernel(par, spans_ref, commit, startup, cap, start, window,
                 commit1, bar_commit1, start1, window1, startup2, grad2, bar_start2, reach2):
    gen_max, cost_commit, cost_start, init = (par[:, i:i + 1] for i in (0, 2, 3, 4))
    spans = jnp.broadcast_to(spans_ref[...], commit.shape)
    lanes = lax.broadcasted_iota(jnp.int32, commit.shape, 1)
    c0, s0, sd0, wd0 = commit[...], startup[...], start[...], window[...]
    grad_c = cost_commit - gen_max * cap[...] + sd0 - shift_left(sd0, 1) - wd0
    grad_s = cost_start - sd0 + window_sum(wd0, spans, shift_left)
    c1 = jnp.clip(c0 - TAU * grad_c, 0.0, 1.0)
    s1 = jnp.clip(s0 - TAU * grad_s, 0.0, 1.0)
    bc1 = 2.0 * c1 - c0
    bs1 = 2.0 * s1 - s0
    before = jnp.where(lanes == 0, init, pltpu.roll(bc1, 1, 1))
    sd1 = jnp.maximum(0.0, sd0 + SIGMA * (bc1 - before - bs1))
    wd1 = jnp.maximum(0.0, wd0 + SIGMA * (window_sum(bs1, spans, shift_right) - bc1))
    grad_s2 = cost_start - sd1 + window_sum(wd1, spans, shift_left)
    s2 = jnp.clip(s1 - TAU * grad_s2, 0.0, 1.0)
    bs2 = 2.0 * s2 - s1
    commit1[...] = c1
    bar_commit1[...] = bc1
    start1[...] = sd1
    window1[...] = wd1
    startup2[...] = s2
    grad2[...] = cost_commit + sd1 - shift_left(sd1, 1) - wd1
    bar_start2[...] = bs2
    reach2[...] = window_sum(bs2, spans, shift_right)


def columns_kernel(bus, ptdf, cols_t, cols, acc):
    step = pl.program_id(0)
    depth = ptdf.shape[1]
    here = bus[...] - step * depth
    hot = (lax.broadcasted_iota(jnp.int32, (bus.shape[0], depth), 1) == here).astype(F32).astype(BF16)
    part = lax.dot_general(hot, ptdf[...], (((1,), (1,)), ((), ())), preferred_element_type=F32)

    @pl.when(step == 0)
    def _():
        acc[...] = part

    @pl.when(step > 0)
    def _():
        acc[...] += part

    @pl.when(step == pl.num_programs(0) - 1)
    def _():
        total = acc[...]
        cols_t[...] = total.astype(BF16)
        cols[...] = total.T.astype(BF16)


def load_kernel(ptdf, load, flow, demand):
    step = pl.program_id(0)
    block = load[...]
    part = jnp.dot(ptdf[...], block, preferred_element_type=F32)
    rows = jnp.sum(block.astype(F32).reshape(-1, 8, block.shape[1]), axis=0)

    @pl.when(step == 0)
    def _():
        flow[...] = part
        demand[...] = rows

    @pl.when(step > 0)
    def _():
        flow[...] += part
        demand[...] += rows


def adjoint_kernel(cols_t, line_dual, balance, part):
    part[...] = (
        jnp.dot(cols_t[...], line_dual[...].astype(BF16), preferred_element_type=F32) + balance[...]
    )


def gen_step(parts, gen, cap, par):
    gen_max, cost_gen = par[:, 0:1], par[:, 1:2]
    weighted = parts[0]
    for i in range(1, parts.shape[0]):
        weighted = weighted + parts[i]
    g0 = gen[...]
    g1 = jnp.clip(g0 - TAU * (cost_gen + (weighted + cap[...])), 0.0, gen_max)
    return g1, 2.0 * g1 - g0


def gen1_kernel(parts, gen, cap, bar_commit, par, spread, gen_out, cap_out):
    g1, bar = gen_step(parts, gen, cap, par)
    half = bar.astype(BF16)
    for i in range(spread.shape[0]):
        spread[i] = half
    gen_out[...] = g1
    cap_out[...] = jnp.maximum(0.0, cap[...] + SIGMA * (bar - par[:, 0:1] * bar_commit[...]))


def gen2_kernel(parts, gen, cap, par, commit, start, window, grad, bar_start, reach,
                spread, gen_out, commit_out, cap_out, start_out, window_out):
    g2, bar = gen_step(parts, gen, cap, par)
    half = bar.astype(BF16)
    for i in range(spread.shape[0]):
        spread[i] = half
    gen_out[...] = g2
    gen_max, init = par[:, 0:1], par[:, 4:5]
    lanes = lax.broadcasted_iota(jnp.int32, gen.shape, 1)
    cap1, c1 = cap[...], commit[...]
    c2 = jnp.clip(c1 - TAU * (grad[...] - gen_max * cap1), 0.0, 1.0)
    bc2 = 2.0 * c2 - c1
    before = jnp.where(lanes == 0, init, pltpu.roll(bc2, 1, 1))
    commit_out[...] = c2
    cap_out[...] = jnp.maximum(0.0, cap1 + SIGMA * (bar - gen_max * bc2))
    start_out[...] = jnp.maximum(0.0, start[...] + SIGMA * (bc2 - before - bar_start[...]))
    window_out[...] = jnp.maximum(0.0, window[...] + SIGMA * (reach[...] - bc2))


def line_step(cols, bars, flow, dual, limit):
    flows = jnp.dot(cols[...], bars[...], preferred_element_type=F32) - flow[...]
    shifted = dual[...] + SIGMA * flows
    bound = limit[...]
    return shifted - SIGMA * jnp.clip(shifted / SIGMA, -bound, bound)


def balance_step(bars, demand, balance):
    totals = jnp.sum(bars[...].astype(F32).reshape(-1, 8, bars.shape[1]), axis=0)
    change = jnp.sum(totals - demand[...], axis=0, keepdims=True)
    return balance[...] + change / bars.shape[0]


def line1_kernel(cols, cols_t, bars, flow, demand, dual, limit, balance, own,
                 part, dual_out, balance_out):
    new = line_step(cols, bars, flow, dual, limit)
    dual_out[...] = new
    moved = balance_step(bars, demand, balance) * own[...]
    balance_out[...] = moved
    part[...] = jnp.dot(cols_t[...], new.astype(BF16), preferred_element_type=F32) + moved


def line2_kernel(cols, bars, flow, demand, dual, limit, balance, dual_out, balance_out):
    dual_out[...] = line_step(cols, bars, flow, dual, limit)
    balance_out[...] = balance_step(bars, demand, balance)


def call(kernel, outs, *args, cost=None):
    shapes = [jax.ShapeDtypeStruct(shape, dtype) for shape, dtype in outs]
    return pl.pallas_call(
        kernel,
        out_shape=shapes,
        in_specs=[VMEM] * len(args),
        out_specs=[VMEM] * len(shapes),
        cost_estimate=cost,
    )(*args)


def block_depth(buses, most):
    return max(d for d in range(128, most + 1, 128) if buses % d == 0)


def on_device(
    ptdf, load, unit_bus, min_up, gen_max, cost_gen, cost_commit, cost_start, init_commit,
    line_limit, gen, commit, startup, line_dual, balance_dual, cap_dual, start_dual, window_dual,
):
    unit_dev, periods = gen.shape
    lines, buses = ptdf.shape
    units = unit_bus.shape[0]
    devices = lax.axis_size("line")
    period_dev = periods // devices
    me = lax.axis_index("line")
    every_load = lax.all_gather(load, "line", axis=0, tiled=True)

    par = jnp.stack(
        [gen_max, cost_gen, cost_commit, cost_start, init_commit, gen_max, gen_max, gen_max], axis=1
    )
    limit = line_limit[:, None]
    places = lax.broadcasted_iota(jnp.int32, (1, periods), 1)
    own = (places // period_dev == me).astype(F32)
    balance = jnp.tile(balance_dual, devices)[None, :] * own

    depth = block_depth(buses, 1536)
    cols_t, cols = pl.pallas_call(
        columns_kernel,
        grid=(buses // depth,),
        out_shape=[
            jax.ShapeDtypeStruct((units, lines), BF16),
            jax.ShapeDtypeStruct((lines, units), BF16),
        ],
        in_specs=[
            pl.BlockSpec((units, 1), lambda k: (0, 0)),
            pl.BlockSpec((lines, depth), lambda k: (0, k)),
        ],
        out_specs=[
            pl.BlockSpec((units, lines), lambda k: (0, 0)),
            pl.BlockSpec((lines, units), lambda k: (0, 0)),
        ],
        scratch_shapes=[pltpu.VMEM((units, lines), F32)],
    )(unit_bus[:, None], ptdf)

    square = (unit_dev, periods)
    parts = call(adjoint_kernel, [((units, periods), F32)], cols_t, line_dual, balance)[0]
    parts = lax.all_to_all(parts, "line", 0, 0, tiled=True).reshape(devices, *square)
    commit1, bar_commit1, start1, window1, startup2, grad2, bar_start2, reach2 = call(
        ahead_kernel, [(square, F32)] * 8, par, min_up[:, None], commit, startup, cap_dual,
        start_dual, window_dual,
    )
    spread, gen1, cap1 = call(
        gen1_kernel, [((devices, *square), BF16)] + [(square, F32)] * 2,
        parts, gen, cap_dual, bar_commit1, par,
    )
    bars = lax.all_to_all(spread, "line", 0, 0).reshape(units, periods)

    depth = block_depth(buses, 1536)
    flow, demand = pl.pallas_call(
        load_kernel,
        grid=(buses // depth,),
        out_shape=[
            jax.ShapeDtypeStruct((lines, periods), F32),
            jax.ShapeDtypeStruct((8, periods), F32),
        ],
        in_specs=[
            pl.BlockSpec((lines, depth), lambda k: (0, k)),
            pl.BlockSpec((depth, periods), lambda k: (k, 0)),
        ],
        out_specs=[
            pl.BlockSpec((lines, periods), lambda k: (0, 0)),
            pl.BlockSpec((8, periods), lambda k: (0, 0)),
        ],
    )(ptdf, every_load)

    parts, dual1, balance1 = call(
        line1_kernel,
        [((units, periods), F32), ((lines, periods), F32), ((1, periods), F32)],
        cols, cols_t, bars, flow, demand, line_dual, limit, balance, own,
    )
    parts = lax.all_to_all(parts, "line", 0, 0, tiled=True).reshape(devices, *square)
    spread, gen2, commit2, cap2, start2, window2 = call(
        gen2_kernel, [((devices, *square), BF16)] + [(square, F32)] * 5,
        parts, gen1, cap1, par, commit1, start1, window1, grad2, bar_start2, reach2,
    )
    bars = lax.all_to_all(spread, "line", 0, 0).reshape(units, periods)
    dual2, balance2 = call(
        line2_kernel, [((lines, periods), F32), ((1, periods), F32)],
        cols, bars, flow, demand, dual1, limit, balance1,
    )
    balance_out = lax.dynamic_slice_in_dim(balance2[0], me * period_dev, period_dev)
    return (gen2, commit2, startup2, dual2, balance_out, cap2, start2, window2)


def solution(mesh):
    wide = P("line", "grp")
    unit = P("line")
    both = P(("grp", "line"))
    in_specs = (
        P("line", None), wide, P(), unit, unit, unit, unit, unit, unit, unit,
        wide, wide, wide, wide, both, wide, wide, wide,
    )
    out_specs = (wide, wide, wide, wide, both, wide, wide, wide)
    return jax.shard_map(
        on_device, mesh=mesh, in_specs=in_specs, out_specs=out_specs, check_vma=False
    )
```

time: 695 us -> 126 us (0.18)
  local copies, waits for them, and re-layouts: 540 us -> 8.15 us
  blocking collectives: 105 us -> 20.4 us
  Pallas kernels: 0 us -> 35.4 us
  waiting for transfers between devices: 2.15 us -> 24.8 us
  matrix products: 14.6 us -> 0 us
  starting transfers between devices: 7.48 us -> 21.3 us
  other arithmetic: 9.8 us -> 1.04 us
    gather x9 -> x0, local copies, waits for them, and re-layouts: 527 us -> none  [the longest x2 130 us: window_forward(): jnp.take_along_axis(sums, positions + 1, axis=1)]
    unnamed x2 -> x0, blocking collectives: 65.3 us -> none
    all_gather x2 -> x0, blocking collectives: 39.6 us -> none  [on_device(): piece = lax.all_gather(bar_half, 'line', axis=0, tiled=True)]
    pallas_call x0 -> x8, Pallas kernels: none -> 35.4 us  [the longest x6 13.8 us: call(): pl.pallas_call(kernel, out_shape=shapes, in_specs=[VMEM] * len(args), out...]
    all_to_all x1 -> x3, waiting for transfers between devices: 0.01 us -> 24.1 us  [the longest x1 14.1 us: on_device(): lax.all_to_all(parts, 'line', 0, 0, tiled=True).reshape(devices, *square)]
    all_to_all x0 -> x1, blocking collectives: none -> 20.4 us  [on_device(): lax.all_to_all(parts, 'line', 0, 0, tiled=True).reshape(devices, *square)]
    dot_general x5 -> x0, matrix products: 14.6 us -> none  [the longest x1 6.3 us: on_device(): add_flow_part = jnp.dot(ptdf, add_piece, preferred_element_type=jnp.float32)]
    all_to_all x1 -> x3, starting transfers between devices: 7.36 us -> 21.3 us  [the longest x2 13.8 us: on_device(): bars = lax.all_to_all(spread, 'line', 0, 0).reshape(units, periods)]
  transfers between devices with their start and end apart: 4 -> 4, of which waited for: 1 -> 2; matrix products, arithmetic and copies ran while one was open for 79% -> 5% of each run, Pallas kernels for 0% -> 23%
where the time goes in v1:
time: 126 us; the launch traced here: 125 us
  Pallas kernels  35.4 us (28%)
  waiting for transfers between devices  24.8 us (20%)
  starting transfers between devices  21.3 us (17%)
  blocking collectives  20.4 us (16%)
  between operations  14.2 us (11%)
  local copies, waits for them, and re-layouts  8.15 us (6%)
    all_to_all x1, blocking collectives, on_device(): lax.all_to_all(parts, 'line', 0, 0, tiled=True).reshape(devices, *square)  20.4 us
    all_to_all x1, waiting for transfers between devices, on_device(): lax.all_to_all(parts, 'line', 0, 0, tiled=True).reshape(devices, *square)  14.1 us
    pallas_call x6, Pallas kernels, call(): pl.pallas_call(kernel, out_shape=shapes, in_specs=[VMEM] * len(args), out...  13.8 us
    all_to_all x2, starting transfers between devices, on_device(): bars = lax.all_to_all(spread, 'line', 0, 0).reshape(units, periods)  13.8 us
    pallas_call x1, Pallas kernels, on_device(): pl.pallas_call(columns_kernel, grid=(buses // depth,), out_shape=[jax.Sha...  12.7 us
    all_to_all x2, waiting for transfers between devices, on_device(): bars = lax.all_to_all(spread, 'line', 0, 0).reshape(units, periods)  10 us
    pallas_call x1, Pallas kernels, on_device(): pl.pallas_call(load_kernel, grid=(buses // depth,), out_shape=[jax.ShapeD...  8.84 us
    all_to_all x1, starting transfers between devices, on_device(): lax.all_to_all(parts, 'line', 0, 0, tiled=True).reshape(devices, *square)  7.45 us
  transfers between devices with their start and end apart: 4, of which 2 were waited for; matrix products, arithmetic and copies ran while one was open for 5% of the time, Pallas kernels for 23%

profile of v1, /device:TPU:0, one launch (start us, length us, event | category | flops | bytes accessed | tf_op | source)
XLA Modules:
  0.0 125.3 jit_solution(17190624666098645724)
XLA Ops:
  7.2 0.0 copy-start.9
  7.2 0.0 copy-start.8
  7.2 0.0 copy-start.7
  7.2 0.0 copy-start.6
  7.2 0.0 copy-start.3
  7.2 0.0 copy-start.5
  7.2 0.0 copy-start.4
  7.2 0.0 all-gather.2.cloned.1.call-start
  7.3 0.7 all-gather.2.cloned.1.call-update
  8.0 0.7 tile.2
  8.6 0.1 broadcast_in_dim_tile.3
  8.7 1.7 %copy.47.bus = s32[1024,1]{1,0:T(8,128)} copy(s32[1024,1]{0,1:T(1,128)} %bitcast.22) | data formatting | bytes 8192 | tf_op jit(solution)/shard_map/broadcast_in_dim | solution.py:232
  10.5 12.7 %shard_map.233 = (bf16[1024,256]{1,0:T(8,128)(2,1)}, bf16[256,1024]{1,0:T(8,128)(2,1)}) custom-call(s32[1024,1]{1,0:T(8,128)} %copy.47.bus, bf16[256,13824]{1,0:T(8,128)(2,1)} %ptdf.3), custom_call_target="tpu_custom_call" | custom-call | tf_op jit(solution)/shard_map/pallas_call | solution.py:216
  23.2 0.5 compare_select_fusion.balance
  23.7 2.2 %shard_map.234 = f32[1024,128]{1,0:T(8,128)} custom-call(bf16[1024,256]{1,0:T(8,128)(2,1)} %get-tuple-element.35.cols_t, f32[256,128]{1,0:T(8,128)} %dual.1, f32[1,128]{1,0:T(1,128)} %compare_select_fusion.balance), custom_call_target="tpu_custom_call" | custom-call | tf_op jit(solution)/shard_map/pallas_call | solution.py:182
  25.9 7.4 %all-to-all-start = ((f32[16,64,128]{2,1,0:T(8,128)}), f32[16,64,128]{2,1,0:T(8,128)S(1)}, u32[]{:S(2)}, u32[]{:S(2)}) async-start(f32[16,64,128]{2,1,0:T(8,128)} %bitcast.14), calls=%async_computation | async-start | bytes 1048576 | tf_op jit(solution)/shard_map/all_to_all | solution.py:236
  33.4 0.0 copy-done.9
  33.4 0.0 copy-done.8
  33.4 0.0 copy-done.7
  33.4 0.0 copy-done.6
  33.4 0.0 copy-done.3
  33.5 0.7 copy.48.par
  34.2 0.0 copy-done.5
  34.2 0.7 copy.49.spans_ref
  34.9 2.7 %shard_map.235 = (f32[64,128]{1,0:T(8,128)}, f32[64,128]{1,0:T(8,128)}, f32[64,128]{1,0:T(8,128)}, f32[64,128]{1,0:T(8,128)}, f32[64,128]{1,0:T(8,128)}, /*index...) custom-call(f32[64,8]{1,0:T(8,128)} %copy.48.par, s32[64,1]{1,0:T(8,128)} %copy.49.spans_ref, f32[64,128]{1,0:T(8,128)} %commit.1, ...), custom_call_target="tpu_custom_call" | custom-call | tf_op jit(solution)/shard_map/pallas_call | solution.py:182
  37.6 14.1 %all-to-all-done.parts = f32[16,64,128]{2,1,0:T(8,128)S(1)} async-done(((f32[16,64,128]{2,1,0:T(8,128)}), f32[16,64,128]{2,1,0:T(8,128)S(1)}, u32[]{:S(2)}, u32[]{:S(2)}) %all-to-all-start) | async-done | bytes 524320 | tf_op jit(solution)/shard_map/all_to_all | solution.py:236
  51.7 0.0 copy-start
  51.7 0.8 copy-done
  52.5 1.9 %shard_map.236 = (bf16[16,64,128]{2,1,0:T(8,128)(2,1)}, f32[64,128]{1,0:T(8,128)}, f32[64,128]{1,0:T(8,128)}) custom-call(f32[16,64,128]{2,1,0:T(8,128)} %copy-done, f32[64,128]{1,0:T(8,128)} %gen.1, f32[64,128]{1,0:T(8,128)} %cap.3, f32[64,128]{1,0:T(8,128)} %get-tuple-element.36.bar_commit, f32[64,8]{1,0:T(8,128)} %copy.48.par), custom_call_target="tpu_custom_call" | custom-call | tf_op jit(solution)/shard_map/pallas_call | solution.py:182
  54.5 9.7 %all-to-all-start.1 = ((bf16[16,64,128]{2,1,0:T(8,128)(2,1)}), bf16[16,64,128]{2,1,0:T(8,128)(2,1)S(1)}, u32[]{:S(2)}, u32[]{:S(2)}) async-start(bf16[16,64,128]{2,1,0:T(8,128)(2,1)} %get-tuple-element.37), calls=%async_computation.1 | async-start | bytes 524288 | tf_op jit(solution)/shard_map/all_to_all | solution.py:245
  64.1 0.0 copy-done.4
  64.1 0.8 copy.51.limit
  64.9 0.5 compare_convert_fusion.own
  65.4 0.0 all-gather.2.cloned.1.call-done.load
  65.4 8.8 %shard_map.237 = (f32[256,128]{1,0:T(8,128)}, f32[8,128]{1,0:T(8,128)}) custom-call(bf16[256,13824]{1,0:T(8,128)(2,1)} %ptdf.3, bf16[13824,128]{1,0:T(8,128)(2,1)} %all-gather.2.cloned.1.call-done.load), custom_call_target="tpu_custom_call" | custom-call | tf_op jit(solution)/shard_map/pallas_call | solution.py:248
  74.3 0.0 all-to-all-done.1
  74.3 0.0 copy-start.2
  74.3 0.7 copy-done.2
  75.0 2.8 %shard_map.238 = (f32[1024,128]{1,0:T(8,128)}, f32[256,128]{1,0:T(8,128)}, f32[1,128]{1,0:T(1,128)}) custom-call(bf16[256,1024]{1,0:T(8,128)(2,1)} %get-tuple-element.34.cols, bf16[1024,256]{1,0:T(8,128)(2,1)} %get-tuple-element.35.cols_t, bf16[1024,128]{1,0:T(8,128)(2,1)} %bitcast.16, f32[256,128]{1,0:T(8,128)} %get-tuple-element.38.flow, ...), custom_call_target="tpu_custom_call" | custom-call | tf_op jit(solution)/shard_map/pallas_call | solution.py:182
  77.8 20.4 %all_to_all.28.parts = f32[16,64,128]{2,1,0:T(8,128)} all-to-all(f32[16,64,128]{2,1,0:T(8,128)} %bitcast.17), channel_id=1, replica_groups=mesh['grp'=2,'line'=16] {'line'}, dimensions={0} | all-to-all | bytes 1048576 | tf_op jit(solution)/shard_map/all_to_all | solution.py:270
  98.2 2.0 %shard_map.239 = (bf16[16,64,128]{2,1,0:T(8,128)(2,1)}, f32[64,128]{1,0:T(8,128)}, f32[64,128]{1,0:T(8,128)}, f32[64,128]{1,0:T(8,128)}, f32[64,128]{1,0:T(8,128)}, /*index=5*/f32[64,128]{1,0:T(8,128)}) custom-call(f32[16,64,128]{2,1,0:T(8,128)} %all_to_all.28.parts, f32[64,128]{1,0:T(8,128)} %get-tuple-element.41.gen, f32[64,128]{1,0:T(8,128)} %get-tuple-element.42.cap, ...), custom_call_target="tpu_custom_call" | custom-call | tf_op jit(solution)/shard_map/pallas_call | solution.py:182
  100.1 4.2 %all-to-all-start.3 = ((bf16[16,64,128]{2,1,0:T(8,128)(2,1)}), bf16[16,64,128]{2,1,0:T(8,128)(2,1)S(1)}, u32[]{:S(2)}, u32[]{:S(2)}) async-start(bf16[16,64,128]{2,1,0:T(8,128)(2,1)} %get-tuple-element.52), calls=%async_computation.3 | async-start | bytes 524288 | tf_op jit(solution)/shard_map/all_to_all | solution.py:275
  104.3 10.0 %all-to-all-done.3 = bf16[16,64,128]{2,1,0:T(8,128)(2,1)S(1)} async-done(((bf16[16,64,128]{2,1,0:T(8,128)(2,1)}), bf16[16,64,128]{2,1,0:T(8,128)(2,1)S(1)}, u32[]{:S(2)}, u32[]{:S(2)}) %all-to-all-start.3) | async-done | bytes 262176 | tf_op jit(solution)/shard_map/all_to_all | solution.py:275
  114.3 0.0 copy-start.1
  114.3 0.7 copy-done.1
  115.0 2.2 %shard_map.240 = (f32[256,128]{1,0:T(8,128)}, f32[1,128]{1,0:T(1,128)}) custom-call(bf16[256,1024]{1,0:T(8,128)(2,1)} %get-tuple-element.34.cols, bf16[1024,128]{1,0:T(8,128)(2,1)} %bitcast.15, f32[256,128]{1,0:T(8,128)} %get-tuple-element.38.flow, f32[8,128]{1,0:T(8,128)} %get-tuple-element.39.demand, f32[256,128]{1,0:T(8,128)} %get-tuple-element.53.dual, ...), custom_call_target="tpu_custom_call" | custom-call | tf_op jit(solution)/shard_map/pallas_call | solution.py:182
  117.2 1.2 dynamic-slice_bitcast_fusion
  (1 shorter events, 0.0 us)
Async XLA Ops:
  7.2 26.2 %copy-start.9 = (f32[64]{0:T(128)S(1)}, f32[64]{0:T(128)}, u32[]{:S(2)}) copy-start(f32[64]{0:T(128)} %param.26) | copy-start | bytes 772
  7.2 26.2 %copy-start.8 = (f32[64]{0:T(128)S(1)}, f32[64]{0:T(128)}, u32[]{:S(2)}) copy-start(f32[64]{0:T(128)} %param.25) | copy-start | bytes 772
  7.2 26.2 %copy-start.7 = (f32[64]{0:T(128)S(1)}, f32[64]{0:T(128)}, u32[]{:S(2)}) copy-start(f32[64]{0:T(128)} %param.24) | copy-start | bytes 772
  7.2 26.2 %copy-start.6 = (f32[64]{0:T(128)S(1)}, f32[64]{0:T(128)}, u32[]{:S(2)}) copy-start(f32[64]{0:T(128)} %param.23) | copy-start | bytes 772
  7.2 26.2 %copy-start.3 = (f32[64]{0:T(128)S(1)}, f32[64]{0:T(128)}, u32[]{:S(2)}) copy-start(f32[64]{0:T(128)} %param.22) | copy-start | bytes 772
  7.2 26.9 %copy-start.5 = (s32[64]{0:T(128)S(1)}, s32[64]{0:T(128)}, u32[]{:S(2)}) copy-start(s32[64]{0:T(128)} %param.21) | copy-start | bytes 772
  7.2 56.9 %copy-start.4 = (f32[256]{0:T(256)S(1)}, f32[256]{0:T(256)}, u32[]{:S(2)}) copy-start(f32[256]{0:T(256)} %param.27) | copy-start | bytes 3076
  7.2 58.2 %all-gather.2.cloned.1.call-start = ((), (), s32[]{:S(2)}) async-start(), calls=%async_computation.4 | async-start | bytes 3760128 | tf_op jit(solution)/shard_map/all_gather | solution.py:205
  25.9 25.8 %all-to-all-start = ((f32[16,64,128]{2,1,0:T(8,128)}), f32[16,64,128]{2,1,0:T(8,128)S(1)}, u32[]{:S(2)}, u32[]{:S(2)}) async-start(f32[16,64,128]{2,1,0:T(8,128)} %bitcast.14), calls=%async_computation | async-start | bytes 1048576 | tf_op jit(solution)/shard_map/all_to_all | solution.py:236
  51.7 0.8 copy-start
  54.5 19.8 %all-to-all-start.1 = ((bf16[16,64,128]{2,1,0:T(8,128)(2,1)}), bf16[16,64,128]{2,1,0:T(8,128)(2,1)S(1)}, u32[]{:S(2)}, u32[]{:S(2)}) async-start(bf16[16,64,128]{2,1,0:T(8,128)(2,1)} %get-tuple-element.37), calls=%async_computation.1 | async-start | bytes 524288 | tf_op jit(solution)/shard_map/all_to_all | solution.py:245
  74.3 0.7 copy-start.2
  100.1 14.2 %all-to-all-start.3 = ((bf16[16,64,128]{2,1,0:T(8,128)(2,1)}), bf16[16,64,128]{2,1,0:T(8,128)(2,1)S(1)}, u32[]{:S(2)}, u32[]{:S(2)}) async-start(bf16[16,64,128]{2,1,0:T(8,128)(2,1)} %get-tuple-element.52), calls=%async_computation.3 | async-start | bytes 524288 | tf_op jit(solution)/shard_map/all_to_all | solution.py:275
  114.3 0.7 copy-start.1
Sparse Core Ops, SparseCore 0:
  10.3 54.1 all-gather.1

commit v2 on v1

v2 whole, which is shorter than its diff:
```python
import jax
import jax.numpy as jnp
from jax import lax
from jax.experimental import pallas as pl
from jax.experimental.pallas import tpu as pltpu
from jax.sharding import Mesh, PartitionSpec as P

ITERS = 2
TAU = 0.05
SIGMA = 0.5
SPAN_BITS = 5

F32 = jnp.float32
BF16 = jnp.bfloat16
LINE = ("chip", "core")
SWAP = [(0, 1), (1, 0)]
VMEM = pl.BlockSpec(memory_space=pltpu.VMEM)
SMEM = pl.BlockSpec(memory_space=pltpu.SMEM)

LIMIT, GEN_MAX, COST_GEN, BALANCE = 0, 1, 2, 3


def shift_right(values, amount):
    lanes = lax.broadcasted_iota(jnp.int32, values.shape, 1)
    return jnp.where(lanes >= amount, pltpu.roll(values, amount, 1), 0.0)


def shift_left(values, amount):
    periods = values.shape[1]
    lanes = lax.broadcasted_iota(jnp.int32, values.shape, 1)
    return jnp.where(lanes < periods - amount, pltpu.roll(values, periods - amount, 1), 0.0)


def window_sum(values, spans, shift):
    block = values
    total = jnp.zeros_like(values)
    for bit in range(SPAN_BITS):
        chosen = (lax.shift_right_logical(spans, bit) & 1) == 1
        total = jnp.where(chosen, block + shift(total, 1 << bit), total)
        if bit + 1 < SPAN_BITS:
            block = block + shift(block, 1 << bit)
    return total


def diagonal(rows, columns):
    shape = (rows, columns)
    return lax.broadcasted_iota(jnp.int32, shape, 0) == lax.broadcasted_iota(jnp.int32, shape, 1)


def to_column(row):
    size = row.shape[1]
    return jnp.sum(jnp.where(diagonal(size, size), row, 0.0), axis=1, keepdims=True)


def to_row(column):
    size = column.shape[0]
    return jnp.sum(jnp.where(diagonal(size, size), column, 0.0), axis=0, keepdims=True)


def half_of(values, core):
    half = values.shape[0] // 2
    return jnp.where(core == 0, values[:half], values[half:])


def by_core(mine, other, core):
    return jnp.where(
        core == 0,
        jnp.concatenate([mine, other], axis=1),
        jnp.concatenate([other, mine], axis=1),
    )


def rows_kernel(place, limit, gen_max, cost_gen, balance, out):
    core, chip = place[0], place[1]
    wide = out.shape[1]

    def put(row):
        return jnp.concatenate([row, jnp.zeros((1, wide - row.shape[1]), F32)], axis=1)

    units, periods = gen_max.shape[1], balance.shape[1]
    out[...] = jnp.zeros_like(out)
    out[LIMIT:LIMIT + 1] = limit[...]
    out[GEN_MAX:GEN_MAX + 1] = pltpu.roll(put(gen_max[...]), core * units, 1)
    out[COST_GEN:COST_GEN + 1] = pltpu.roll(put(cost_gen[...]), core * units, 1)
    out[BALANCE:BALANCE + 1] = pltpu.roll(put(balance[...]), (2 * chip + core) * periods, 1)


def ahead_kernel(par, spans_ref, gen, commit, startup, cap, start, window,
                 pack, commit1, start1, window1, startup2, grad2, bar_start2, reach2):
    gen_max, cost_commit, cost_start, init = (par[:, i:i + 1] for i in range(4))
    spans = jnp.broadcast_to(spans_ref[...], commit.shape)
    lanes = lax.broadcasted_iota(jnp.int32, commit.shape, 1)
    c0, s0, sd0, wd0 = commit[...], startup[...], start[...], window[...]
    grad_c = cost_commit - gen_max * cap[...] + sd0 - shift_left(sd0, 1) - wd0
    grad_s = cost_start - sd0 + window_sum(wd0, spans, shift_left)
    c1 = jnp.clip(c0 - TAU * grad_c, 0.0, 1.0)
    s1 = jnp.clip(s0 - TAU * grad_s, 0.0, 1.0)
    bc1 = 2.0 * c1 - c0
    bs1 = 2.0 * s1 - s0
    before = jnp.where(lanes == 0, init, pltpu.roll(bc1, 1, 1))
    sd1 = jnp.maximum(0.0, sd0 + SIGMA * (bc1 - before - bs1))
    wd1 = jnp.maximum(0.0, wd0 + SIGMA * (window_sum(bs1, spans, shift_right) - bc1))
    grad_s2 = cost_start - sd1 + window_sum(wd1, spans, shift_left)
    s2 = jnp.clip(s1 - TAU * grad_s2, 0.0, 1.0)
    bs2 = 2.0 * s2 - s1
    units = gen.shape[0]
    pack[0:units] = gen[...]
    pack[units:2 * units] = cap[...]
    pack[2 * units:3 * units] = bc1
    commit1[...] = c1
    start1[...] = sd1
    window1[...] = wd1
    startup2[...] = s2
    grad2[...] = cost_commit + sd1 - shift_left(sd1, 1) - wd1
    bar_start2[...] = bs2
    reach2[...] = window_sum(bs2, spans, shift_right)


def columns_kernel(bus, ptdf, cols, acc):
    step = pl.program_id(0)
    depth = ptdf.shape[1]
    here = bus[...] - step * depth
    places = lax.broadcasted_iota(jnp.int32, (depth, bus.shape[1]), 0)
    hot = jnp.where(places == here, 1.0, 0.0).astype(BF16)
    part = jnp.dot(ptdf[...], hot, preferred_element_type=F32)

    @pl.when(step == 0)
    def _():
        acc[...] = part

    @pl.when(step > 0)
    def _():
        acc[...] += part

    @pl.when(step == pl.num_programs(0) - 1)
    def _():
        cols[...] = acc[...].astype(BF16)


def put_parts(part, dual, cols_m, cols_o, balance):
    lines = cols_m.shape[0]
    half = dual.astype(BF16)
    total = jnp.dot(half[:, :lines], cols_m[...], preferred_element_type=F32)
    total += jnp.dot(half[:, lines:], cols_o[...], preferred_element_type=F32)
    total += balance
    wide = part.shape[2]
    for i in range(part.shape[0]):
        part[i] = total[:, i * wide:(i + 1) * wide]


def adjoint_kernel(place, cols_m, cols_o, dual_m, dual_o, rows_m, rows_o, part, dual_t, balance):
    core = place[0]
    periods = dual_m.shape[1]
    dual = jnp.concatenate([half_of(dual_m[...].T, core), half_of(dual_o[...].T, core)], axis=1)
    dual_t[...] = dual
    row = rows_m[BALANCE:BALANCE + 1, :periods] + rows_o[BALANCE:BALANCE + 1, :periods]
    column = half_of(to_column(row), core)
    balance[...] = column
    put_parts(part, dual, cols_m, cols_o, column)


def gen_step(parts, gen, cap, rows_m, rows_o):
    wide = gen.shape[1]

    def row(i):
        return rows_m[i:i + 1, :wide] + rows_o[i:i + 1, :wide]

    weighted = parts[0]
    for i in range(1, parts.shape[0]):
        weighted = weighted + parts[i]
    gen_max = row(GEN_MAX)
    g1 = jnp.clip(gen - TAU * (row(COST_GEN) + (weighted + cap)), 0.0, gen_max)
    return g1, 2.0 * g1 - gen, gen_max


def gen1_kernel(place, parts, pack_m, pack_o, rows_m, rows_o, spread, state):
    core = place[0]
    units = pack_m.shape[0] // 3

    def turned(i):
        rows = slice(i * units, (i + 1) * units)
        return by_core(half_of(pack_m[rows].T, core), half_of(pack_o[rows].T, core), core)

    cap = turned(1)
    g1, bar, gen_max = gen_step(parts, turned(0), cap, rows_m, rows_o)
    half = bar.astype(BF16)
    for i in range(spread.shape[0]):
        spread[i] = half
    state[0] = g1
    state[1] = jnp.maximum(0.0, cap + SIGMA * (bar - gen_max * turned(2)))


def gen2_kernel(parts, state, rows_m, rows_o, spread, gen_out):
    g2, bar, _ = gen_step(parts, state[0], state[1], rows_m, rows_o)
    half = bar.astype(BF16)
    for i in range(spread.shape[0]):
        spread[i] = half
    gen_out[...] = g2


def own_units(mine, other, core):
    units = mine.shape[1] // 2
    here, there = mine.T, other.T
    here = jnp.where(core == 0, here[:units], here[units:])
    there = jnp.where(core == 0, there[:units], there[units:])
    return by_core(here, there, core)


def late_kernel(place, par, state_m, state_o, commit, start, window, grad, bar_start, reach,
                gen1, cap1, bar_commit, commit_out, start_out, window_out):
    core = place[0]
    gen_max, init = par[:, 0:1], par[:, 3:4]
    cap = own_units(state_m[1], state_o[1], core)
    gen1[...] = own_units(state_m[0], state_o[0], core)
    cap1[...] = cap
    lanes = lax.broadcasted_iota(jnp.int32, commit.shape, 1)
    c1 = commit[...]
    c2 = jnp.clip(c1 - TAU * (grad[...] - gen_max * cap), 0.0, 1.0)
    bc2 = 2.0 * c2 - c1
    before = jnp.where(lanes == 0, init, pltpu.roll(bc2, 1, 1))
    commit_out[...] = c2
    bar_commit[...] = bc2
    start_out[...] = jnp.maximum(0.0, start[...] + SIGMA * (bc2 - before - bar_start[...]))
    window_out[...] = jnp.maximum(0.0, window[...] + SIGMA * (reach[...] - bc2))


def units_kernel(place, par, gen_m, gen_o, gen1, cap1, bar_commit, gen_out, cap_out):
    g2 = own_units(gen_m[...], gen_o[...], place[0])
    gen_out[...] = g2
    bar = 2.0 * g2 - gen1[...]
    cap_out[...] = jnp.maximum(0.0, cap1[...] + SIGMA * (bar - par[:, 0:1] * bar_commit[...]))


def load_kernel(place, ptdf, load, keep, send, demand, flow):
    step = pl.program_id(0)
    block = load[...]
    part = jnp.dot(ptdf[...], block, preferred_element_type=F32)
    rows = jnp.sum(block.astype(F32).reshape(-1, 8, block.shape[1]), axis=0)

    @pl.when(step == 0)
    def _():
        flow[...] = part
        demand[...] = rows

    @pl.when(step > 0)
    def _():
        flow[...] += part
        demand[...] += rows

    @pl.when(step == pl.num_programs(0) - 1)
    def _():
        turned = flow[...].T
        keep[...] = half_of(turned, place[0])
        send[...] = half_of(turned, 1 - place[0])


def line_step(bars, cols_m, cols_o, flow_m, flow_o, dual, rows_m, rows_o, held):
    wide = bars.shape[2]
    for i in range(bars.shape[0]):
        held[:, i * wide:(i + 1) * wide] = bars[i]
    bar = held[...]
    turn = (((1,), (1,)), ((), ()))
    mine = lax.dot_general(bar, cols_m[...], turn, preferred_element_type=F32) - flow_m[...]
    other = lax.dot_general(bar, cols_o[...], turn, preferred_element_type=F32) - flow_o[...]
    flows = jnp.concatenate([mine, other], axis=1)
    bound = jnp.concatenate([rows_m[LIMIT:LIMIT + 1], rows_o[LIMIT:LIMIT + 1]], axis=1)
    shifted = dual[...] + SIGMA * flows
    new = shifted - SIGMA * jnp.clip(shifted / SIGMA, -bound, bound)
    totals = jnp.sum(bar.astype(F32), axis=1, keepdims=True)
    return new, totals


def balance_step(place, totals, demand, balance, units):
    wanted = to_column(jnp.sum(demand[...], axis=0, keepdims=True))
    change = (totals - half_of(wanted, place[0])) / units
    return balance[...] + change


def line1_kernel(place, bars, cols_m, cols_o, flow_m, flow_o, dual, rows_m, rows_o, demand,
                 balance, part, dual_out, balance_out, held):
    new, totals = line_step(bars, cols_m, cols_o, flow_m, flow_o, dual, rows_m, rows_o, held)
    dual_out[...] = new
    periods = totals.shape[0]
    own = 2 * periods // part.shape[0]
    rows = lax.broadcasted_iota(jnp.int32, totals.shape, 0) + place[0] * periods
    held_here = (rows >= place[1] * own) & (rows < (place[1] + 1) * own)
    moved = balance_step(place, totals, demand, balance, cols_m.shape[1])
    moved = jnp.where(held_here, moved, 0.0)
    balance_out[...] = moved
    put_parts(part, new, cols_m, cols_o, moved)


def line2_kernel(place, bars, cols_m, cols_o, flow_m, flow_o, dual, rows_m, rows_o, demand,
                 balance, keep, send, held):
    new, totals = line_step(bars, cols_m, cols_o, flow_m, flow_o, dual, rows_m, rows_o, held)
    lines, periods = cols_m.shape[0], totals.shape[0]
    moved = to_row(balance_step(place, totals, demand, balance, cols_m.shape[1]))
    moved = jnp.concatenate([moved, jnp.zeros((1, lines - periods), F32)], axis=1)
    extra = jnp.broadcast_to(moved, (8, lines))
    keep[0:periods] = new[:, :lines]
    keep[periods:] = extra
    send[0:periods] = new[:, lines:]
    send[periods:] = extra


def last_kernel(place, mine, other, dual_out, balance_out):
    core, chip = place[0], place[1]
    half = dual_out.shape[1] // 2
    dual_out[...] = by_core(mine[0:half].T, other[0:half].T, core)
    own = balance_out.shape[1]
    first = (2 * chip + core) * own
    side = first // half
    row = jnp.where(core == side, mine[half:half + 1], other[half:half + 1])
    wide = row.shape[1]
    row = pltpu.roll(row, lax.rem(wide - (first - side * half), wide), 1)
    balance_out[...] = row[:, :own]


def work(flops, moved):
    return pl.CostEstimate(flops=flops, bytes_accessed=moved, transcendentals=0)


def call(kernel, outs, *args, placed=True, scratch=(), cost=None):
    shapes = [jax.ShapeDtypeStruct(shape, dtype) for shape, dtype in outs]
    return pl.pallas_call(
        kernel,
        out_shape=shapes,
        in_specs=([SMEM] if placed else []) + [VMEM] * (len(args) - placed),
        out_specs=[VMEM] * len(shapes),
        scratch_shapes=scratch,
        cost_estimate=cost,
    )(*args)


def block_depth(buses, most):
    return max(d for d in range(128, most + 1, 128) if buses % d == 0)


def swap(values):
    return lax.ppermute(values, "core", SWAP)


def on_device(
    ptdf, load, unit_bus, min_up, gen_max, cost_gen, cost_commit, cost_start, init_commit,
    line_limit, gen, commit, startup, line_dual, balance_dual, cap_dual, start_dual, window_dual,
):
    unit_dev, periods = gen.shape
    lines, buses = ptdf.shape
    units = unit_bus.shape[0]
    chips = lax.axis_size("chip")
    half = periods // 2
    unit_chip = 2 * unit_dev
    place = jnp.stack([lax.axis_index("core"), lax.axis_index("chip")])
    every_load = lax.all_gather(load, LINE, axis=0, tiled=True)

    dual_o = swap(line_dual)
    rows_m = call(
        rows_kernel, [((8, lines), F32)], place, line_limit[None], gen_max[None], cost_gen[None],
        balance_dual[None],
    )[0]
    rows_o = swap(rows_m)

    depth = block_depth(buses, 2304)
    cols_m = pl.pallas_call(
        columns_kernel,
        grid=(buses // depth,),
        out_shape=jax.ShapeDtypeStruct((lines, units), BF16),
        in_specs=[
            pl.BlockSpec((1, units), lambda k: (0, 0)),
            pl.BlockSpec((lines, depth), lambda k: (0, k)),
        ],
        out_specs=pl.BlockSpec((lines, units), lambda k: (0, 0)),
        scratch_shapes=[pltpu.VMEM((lines, units), F32)],
        cost_estimate=work(2 * units * lines * buses, ptdf.size * 2),
    )(unit_bus[None], ptdf)
    cols_o = swap(cols_m)

    par = jnp.stack([gen_max, cost_commit, cost_start, init_commit], axis=1)
    square = (unit_dev, periods)
    pack_m, commit1, start1, window1, startup2, grad2, bar_start2, reach2 = call(
        ahead_kernel, [((3 * unit_dev, periods), F32)] + [(square, F32)] * 7, par, min_up[:, None],
        gen, commit, startup, cap_dual, start_dual, window_dual, placed=False,
    )
    pack_o = swap(pack_m)

    blocks = (chips, half, unit_chip)
    parts, dual0, balance0 = call(
        adjoint_kernel, [(blocks, F32), ((half, 2 * lines), F32), ((half, 1), F32)],
        place, cols_m, cols_o, line_dual, dual_o, rows_m, rows_o,
    )
    parts = lax.all_to_all(parts, "chip", 0, 0)
    spread, state_m = call(
        gen1_kernel, [(blocks, BF16), ((2, half, unit_chip), F32)],
        place, parts, pack_m, pack_o, rows_m, rows_o,
    )
    bars = lax.all_to_all(spread, "chip", 0, 0)
    state_o = swap(state_m)

    depth = block_depth(buses, 4608)
    flow_m, send, demand = pl.pallas_call(
        load_kernel,
        grid=(buses // depth,),
        out_shape=[
            jax.ShapeDtypeStruct((half, lines), F32),
            jax.ShapeDtypeStruct((half, lines), F32),
            jax.ShapeDtypeStruct((8, periods), F32),
        ],
        in_specs=[
            SMEM,
            pl.BlockSpec((lines, depth), lambda k: (0, k)),
            pl.BlockSpec((depth, periods), lambda k: (k, 0)),
        ],
        out_specs=[
            pl.BlockSpec((half, lines), lambda k: (0, 0)),
            pl.BlockSpec((half, lines), lambda k: (0, 0)),
            pl.BlockSpec((8, periods), lambda k: (0, 0)),
        ],
        scratch_shapes=[pltpu.VMEM((lines, periods), F32)],
        cost_estimate=work(2 * periods * lines * buses, ptdf.size * 2 + every_load.size * 2),
    )(place, ptdf, every_load)
    flow_o = swap(send)

    held = [pltpu.VMEM((half, units), BF16)]
    parts, dual1, balance1 = call(
        line1_kernel, [(blocks, F32), ((half, 2 * lines), F32), ((half, 1), F32)],
        place, bars, cols_m, cols_o, flow_m, flow_o, dual0, rows_m, rows_o, demand, balance0,
        scratch=held,
    )
    parts = lax.all_to_all(parts, "chip", 0, 0)
    gen1, cap1, bar_commit2, commit2, start2, window2 = call(
        late_kernel, [(square, F32)] * 6,
        place, par, state_m, state_o, commit1, start1, window1, grad2, bar_start2, reach2,
    )
    spread, gen2_m = call(
        gen2_kernel, [(blocks, BF16), ((half, unit_chip), F32)],
        parts, state_m, rows_m, rows_o, placed=False,
    )
    bars = lax.all_to_all(spread, "chip", 0, 0)
    gen2_o = swap(gen2_m)
    gen2, cap2 = call(
        units_kernel, [(square, F32)] * 2, place, par, gen2_m, gen2_o, gen1, cap1, bar_commit2
    )
    dual2, send = call(
        line2_kernel, [((half + 8, lines), F32)] * 2,
        place, bars, cols_m, cols_o, flow_m, flow_o, dual1, rows_m, rows_o, demand, balance1,
        scratch=held,
    )
    dual2, balance2 = call(
        last_kernel, [((lines, periods), F32), ((1, balance_dual.shape[0]), F32)],
        place, dual2, swap(send),
    )
    return (gen2, commit2, startup2, dual2, balance2[0], cap2, start2, window2)


def solution(mesh):
    groups, lines = mesh.devices.shape
    mesh = Mesh(mesh.devices.reshape(groups, lines // 2, 2), ("grp", *LINE))
    wide = P(LINE, "grp")
    unit = P(LINE)
    both = P(("grp", *LINE))
    in_specs = (
        P(LINE, None), wide, P(), unit, unit, unit, unit, unit, unit, unit,
        wide, wide, wide, wide, both, wide, wide, wide,
    )
    out_specs = (wide, wide, wide, wide, both, wide, wide, wide)
    return jax.shard_map(
        on_device, mesh=mesh, in_specs=in_specs, out_specs=out_specs, check_vma=False
    )
```

time: 126 us -> 121 us (0.960)
  starting transfers between devices: 21.3 us -> 14.7 us
  blocking collectives: 20.4 us -> 25 us
  waiting for transfers between devices: 24.8 us -> 21.1 us
  Pallas kernels: 35.4 us -> 38.3 us
  local copies, waits for them, and re-layouts: 8.15 us -> 6.08 us
    all_to_all x3 -> x2, waiting for transfers between devices: 24.1 us -> 5.79 us  [the longest x1 5.79 us: on_device(): parts = lax.all_to_all(parts, 'chip', 0, 0)]
    all_gather x1, waiting for transfers between devices: 0.01 us -> 9.69 us  [on_device(): every_load = lax.all_gather(load, LINE, axis=0, tiled=True)]
    all_to_all x3 -> x2, starting transfers between devices: 21.3 us -> 12.8 us  [the longest x1 7.16 us: on_device(): parts = lax.all_to_all(parts, 'chip', 0, 0)]
    pallas_call x7 -> x11, Pallas kernels: 26.6 us -> 32 us  [the longest x10 20.8 us: call(): pl.pallas_call(kernel, out_shape=shapes, in_specs=([SMEM] if placed else...]
    ppermute x0 -> x8, waiting for transfers between devices: none -> 4.91 us  [swap(): return lax.ppermute(values, 'core', SWAP)]
    all_to_all x1 -> x2, blocking collectives: 20.4 us -> 25 us  [the longest x1 13.6 us: on_device(): parts = lax.all_to_all(parts, 'chip', 0, 0)]
    broadcast_in_dim x2 -> x0, local copies, waits for them, and re-layouts: 2.51 us -> none  [the longest x1 1.73 us: on_device(): unit_bus[:, None]]
    pallas_call x1, Pallas kernels: 8.84 us -> 6.37 us  [on_device(): pl.pallas_call(load_kernel, grid=(buses // depth,), out_shape=[jax.ShapeD...]
  transfers between devices with their start and end apart: 4 -> 11, of which waited for: 2 -> 6; matrix products, arithmetic and copies ran while one was open for 5% -> 2% of each run, Pallas kernels for 23% -> 25%
where the time goes in v2:
time: 121 us; the launch traced here: 120 us
  Pallas kernels  38.3 us (32%)
  blocking collectives  25 us (21%)
  waiting for transfers between devices  21.1 us (17%)
  starting transfers between devices  14.7 us (12%)
  between operations  14.2 us (12%)
  local copies, waits for them, and re-layouts  6.08 us (5%)
    pallas_call x10, Pallas kernels, call(): pl.pallas_call(kernel, out_shape=shapes, in_specs=([SMEM] if placed else...  20.8 us
    all_to_all x1, blocking collectives, on_device(): parts = lax.all_to_all(parts, 'chip', 0, 0)  13.6 us
    all_to_all x1, blocking collectives, on_device(): bars = lax.all_to_all(spread, 'chip', 0, 0)  11.3 us
    pallas_call x1, Pallas kernels, on_device(): pl.pallas_call(columns_kernel, grid=(buses // depth,), out_shape=jax.Shap...  11.2 us
    all_gather x1, waiting for transfers between devices, on_device(): every_load = lax.all_gather(load, LINE, axis=0, tiled=True)  9.69 us
    all_to_all x1, starting transfers between devices, on_device(): parts = lax.all_to_all(parts, 'chip', 0, 0)  7.16 us
    pallas_call x1, Pallas kernels, on_device(): pl.pallas_call(load_kernel, grid=(buses // depth,), out_shape=[jax.ShapeD...  6.37 us
    all_to_all x1, waiting for transfers between devices, on_device(): parts = lax.all_to_all(parts, 'chip', 0, 0)  5.79 us
  transfers between devices with their start and end apart: 11, of which 6 were waited for; matrix products, arithmetic and copies ran while one was open for 2% of the time, Pallas kernels for 25%

profile of v2, /device:TPU:0, one launch (start us, length us, event | category | flops | bytes accessed | tf_op | source)
XLA Modules:
  0.0 119.9 jit_solution(14190757401545981659)
XLA Ops:
  7.2 0.0 all-gather.2.cloned.1.call-start
  7.2 0.7 all-gather.2.cloned.1.call-update
  7.9 0.0 copy-start.6
  7.9 0.0 copy-start.12
  7.9 0.0 copy-start.14
  7.9 0.0 copy-start.15
  7.9 0.0 copy-start.16
  8.0 0.0 copy-start.13
  8.0 11.2 %shard_map.233.cols_m = bf16[256,1024]{1,0:T(8,128)(2,1)} custom-call(s32[1,1024]{1,0:T(1,128)} %bitcast.22, bf16[256,13824]{1,0:T(8,128)(2,1)} %ptdf.3), custom_call_target="tpu_custom_call" | custom-call | flops 7247757312 | bytes 7077888 | tf_op jit(solution)/shard_map/pallas_call | solution.py:364
  19.2 0.5 collective-permute-start
  19.7 0.0 copy-done.6
  19.7 0.0 collective-permute-start.1
  19.7 0.6 pad_add_fusion.place
  20.3 1.5 %shard_map.234.rows_m = f32[8,256]{1,0:T(8,128)} custom-call(s32[2]{0:T(128)} %pad_add_fusion.place, f32[1,256]{1,0:T(1,128)} %bitcast.15, f32[1,64]{1,0:T(1,128)} %bitcast.13, f32[1,64]{1,0:T(1,128)} %bitcast.17, f32[1,8]{1,0:T(1,128)} %bitcast.18), custom_call_target="tpu_custom_call" | custom-call | tf_op jit(solution)/shard_map/pallas_call | solution.py:325
  21.7 0.5 collective-permute-start.2
  22.2 1.0 collective-permute-done.2.rows_o
  23.3 0.0 collective-permute-done.1.dual_o
  23.3 0.0 collective-permute-done.cols_o
  23.3 0.6 copy-done.5
  23.9 0.1 copy-done.7
  23.9 0.8 copy-done
  24.7 2.3 %shard_map.235 = (f32[8,64,128]{2,1,0:T(8,128)}, f32[64,512]{1,0:T(8,128)}, f32[64,1]{1,0:T(8,128)}) custom-call(s32[2]{0:T(128)} %pad_add_fusion.place, bf16[256,1024]{1,0:T(8,128)(2,1)} %shard_map.233.cols_m, bf16[256,1024]{1,0:T(8,128)(2,1)} %copy-done, f32[256,128]{1,0:T(8,128)} %dual_m.1, f32[256,128]{1,0:T(8,128)} %copy-done.7, ...), custom_call_target="tpu_custom_call" | custom-call | tf_op jit(solution)/shard_map/pallas_call | solution.py:325
  27.1 7.2 %all-to-all-start = ((f32[8,64,128]{2,1,0:T(8,128)}), f32[8,64,128]{2,1,0:T(8,128)S(1)}, u32[]{:S(2)}, u32[]{:S(2)}) async-start(f32[8,64,128]{2,1,0:T(8,128)} %get-tuple-element.41), calls=%async_computation | async-start | bytes 524288 | tf_op jit(solution)/shard_map/all_to_all | solution.py:391
  34.2 0.0 copy-done.12
  34.2 0.0 copy-done.14
  34.3 0.0 copy-done.15
  34.3 0.0 copy-done.16
  34.3 0.7 copy.34.par
  35.0 0.0 copy-done.13
  35.0 0.7 copy.32.spans_ref
  35.7 2.7 %shard_map.236 = (f32[192,128]{1,0:T(8,128)}, f32[64,128]{1,0:T(8,128)}, f32[64,128]{1,0:T(8,128)}, f32[64,128]{1,0:T(8,128)}, f32[64,128]{1,0:T(8,128)}, /*inde...) custom-call(f32[64,4]{1,0:T(8,128)} %copy.34.par, s32[64,1]{1,0:T(8,128)} %copy.32.spans_ref, f32[64,128]{1,0:T(8,128)} %gen.1, ...), custom_call_target="tpu_custom_call" | custom-call | tf_op jit(solution)/shard_map/pallas_call | solution.py:325
  38.4 0.0 collective-permute-start.3
  38.5 1.6 %collective-permute-done.3.pack_o = f32[192,128]{1,0:T(8,128)S(1)} collective-permute-done((f32[192,128]{1,0:T(8,128)}, f32[192,128]{1,0:T(8,128)S(1)}, u32[]{:S(2)}, u32[]{:S(2)}) %collective-permute-start.3) | collective-permute-done | bytes 98336 | tf_op jit(solution)/shard_map/ppermute | solution.py:340
  40.1 5.8 %all-to-all-done.parts = f32[8,64,128]{2,1,0:T(8,128)S(1)} async-done(((f32[8,64,128]{2,1,0:T(8,128)}), f32[8,64,128]{2,1,0:T(8,128)S(1)}, u32[]{:S(2)}, u32[]{:S(2)}) %all-to-all-start) | async-done | bytes 262176 | tf_op jit(solution)/shard_map/all_to_all | solution.py:391
  45.9 0.0 copy-done.8
  45.9 0.7 copy-done.1
  46.6 2.0 %shard_map.237 = (bf16[8,64,128]{2,1,0:T(8,128)(2,1)}, f32[2,64,128]{2,1,0:T(8,128)}) custom-call(s32[2]{0:T(128)} %pad_add_fusion.place, f32[8,64,128]{2,1,0:T(8,128)} %copy-done.1, f32[192,128]{1,0:T(8,128)} %get-tuple-element.42.pack_m, f32[192,128]{1,0:T(8,128)} %copy-done.8, f32[8,256]{1,0:T(8,128)} %shard_map.234.rows_m, f32[8,256]{1,0:T(8,128)} %copy-done.5), custom_call_target="tpu_custom_call" | custom-call | tf_op jit(solution)/shard_map/pallas_call | solution.py:325
  48.6 5.6 %all-to-all-start.1 = ((bf16[8,64,128]{2,1,0:T(8,128)(2,1)}), bf16[8,64,128]{2,1,0:T(8,128)(2,1)S(1)}, u32[]{:S(2)}, u32[]{:S(2)}) async-start(bf16[8,64,128]{2,1,0:T(8,128)(2,1)} %get-tuple-element.43), calls=%async_computation.1 | async-start | bytes 262144 | tf_op jit(solution)/shard_map/all_to_all | solution.py:396
  54.2 9.7 %all-gather.2.cloned.1.call-done.load = bf16[13824,128]{1,0:T(8,128)(2,1)} async-done(((bf16[864,128]{1,0:T(8,128)(2,1)}), bf16[13824,128]{1,0:T(8,128)(2,1)}) %all-gather.2.cloned.1.call-update) | async-done | bytes 3538960 | tf_op jit(solution)/shard_map/all_gather | solution.py:354
  63.9 6.4 %shard_map.238 = (f32[64,256]{1,0:T(8,128)}, f32[64,256]{1,0:T(8,128)}, f32[8,128]{1,0:T(8,128)}) custom-call(s32[2]{0:T(128)} %pad_add_fusion.place, bf16[256,13824]{1,0:T(8,128)(2,1)} %ptdf.3, bf16[13824,128]{1,0:T(8,128)(2,1)} %all-gather.2.cloned.1.call-done.load), custom_call_target="tpu_custom_call" | custom-call | flops 905969664 | bytes 10616832 | tf_op jit(solution)/shard_map/pallas_call | solution.py:400
  70.3 0.2 collective-permute-start.4
  70.6 0.0 all-to-all-done.1.bars
  70.6 1.2 %collective-permute-done.4.flow_o = f32[64,256]{1,0:T(8,128)S(1)} collective-permute-done((f32[64,256]{1,0:T(8,128)}, f32[64,256]{1,0:T(8,128)S(1)}, u32[]{:S(2)}, u32[]{:S(2)}) %collective-permute-start.4) | collective-permute-done | bytes 65568 | tf_op jit(solution)/shard_map/ppermute | solution.py:340
  71.8 0.0 copy-done.2
  71.8 0.6 copy-done.3
  72.4 2.8 %shard_map.239 = (f32[8,64,128]{2,1,0:T(8,128)}, f32[64,512]{1,0:T(8,128)}, f32[64,1]{1,0:T(8,128)}) custom-call(s32[2]{0:T(128)} %pad_add_fusion.place, bf16[8,64,128]{2,1,0:T(8,128)(2,1)} %copy-done.2, bf16[256,1024]{1,0:T(8,128)(2,1)} %shard_map.233.cols_m, bf16[256,1024]{1,0:T(8,128)(2,1)} %copy-done, f32[64,256]{1,0:T(8,128)} %get-tuple-element.44.flow_m, ...), custom_call_target="tpu_custom_call" | custom-call | tf_op jit(solution)/shard_map/pallas_call | solution.py:325
  75.2 13.6 %all_to_all.20.parts = f32[8,64,128]{2,1,0:T(8,128)} all-to-all(f32[8,64,128]{2,1,0:T(8,128)} %get-tuple-element.49), channel_id=1, replica_groups=mesh['grp'=2,'chip'=8,'core'=2] {'chip'}, dimensions={0} | all-to-all | bytes 524288 | tf_op jit(solution)/shard_map/all_to_all | solution.py:429
  88.8 1.7 %shard_map.240 = (bf16[8,64,128]{2,1,0:T(8,128)(2,1)}, f32[64,128]{1,0:T(8,128)}) custom-call(f32[8,64,128]{2,1,0:T(8,128)} %all_to_all.20.parts, f32[2,64,128]{2,1,0:T(8,128)} %get-tuple-element.50.state.state_m, f32[8,256]{1,0:T(8,128)} %shard_map.234.rows_m, f32[8,256]{1,0:T(8,128)} %copy-done.5), custom_call_target="tpu_custom_call" | custom-call | tf_op jit(solution)/shard_map/pallas_call | solution.py:325
  90.5 11.3 %all_to_all.21.bars = bf16[8,64,128]{2,1,0:T(8,128)(2,1)} all-to-all(bf16[8,64,128]{2,1,0:T(8,128)(2,1)} %get-tuple-element.64), channel_id=1, replica_groups=mesh['grp'=2,'chip'=8,'core'=2] {'chip'}, dimensions={0} | all-to-all | bytes 262144 | tf_op jit(solution)/shard_map/all_to_all | solution.py:438
  101.8 2.5 %shard_map.243 = (f32[72,256]{1,0:T(8,128)}, f32[72,256]{1,0:T(8,128)}) custom-call(s32[2]{0:T(128)} %pad_add_fusion.place, bf16[8,64,128]{2,1,0:T(8,128)(2,1)} %all_to_all.21.bars, bf16[256,1024]{1,0:T(8,128)(2,1)} %shard_map.233.cols_m, bf16[256,1024]{1,0:T(8,128)(2,1)} %copy-done, f32[64,256]{1,0:T(8,128)} %get-tuple-element.44.flow_m, ...), custom_call_target="tpu_custom_call" | custom-call | tf_op jit(solution)/shard_map/pallas_call | solution.py:325
  104.3 0.0 collective-permute-start.7
  104.3 0.0 copy-done.4
  104.3 0.5 collective-permute-start.6
  104.8 0.1 collective-permute-start.5
  104.9 1.0 collective-permute-done.6.state_o
  105.8 0.6 copy-done.10
  106.5 1.9 %shard_map.241 = (f32[64,128]{1,0:T(8,128)}, f32[64,128]{1,0:T(8,128)}, f32[64,128]{1,0:T(8,128)}, f32[64,128]{1,0:T(8,128)}, f32[64,128]{1,0:T(8,128)}, /*index=5*/f32[64,128]{1,0:T(8,128)}) custom-call(s32[2]{0:T(128)} %pad_add_fusion.place, f32[64,4]{1,0:T(8,128)} %copy.34.par, f32[2,64,128]{2,1,0:T(8,128)} %get-tuple-element.50.state.state_m, ...), custom_call_target="tpu_custom_call" | custom-call | tf_op jit(solution)/shard_map/pallas_call | solution.py:325
  108.3 0.0 collective-permute-done.5.gen_o
  108.3 0.0 copy-start.11
  108.4 0.6 copy-done.11
  109.0 1.6 %shard_map.242 = (f32[64,128]{1,0:T(8,128)}, f32[64,128]{1,0:T(8,128)}) custom-call(s32[2]{0:T(128)} %pad_add_fusion.place, f32[64,4]{1,0:T(8,128)} %copy.34.par, f32[64,128]{1,0:T(8,128)} %get-tuple-element.51.gen_m, f32[64,128]{1,0:T(8,128)} %copy-done.11, f32[64,128]{1,0:T(8,128)} %get-tuple-element.58.gen1, f32[64,128]{1,0:T(8,128)} %get-tuple-element.59.cap1, ...), custom_call_target="tpu_custom_call" | custom-call | tf_op jit(solution)/shard_map/pallas_call | solution.py:325
  110.6 0.0 collective-permute-done.7.other
  110.6 0.6 copy-done.9
  111.2 1.8 %shard_map.244 = (f32[256,128]{1,0:T(8,128)}, f32[1,8]{1,0:T(1,128)}) custom-call(s32[2]{0:T(128)} %pad_add_fusion.place, f32[72,256]{1,0:T(8,128)} %get-tuple-element.67.mine, f32[72,256]{1,0:T(8,128)} %copy-done.9), custom_call_target="tpu_custom_call" | custom-call | tf_op jit(solution)/shard_map/pallas_call | solution.py:325
  (11 shorter events, 0.0 us)
Async XLA Ops:
  7.2 56.8 %all-gather.2.cloned.1.call-start = ((), (), s32[]{:S(2)}) async-start(), calls=%async_computation.4 | async-start | bytes 3760128 | tf_op jit(solution)/shard_map/all_gather | solution.py:354
  7.9 11.8 %copy-start.6 = (f32[256,128]{1,0:T(8,128)S(1)}, f32[256,128]{1,0:T(8,128)}, u32[]{:S(2)}) copy-start(f32[256,128]{1,0:T(8,128)} %dual_m.1) | copy-start | bytes 393220
  7.9 26.3 %copy-start.12 = (f32[64]{0:T(128)S(1)}, f32[64]{0:T(128)}, u32[]{:S(2)}) copy-start(f32[64]{0:T(128)} %param.22) | copy-start | bytes 772
  7.9 26.3 %copy-start.14 = (f32[64]{0:T(128)S(1)}, f32[64]{0:T(128)}, u32[]{:S(2)}) copy-start(f32[64]{0:T(128)} %param.26) | copy-start | bytes 772
  7.9 26.3 %copy-start.15 = (f32[64]{0:T(128)S(1)}, f32[64]{0:T(128)}, u32[]{:S(2)}) copy-start(f32[64]{0:T(128)} %param.25) | copy-start | bytes 772
  7.9 26.3 %copy-start.16 = (f32[64]{0:T(128)S(1)}, f32[64]{0:T(128)}, u32[]{:S(2)}) copy-start(f32[64]{0:T(128)} %param.24) | copy-start | bytes 772
  8.0 27.0 %copy-start.13 = (s32[64]{0:T(128)S(1)}, s32[64]{0:T(128)}, u32[]{:S(2)}) copy-start(s32[64]{0:T(128)} %param.21) | copy-start | bytes 772
  19.2 4.1 %collective-permute-start = (bf16[256,1024]{1,0:T(8,128)(2,1)}, bf16[256,1024]{1,0:T(8,128)(2,1)S(1)}, u32[]{:S(2)}, u32[]{:S(2)}) collective-permute-start(bf16[256,1024]{1,0:T(8,128)(2,1)} %shard_map.233.cols_m), channel_id=1, source_target_pairs={{0,1},{1,0},{2,3},{3,2},{4,5},{5,4},{6,7},{7,6},{8,9},{9,8},{10,11... | collective-permute-start | bytes 1572872 | tf_op jit(solution)/shard_map/ppermute | solution.py:340
  19.7 3.6 %collective-permute-start.1 = (f32[256,128]{1,0:T(8,128)S(1)}, f32[256,128]{1,0:T(8,128)S(1)}, u32[]{:S(2)}, u32[]{:S(2)}) collective-permute-start(f32[256,128]{1,0:T(8,128)S(1)} %copy-done.6), channel_id=1, source_target_pairs={{0,1},{1,0},{2,3},{3,2},{4,5},{5,4},{6,7},{7,6},{8,9},{9,8},{10,11... | collective-permute-start | bytes 393224 | tf_op jit(solution)/shard_map/ppermute | solution.py:340
  21.7 1.5 %collective-permute-start.2 = (f32[8,256]{1,0:T(8,128)}, f32[8,256]{1,0:T(8,128)S(1)}, u32[]{:S(2)}, u32[]{:S(2)}) collective-permute-start(f32[8,256]{1,0:T(8,128)} %shard_map.234.rows_m), channel_id=1, source_target_pairs={{0,1},{1,0},{2,3},{3,2},{4,5},{5,4},{6,7},{7,6},{8,9},{9,8},{10,11... | collective-permute-start | bytes 24584 | tf_op jit(solution)/shard_map/ppermute | solution.py:340
  23.3 0.6 copy-start.5
  23.3 0.7 copy-start.7
  23.9 0.8 copy-start
  27.1 18.8 %all-to-all-start = ((f32[8,64,128]{2,1,0:T(8,128)}), f32[8,64,128]{2,1,0:T(8,128)S(1)}, u32[]{:S(2)}, u32[]{:S(2)}) async-start(f32[8,64,128]{2,1,0:T(8,128)} %get-tuple-element.41), calls=%async_computation | async-start | bytes 524288 | tf_op jit(solution)/shard_map/all_to_all | solution.py:391
  38.4 1.7 %collective-permute-start.3 = (f32[192,128]{1,0:T(8,128)}, f32[192,128]{1,0:T(8,128)S(1)}, u32[]{:S(2)}, u32[]{:S(2)}) collective-permute-start(f32[192,128]{1,0:T(8,128)} %get-tuple-element.42.pack_m), channel_id=1, source_target_pairs={{0,1},{1,0},{2,3},{3,2},{4,5},{5,4},{6,7},{7,6},{8,9},{9,8},{10,11... | collective-permute-start | bytes 294920 | tf_op jit(solution)/shard_map/ppermute | solution.py:340
  40.1 5.8 %copy-start.8 = (f32[192,128]{1,0:T(8,128)}, f32[192,128]{1,0:T(8,128)S(1)}, u32[]{:S(2)}) copy-start(f32[192,128]{1,0:T(8,128)S(1)} %collective-permute-done.3.pack_o) | copy-start | bytes 294916
  45.9 0.7 copy-start.1
  48.6 22.0 %all-to-all-start.1 = ((bf16[8,64,128]{2,1,0:T(8,128)(2,1)}), bf16[8,64,128]{2,1,0:T(8,128)(2,1)S(1)}, u32[]{:S(2)}, u32[]{:S(2)}) async-start(bf16[8,64,128]{2,1,0:T(8,128)(2,1)} %get-tuple-element.43), calls=%async_computation.1 | async-start | bytes 262144 | tf_op jit(solution)/shard_map/all_to_all | solution.py:396
  54.2 50.0 %copy-start.4 = (f32[2,64,128]{2,1,0:T(8,128)S(1)}, f32[2,64,128]{2,1,0:T(8,128)}, u32[]{:S(2)}) copy-start(f32[2,64,128]{2,1,0:T(8,128)} %get-tuple-element.50.state.state_m) | copy-start | bytes 196612
  70.3 1.5 %collective-permute-start.4 = (f32[64,256]{1,0:T(8,128)}, f32[64,256]{1,0:T(8,128)S(1)}, u32[]{:S(2)}, u32[]{:S(2)}) collective-permute-start(f32[64,256]{1,0:T(8,128)} %get-tuple-element.45), channel_id=1, source_target_pairs={{0,1},{1,0},{2,3},{3,2},{4,5},{5,4},{6,7},{7,6},{8,9},{9,8},{10,11... | collective-permute-start | bytes 196616 | tf_op jit(solution)/shard_map/ppermute | solution.py:340
  70.6 1.2 %copy-start.2 = (bf16[8,64,128]{2,1,0:T(8,128)(2,1)}, bf16[8,64,128]{2,1,0:T(8,128)(2,1)S(1)}, u32[]{:S(2)}) copy-start(bf16[8,64,128]{2,1,0:T(8,128)(2,1)S(1)} %all-to-all-done.1.bars) | copy-start | bytes 393220
  71.8 0.6 copy-start.3
  104.3 6.3 %collective-permute-start.7 = (f32[72,256]{1,0:T(8,128)}, f32[72,256]{1,0:T(8,128)S(1)}, u32[]{:S(2)}, u32[]{:S(2)}) collective-permute-start(f32[72,256]{1,0:T(8,128)} %get-tuple-element.68), channel_id=1, source_target_pairs={{0,1},{1,0},{2,3},{3,2},{4,5},{5,4},{6,7},{7,6},{8,9},{9,8},{10,11... | collective-permute-start | bytes 221192 | tf_op jit(solution)/shard_map/ppermute | solution.py:340
  104.3 1.6 %collective-permute-start.6 = (f32[2,64,128]{2,1,0:T(8,128)S(1)}, f32[2,64,128]{2,1,0:T(8,128)S(1)}, u32[]{:S(2)}, u32[]{:S(2)}) collective-permute-start(f32[2,64,128]{2,1,0:T(8,128)S(1)} %copy-done.4), channel_id=1, source_target_pairs={{0,1},{1,0},{2,3},{3,2},{4,5},{5,4},{6,7},{7,6},{8,9},{9,8},{10,11... | collective-permute-start | bytes 196616 | tf_op jit(solution)/shard_map/ppermute | solution.py:340
  104.8 3.6 %collective-permute-start.5 = (f32[64,128]{1,0:T(8,128)}, f32[64,128]{1,0:T(8,128)S(1)}, u32[]{:S(2)}, u32[]{:S(2)}) collective-permute-start(f32[64,128]{1,0:T(8,128)} %get-tuple-element.51.gen_m), channel_id=1, source_target_pairs={{0,1},{1,0},{2,3},{3,2},{4,5},{5,4},{6,7},{7,6},{8,9},{9,8},{10,11... | collective-permute-start | bytes 98312 | tf_op jit(solution)/shard_map/ppermute | solution.py:340
  105.8 0.6 copy-start.10
  108.3 0.6 copy-start.11
  110.6 0.6 copy-start.9
Sparse Core Ops, SparseCore 0:
  10.3 53.6 all-gather.1

commit v3 on v2

--- a/solution.py
+++ b/solution.py
@@ -1,3 +1,5 @@
+import functools
+
 import jax
 import jax.numpy as jnp
 from jax import lax
@@ -5,7 +7,6 @@
 from jax.experimental.pallas import tpu as pltpu
 from jax.sharding import Mesh, PartitionSpec as P
 
-ITERS = 2
 TAU = 0.05
 SIGMA = 0.5
 SPAN_BITS = 5
@@ -14,10 +15,10 @@
 BF16 = jnp.bfloat16
 LINE = ("chip", "core")
 SWAP = [(0, 1), (1, 0)]
+SLAB_BEFORE = (1, 3, 0, 2)
 VMEM = pl.BlockSpec(memory_space=pltpu.VMEM)
-SMEM = pl.BlockSpec(memory_space=pltpu.SMEM)
-
-LIMIT, GEN_MAX, COST_GEN, BALANCE = 0, 1, 2, 3
+
+LIMIT, GEN_MAX, COST_GEN = 0, 1, 2
 
 
 def shift_right(values, amount):
@@ -70,19 +71,18 @@
     )
 
 
-def rows_kernel(place, limit, gen_max, cost_gen, balance, out):
-    core, chip = place[0], place[1]
+def rows_kernel(limit, gen_max, cost_gen, out):
+    core = lax.axis_index("core")
     wide = out.shape[1]
 
     def put(row):
         return jnp.concatenate([row, jnp.zeros((1, wide - row.shape[1]), F32)], axis=1)
 
-    units, periods = gen_max.shape[1], balance.shape[1]
+    units = gen_max.shape[1]
     out[...] = jnp.zeros_like(out)
     out[LIMIT:LIMIT + 1] = limit[...]
     out[GEN_MAX:GEN_MAX + 1] = pltpu.roll(put(gen_max[...]), core * units, 1)
     out[COST_GEN:COST_GEN + 1] = pltpu.roll(put(cost_gen[...]), core * units, 1)
-    out[BALANCE:BALANCE + 1] = pltpu.roll(put(balance[...]), (2 * chip + core) * periods, 1)
 
 
 def ahead_kernel(par, spans_ref, gen, commit, startup, cap, start, window,
@@ -116,17 +116,18 @@
     reach2[...] = window_sum(bs2, spans, shift_right)
 
 
-def columns_kernel(bus, ptdf, cols, acc):
+def columns_kernel(first, bus, ptdf, *refs):
+    *before, cols, acc = refs
     step = pl.program_id(0)
     depth = ptdf.shape[1]
-    here = bus[...] - step * depth
+    here = bus[...] - (first + step) * depth
     places = lax.broadcasted_iota(jnp.int32, (depth, bus.shape[1]), 0)
     hot = jnp.where(places == here, 1.0, 0.0).astype(BF16)
     part = jnp.dot(ptdf[...], hot, preferred_element_type=F32)
 
     @pl.when(step == 0)
     def _():
-        acc[...] = part
+        acc[...] = before[0][...] + part if before else part
 
     @pl.when(step > 0)
     def _():
@@ -134,7 +135,7 @@
 
     @pl.when(step == pl.num_programs(0) - 1)
     def _():
-        cols[...] = acc[...].astype(BF16)
+        cols[...] = acc[...].astype(cols.dtype)
 
 
 def put_parts(part, dual, cols_m, cols_o, balance):
@@ -148,12 +149,16 @@
         part[i] = total[:, i * wide:(i + 1) * wide]
 
 
-def adjoint_kernel(place, cols_m, cols_o, dual_m, dual_o, rows_m, rows_o, part, dual_t, balance):
-    core = place[0]
+def adjoint_kernel(cols_m, cols_o, dual_m, dual_o, balance_m, balance_o, part, dual_t, balance):
+    core, chip = lax.axis_index("core"), lax.axis_index("chip")
     periods = dual_m.shape[1]
     dual = jnp.concatenate([half_of(dual_m[...].T, core), half_of(dual_o[...].T, core)], axis=1)
     dual_t[...] = dual
-    row = rows_m[BALANCE:BALANCE + 1, :periods] + rows_o[BALANCE:BALANCE + 1, :periods]
+    own = balance_m.shape[1]
+    mine, other = balance_m[...], balance_o[...]
+    rest = jnp.zeros((1, periods - 2 * own), F32)
+    row = jnp.concatenate([by_core(mine, other, core), rest], axis=1)
+    row = pltpu.roll(row, 2 * chip * own, 1)
     column = half_of(to_column(row), core)
     balance[...] = column
     put_parts(part, dual, cols_m, cols_o, column)
@@ -173,8 +178,8 @@
     return g1, 2.0 * g1 - gen, gen_max
 
 
-def gen1_kernel(place, parts, pack_m, pack_o, rows_m, rows_o, spread, state):
-    core = place[0]
+def gen1_kernel(parts, pack_m, pack_o, rows_m, rows_o, spread, state):
+    core = lax.axis_index("core")
     units = pack_m.shape[0] // 3
 
     def turned(i):
@@ -206,9 +211,9 @@
     return by_core(here, there, core)
 
 
-def late_kernel(place, par, state_m, state_o, commit, start, window, grad, bar_start, reach,
+def late_kernel(par, state_m, state_o, commit, start, window, grad, bar_start, reach,
                 gen1, cap1, bar_commit, commit_out, start_out, window_out):
-    core = place[0]
+    core = lax.axis_index("core")
     gen_max, init = par[:, 0:1], par[:, 3:4]
     cap = own_units(state_m[1], state_o[1], core)
     gen1[...] = own_units(state_m[0], state_o[0], core)
@@ -224,14 +229,14 @@
     window_out[...] = jnp.maximum(0.0, window[...] + SIGMA * (reach[...] - bc2))
 
 
-def units_kernel(place, par, gen_m, gen_o, gen1, cap1, bar_commit, gen_out, cap_out):
-    g2 = own_units(gen_m[...], gen_o[...], place[0])
+def units_kernel(par, gen_m, gen_o, gen1, cap1, bar_commit, gen_out, cap_out):
+    g2 = own_units(gen_m[...], gen_o[...], lax.axis_index("core"))
     gen_out[...] = g2
     bar = 2.0 * g2 - gen1[...]
     cap_out[...] = jnp.maximum(0.0, cap1[...] + SIGMA * (bar - par[:, 0:1] * bar_commit[...]))
 
 
-def load_kernel(place, ptdf, load, keep, send, demand, flow):
+def load_kernel(ptdf, load, keep, send, demand, flow):
     step = pl.program_id(0)
     block = load[...]
     part = jnp.dot(ptdf[...], block, preferred_element_type=F32)
@@ -250,8 +255,45 @@
     @pl.when(step == pl.num_programs(0) - 1)
     def _():
         turned = flow[...].T
-        keep[...] = half_of(turned, place[0])
-        send[...] = half_of(turned, 1 - place[0])
+        core = lax.axis_index("core")
+        keep[...] = half_of(turned, core)
+        send[...] = half_of(turned, 1 - core)
+
+
+def slab_kernel(ptdf, *refs):
+    pieces, (keep, send, demand, buffers, slab, sems) = refs[:-6], refs[-6:]
+    core, chip = lax.axis_index("core"), lax.axis_index("chip")
+    side, here = chip % 2, chip // 2
+    count, _, depth = buffers.shape
+    copies = []
+    for i in range(count):
+        start = pl.multiple_of(here * depth, depth)
+        before = jnp.where(here == 2, SLAB_BEFORE[2], SLAB_BEFORE[3])
+        here = jnp.where(here == 0, SLAB_BEFORE[0], jnp.where(here == 1, SLAB_BEFORE[1], before))
+        copies.append(
+            pltpu.make_async_copy(ptdf.at[:, pl.ds(start, depth)], buffers.at[i], sems.at[i])
+        )
+        copies[i].start()
+    flow, rows = 0.0, 0.0
+    for i in range(count):
+        near, across, swapped, far = (ref[...] for ref in pieces[4 * i:4 * i + 4])
+        bus_dev, periods = near.shape
+        for yy in range(2):
+            for kk in range(2):
+                chosen = jnp.where(
+                    side == yy,
+                    jnp.where(core == kk, near, swapped),
+                    jnp.where(core == kk, across, far),
+                )
+                at = (2 * yy + kk) * bus_dev
+                slab[at:at + bus_dev] = chosen
+                rows += jnp.sum(chosen.astype(F32).reshape(-1, 8, periods), axis=0)
+        copies[i].wait()
+        flow += jnp.dot(buffers[i], slab[...], preferred_element_type=F32)
+    turned = flow.T
+    keep[...] = half_of(turned, core)
+    send[...] = half_of(turned, 1 - core)
+    demand[...] = rows
 
 
 def line_step(bars, cols_m, cols_o, flow_m, flow_o, dual, rows_m, rows_o, held):
@@ -270,31 +312,32 @@
     return new, totals
 
 
-def balance_step(place, totals, demand, balance, units):
+def balance_step(totals, demand, balance, units):
     wanted = to_column(jnp.sum(demand[...], axis=0, keepdims=True))
-    change = (totals - half_of(wanted, place[0])) / units
+    change = (totals - half_of(wanted, lax.axis_index("core"))) / units
     return balance[...] + change
 
 
-def line1_kernel(place, bars, cols_m, cols_o, flow_m, flow_o, dual, rows_m, rows_o, demand,
+def line1_kernel(bars, cols_m, cols_o, flow_m, flow_o, dual, rows_m, rows_o, demand,
                  balance, part, dual_out, balance_out, held):
     new, totals = line_step(bars, cols_m, cols_o, flow_m, flow_o, dual, rows_m, rows_o, held)
     dual_out[...] = new
     periods = totals.shape[0]
     own = 2 * periods // part.shape[0]
-    rows = lax.broadcasted_iota(jnp.int32, totals.shape, 0) + place[0] * periods
-    held_here = (rows >= place[1] * own) & (rows < (place[1] + 1) * own)
-    moved = balance_step(place, totals, demand, balance, cols_m.shape[1])
+    rows = lax.broadcasted_iota(jnp.int32, totals.shape, 0) + lax.axis_index("core") * periods
+    chip = lax.axis_index("chip")
+    held_here = (rows >= chip * own) & (rows < (chip + 1) * own)
+    moved = balance_step(totals, demand, balance, cols_m.shape[1])
     moved = jnp.where(held_here, moved, 0.0)
     balance_out[...] = moved
     put_parts(part, new, cols_m, cols_o, moved)
 
 
-def line2_kernel(place, bars, cols_m, cols_o, flow_m, flow_o, dual, rows_m, rows_o, demand,
+def line2_kernel(bars, cols_m, cols_o, flow_m, flow_o, dual, rows_m, rows_o, demand,
                  balance, keep, send, held):
     new, totals = line_step(bars, cols_m, cols_o, flow_m, flow_o, dual, rows_m, rows_o, held)
     lines, periods = cols_m.shape[0], totals.shape[0]
-    moved = to_row(balance_step(place, totals, demand, balance, cols_m.shape[1]))
+    moved = to_row(balance_step(totals, demand, balance, cols_m.shape[1]))
     moved = jnp.concatenate([moved, jnp.zeros((1, lines - periods), F32)], axis=1)
     extra = jnp.broadcast_to(moved, (8, lines))
     keep[0:periods] = new[:, :lines]
@@ -303,8 +346,8 @@
     send[periods:] = extra
 
 
-def last_kernel(place, mine, other, dual_out, balance_out):
-    core, chip = place[0], place[1]
+def last_kernel(mine, other, dual_out, balance_out):
+    core, chip = lax.axis_index("core"), lax.axis_index("chip")
     half = dual_out.shape[1] // 2
     dual_out[...] = by_core(mine[0:half].T, other[0:half].T, core)
     own = balance_out.shape[1]
@@ -320,12 +363,12 @@
     return pl.CostEstimate(flops=flops, bytes_accessed=moved, transcendentals=0)
 
 
-def call(kernel, outs, *args, placed=True, scratch=(), cost=None):
+def call(kernel, outs, *args, scratch=(), cost=None):
     shapes = [jax.ShapeDtypeStruct(shape, dtype) for shape, dtype in outs]
     return pl.pallas_call(
         kernel,
         out_shape=shapes,
-        in_specs=([SMEM] if placed else []) + [VMEM] * (len(args) - placed),
+        in_specs=[VMEM] * len(args),
         out_specs=[VMEM] * len(shapes),
         scratch_shapes=scratch,
         cost_estimate=cost,
@@ -340,64 +383,12 @@
     return lax.ppermute(values, "core", SWAP)
 
 
-def on_device(
-    ptdf, load, unit_bus, min_up, gen_max, cost_gen, cost_commit, cost_start, init_commit,
-    line_limit, gen, commit, startup, line_dual, balance_dual, cap_dual, start_dual, window_dual,
-):
-    unit_dev, periods = gen.shape
+def gathered_product(ptdf, every_load):
     lines, buses = ptdf.shape
-    units = unit_bus.shape[0]
-    chips = lax.axis_size("chip")
+    periods = every_load.shape[1]
     half = periods // 2
-    unit_chip = 2 * unit_dev
-    place = jnp.stack([lax.axis_index("core"), lax.axis_index("chip")])
-    every_load = lax.all_gather(load, LINE, axis=0, tiled=True)
-
-    dual_o = swap(line_dual)
-    rows_m = call(
-        rows_kernel, [((8, lines), F32)], place, line_limit[None], gen_max[None], cost_gen[None],
-        balance_dual[None],
-    )[0]
-    rows_o = swap(rows_m)
-
-    depth = block_depth(buses, 2304)
-    cols_m = pl.pallas_call(
-        columns_kernel,
-        grid=(buses // depth,),
-        out_shape=jax.ShapeDtypeStruct((lines, units), BF16),
-        in_specs=[
-            pl.BlockSpec((1, units), lambda k: (0, 0)),
-            pl.BlockSpec((lines, depth), lambda k: (0, k)),
-        ],
-        out_specs=pl.BlockSpec((lines, units), lambda k: (0, 0)),
-        scratch_shapes=[pltpu.VMEM((lines, units), F32)],
-        cost_estimate=work(2 * units * lines * buses, ptdf.size * 2),
-    )(unit_bus[None], ptdf)
-    cols_o = swap(cols_m)
-
-    par = jnp.stack([gen_max, cost_commit, cost_start, init_commit], axis=1)
-    square = (unit_dev, periods)
-    pack_m, commit1, start1, window1, startup2, grad2, bar_start2, reach2 = call(
-        ahead_kernel, [((3 * unit_dev, periods), F32)] + [(square, F32)] * 7, par, min_up[:, None],
-        gen, commit, startup, cap_dual, start_dual, window_dual, placed=False,
-    )
-    pack_o = swap(pack_m)
-
-    blocks = (chips, half, unit_chip)
-    parts, dual0, balance0 = call(
-        adjoint_kernel, [(blocks, F32), ((half, 2 * lines), F32), ((half, 1), F32)],
-        place, cols_m, cols_o, line_dual, dual_o, rows_m, rows_o,
-    )
-    parts = lax.all_to_all(parts, "chip", 0, 0)
-    spread, state_m = call(
-        gen1_kernel, [(blocks, BF16), ((2, half, unit_chip), F32)],
-        place, parts, pack_m, pack_o, rows_m, rows_o,
-    )
-    bars = lax.all_to_all(spread, "chip", 0, 0)
-    state_o = swap(state_m)
-
     depth = block_depth(buses, 4608)
-    flow_m, send, demand = pl.pallas_call(
+    return pl.pallas_call(
         load_kernel,
         grid=(buses // depth,),
         out_shape=[
@@ -406,7 +397,6 @@
             jax.ShapeDtypeStruct((8, periods), F32),
         ],
         in_specs=[
-            SMEM,
             pl.BlockSpec((lines, depth), lambda k: (0, k)),
             pl.BlockSpec((depth, periods), lambda k: (k, 0)),
         ],
@@ -417,37 +407,155 @@
         ],
         scratch_shapes=[pltpu.VMEM((lines, periods), F32)],
         cost_estimate=work(2 * periods * lines * buses, ptdf.size * 2 + every_load.size * 2),
-    )(place, ptdf, every_load)
+    )(ptdf, every_load)
+
+
+def slab_product(ptdf, pieces):
+    lines, buses = ptdf.shape
+    bus_dev, periods = pieces[0].shape
+    count = len(pieces) // 4
+    shapes = [((periods // 2, lines), F32)] * 2 + [((8, periods), F32)]
+    return pl.pallas_call(
+        slab_kernel,
+        out_shape=[jax.ShapeDtypeStruct(*shape) for shape in shapes],
+        in_specs=[pl.BlockSpec(memory_space=pl.ANY)] + [VMEM] * len(pieces),
+        out_specs=[VMEM] * len(shapes),
+        scratch_shapes=[
+            pltpu.VMEM((count, lines, 4 * bus_dev), BF16),
+            pltpu.VMEM((4 * bus_dev, periods), BF16),
+            pltpu.SemaphoreType.DMA((count,)),
+        ],
+        cost_estimate=work(2 * lines * periods * buses, buses * (lines + periods) * 2),
+    )(ptdf, *pieces)
+
+
+def unit_columns(ptdf, unit_bus, first, last, *before):
+    lines, buses = ptdf.shape
+    units = unit_bus.shape[0]
+    depth = block_depth(buses, 2304)
+    steps = buses // depth
+    kept = BF16 if last == 2 else F32
+    start, steps = steps * first // 2, steps * last // 2 - steps * first // 2
+    return pl.pallas_call(
+        functools.partial(columns_kernel, start),
+        grid=(steps,),
+        out_shape=jax.ShapeDtypeStruct((lines, units), kept),
+        in_specs=[
+            pl.BlockSpec((1, units), lambda k: (0, 0)),
+            pl.BlockSpec((lines, depth), lambda k: (0, start + k)),
+        ] + [pl.BlockSpec((lines, units), lambda k: (0, 0)) for _ in before],
+        out_specs=pl.BlockSpec((lines, units), lambda k: (0, 0)),
+        scratch_shapes=[pltpu.VMEM((lines, units), F32)],
+        cost_estimate=work(2 * units * lines * depth * steps, lines * depth * steps * 2),
+    )(unit_bus[None], ptdf, *before)
+
+
+def on_device(
+    ptdf, load, unit_bus, min_up, gen_max, cost_gen, cost_commit, cost_start, init_commit,
+    line_limit, gen, commit, startup, line_dual, balance_dual, cap_dual, start_dual, window_dual,
+):
+    unit_dev, periods = gen.shape
+    lines, _ = ptdf.shape
+    units = unit_bus.shape[0]
+    chips = lax.axis_size("chip")
+    half = periods // 2
+    unit_chip = 2 * unit_dev
+    across = [(i, i ^ 1) for i in range(chips)]
+    by_slab = chips == 8 and 4 * load.shape[0] % 128 == 0
+    after = lax.optimization_barrier
+
+    def relay(piece):
+        pairs = [(2 * SLAB_BEFORE[i // 2] + i % 2, i) for i in range(chips)]
+        return lax.ppermute(piece, "chip", pairs)
+
+    def cross(piece):
+        return lax.ppermute(piece, "chip", across)
+
+    if by_slab:
+        near = [load, relay(load)]
+        far = [cross(load)]
+    else:
+        every_load = lax.all_gather(load, LINE, axis=0, tiled=True)
+    dual_o, balance_o = swap(line_dual), swap(balance_dual)
+
+    some = unit_columns(ptdf, unit_bus, 0, 1)
+    if by_slab:
+        near[1] = after((near[1], some))[0]
+        near.append(relay(near[1]))
+        far.append(cross(near[1]))
+    cols_m = unit_columns(ptdf, unit_bus, 1, 2, some)
+    if by_slab:
+        near[2] = after((near[2], cols_m))[0]
+        near.append(relay(near[2]))
+        far.append(cross(near[2]))
+    cols_o = swap(cols_m)
+
+    blocks = (chips, half, unit_chip)
+    parts, dual0, balance0 = call(
+        adjoint_kernel, [(blocks, F32), ((half, 2 * lines), F32), ((half, 1), F32)],
+        cols_m, cols_o, line_dual, dual_o, balance_dual[None], balance_o[None],
+    )
+    commit, startup, gen_max, min_up, parts = after((commit, startup, gen_max, min_up, parts))
+    sums = lax.all_to_all(parts, "chip", 0, 0)
+    if by_slab:
+        near[3] = after((near[3], parts))[0]
+        far.append(cross(near[3]))
+    rows_m = call(
+        rows_kernel, [((8, lines), F32)], line_limit[None], gen_max[None], cost_gen[None]
+    )[0]
+    rows_o = swap(rows_m)
+    par = jnp.stack([gen_max, cost_commit, cost_start, init_commit], axis=1)
+    square = (unit_dev, periods)
+    pack_m, commit1, start1, window1, startup2, grad2, bar_start2, reach2 = call(
+        ahead_kernel, [((3 * unit_dev, periods), F32)] + [(square, F32)] * 7, par,
+        min_up[:, None], gen, commit, startup, cap_dual, start_dual, window_dual,
+    )
+    pack_o = swap(pack_m)
+    spread, state_m = call(
+        gen1_kernel, [(blocks, BF16), ((2, half, unit_chip), F32)],
+        sums, pack_m, pack_o, rows_m, rows_o,
+    )
+
+    bars = lax.all_to_all(spread, "chip", 0, 0)
+    if by_slab:
+        near[2:] = after((*near[2:], spread))[:2]
+        far[1:] = after((*far[1:], spread))[:3]
+        pieces = [[n, f, swap(n), swap(f)] for n, f in zip(near, far)]
+        flow_m, send, demand = slab_product(ptdf, sum(pieces, []))
+    else:
+        flow_m, send, demand = gathered_product(ptdf, every_load)
     flow_o = swap(send)
 
     held = [pltpu.VMEM((half, units), BF16)]
     parts, dual1, balance1 = call(
         line1_kernel, [(blocks, F32), ((half, 2 * lines), F32), ((half, 1), F32)],
-        place, bars, cols_m, cols_o, flow_m, flow_o, dual0, rows_m, rows_o, demand, balance0,
+        bars, cols_m, cols_o, flow_m, flow_o, dual0, rows_m, rows_o, demand, balance0,
         scratch=held,
     )
-    parts = lax.all_to_all(parts, "chip", 0, 0)
+    sums = lax.all_to_all(parts, "chip", 0, 0)
+    state, parts = after((state_m, parts))
     gen1, cap1, bar_commit2, commit2, start2, window2 = call(
         late_kernel, [(square, F32)] * 6,
-        place, par, state_m, state_o, commit1, start1, window1, grad2, bar_start2, reach2,
-    )
+        par, state, swap(state), commit1, start1, window1, grad2, bar_start2, reach2,
+    )
+    state_m, bar_commit2 = after((state_m, bar_commit2))
     spread, gen2_m = call(
         gen2_kernel, [(blocks, BF16), ((half, unit_chip), F32)],
-        parts, state_m, rows_m, rows_o, placed=False,
+        sums, state_m, rows_m, rows_o,
     )
     bars = lax.all_to_all(spread, "chip", 0, 0)
-    gen2_o = swap(gen2_m)
     gen2, cap2 = call(
-        units_kernel, [(square, F32)] * 2, place, par, gen2_m, gen2_o, gen1, cap1, bar_commit2
-    )
+        units_kernel, [(square, F32)] * 2, par, gen2_m, swap(gen2_m), gen1, cap1, bar_commit2
+    )
+    dual1, cap2 = after((dual1, cap2))
     dual2, send = call(
         line2_kernel, [((half + 8, lines), F32)] * 2,
-        place, bars, cols_m, cols_o, flow_m, flow_o, dual1, rows_m, rows_o, demand, balance1,
+        bars, cols_m, cols_o, flow_m, flow_o, dual1, rows_m, rows_o, demand, balance1,
         scratch=held,
     )
     dual2, balance2 = call(
         last_kernel, [((lines, periods), F32), ((1, balance_dual.shape[0]), F32)],
-        place, dual2, swap(send),
+        dual2, swap(send),
     )
     return (gen2, commit2, startup2, dual2, balance2[0], cap2, start2, window2)
 
@@ -463,6 +571,7 @@
         wide, wide, wide, wide, both, wide, wide, wide,
     )
     out_specs = (wide, wide, wide, wide, both, wide, wide, wide)
+
     return jax.shard_map(
         on_device, mesh=mesh, in_specs=in_specs, out_specs=out_specs, check_vma=False
     )

time: 121 us -> 116 us (0.959)
  blocking collectives: 25 us -> 0 us
  starting transfers between devices: 14.7 us -> 34.4 us
  between operations: 14.2 us -> 0.94 us
  waiting for transfers between devices: 21.1 us -> 29.3 us
  Pallas kernels: 38.3 us -> 42.1 us
  local copies, waits for them, and re-layouts: 6.08 us -> 8.11 us
    all_to_all x2 -> x0, blocking collectives: 25 us -> none  [the longest x1 13.6 us: on_device(): parts = lax.all_to_all(parts, 'chip', 0, 0)]
    ppermute x0 -> x7, starting transfers between devices: none -> 14 us  [the longest x3 9.97 us: relay(): return lax.ppermute(piece, 'chip', pairs)]
    ppermute x0 -> x7, waiting for transfers between devices: none -> 13.9 us  [the longest x4 8.34 us: cross(): return lax.ppermute(piece, 'chip', across)]
    all_gather x1 -> x0, waiting for transfers between devices: 9.69 us -> none  [on_device(): every_load = lax.all_gather(load, LINE, axis=0, tiled=True)]
    pallas_call x12 -> x13, Pallas kernels: 38.3 us -> 42.1 us  [the longest x10 20.6 us: call(): pl.pallas_call(kernel, out_shape=shapes, in_specs=[VMEM] * len(args), out...]
    all_to_all x1 -> x2, waiting for transfers between devices: 0.01 us -> 3.66 us  [on_device(): bars = lax.all_to_all(spread, 'chip', 0, 0)]
    all_to_all x1 -> x2, starting transfers between devices: 7.16 us -> 9.58 us  [on_device(): sums = lax.all_to_all(parts, 'chip', 0, 0)]
    unnamed x34 -> x70, local copies, waits for them, and re-layouts: 4.67 us -> 6.7 us
  transfers between devices with their start and end apart: 11 -> 28, of which waited for: 6 -> 12; matrix products, arithmetic and copies ran while one was open for 2% -> 1% of each run, Pallas kernels for 25% -> 17%
where the time goes in v3:
time: 116 us; the launch traced here: 115 us
  Pallas kernels  42.1 us (36%)
  starting transfers between devices  34.4 us (30%)
  waiting for transfers between devices  29.3 us (25%)
  local copies, waits for them, and re-layouts  8.11 us (7%)
    pallas_call x10, Pallas kernels, call(): pl.pallas_call(kernel, out_shape=shapes, in_specs=[VMEM] * len(args), out...  20.6 us
    pallas_call x2, Pallas kernels, unit_columns(): pl.pallas_call(functools.partial(columns_kernel, start), grid=(steps,), o...  14 us
    ppermute x3, starting transfers between devices, relay(): return lax.ppermute(piece, 'chip', pairs)  9.97 us
    all_to_all x2, starting transfers between devices, on_device(): sums = lax.all_to_all(parts, 'chip', 0, 0)  9.58 us
    ppermute x4, waiting for transfers between devices, cross(): return lax.ppermute(piece, 'chip', across)  8.34 us
    pallas_call x1, Pallas kernels, slab_product(): pl.pallas_call(slab_kernel, out_shape=[jax.ShapeDtypeStruct(*shape) for s...  7.51 us
    all_to_all x2, starting transfers between devices, on_device(): bars = lax.all_to_all(spread, 'chip', 0, 0)  7.29 us
    unnamed x70, local copies, waits for them, and re-layouts  6.7 us
  transfers between devices with their start and end apart: 28, of which 12 were waited for; matrix products, arithmetic and copies ran while one was open for 1% of the time, Pallas kernels for 17%

profile of v3, /device:TPU:0, one launch (start us, length us, event | category | flops | bytes accessed | tf_op | source)
XLA Modules:
  0.0 114.9 jit_solution(73540084303101842)
XLA Ops:
  0.6 6.8 %shard_map.233.refs_0_ = f32[256,1024]{1,0:T(8,128)} custom-call(s32[1,1024]{1,0:T(1,128)} %bitcast.22, bf16[256,13824]{1,0:T(8,128)(2,1)} %ptdf.5), custom_call_target="tpu_custom_call" | custom-call | flops 3623878656 | bytes 3538944 | tf_op jit(solution)/shard_map/pallas_call | solution.py:439
  7.5 7.2 %shard_map.234.cols_m = bf16[256,1024]{1,0:T(8,128)(2,1)} custom-call(s32[1,1024]{1,0:T(1,128)} %bitcast.23, bf16[256,13824]{1,0:T(8,128)(2,1)} %ptdf.5, f32[256,1024]{1,0:T(8,128)} %shard_map.233.refs_0_), custom_call_target="tpu_custom_call" | custom-call | flops 3623878656 | bytes 3538944 | tf_op jit(solution)/shard_map/pallas_call | solution.py:439
  14.7 0.5 collective-permute-start
  15.2 3.6 %collective-permute-start.8 = (bf16[864,128]{1,0:T(8,128)(2,1)S(1)}, bf16[864,128]{1,0:T(8,128)(2,1)S(1)}, u32[]{:S(2)}, u32[]{:S(2)}) collective-permute-start(bf16[864,128]{1,0:T(8,128)(2,1)S(1)} %copy-done.7), channel_id=1, source_target_pairs={{4,0},{6,2},{12,4},{14,6},{0,8},{2,10},{8,12},{10,14},{5,1},{7,3},... | collective-permute-start | bytes 663560 | tf_op jit(solution)/shard_map/ppermute | solution.py:469
  18.8 5.3 %collective-permute-done.8.refs_4_ = bf16[864,128]{1,0:T(8,128)(2,1)S(1)} collective-permute-done((bf16[864,128]{1,0:T(8,128)(2,1)S(1)}, bf16[864,128]{1,0:T(8,128)(2,1)S(1)}, u32[]{:S(2)}, u32[]{:S(2)}) %collective-permute-start.8) | collective-permute-done | bytes 221216 | tf_op jit(solution)/shard_map/ppermute | solution.py:469
  24.1 3.4 %collective-permute-start.10 = (bf16[864,128]{1,0:T(8,128)(2,1)S(1)}, bf16[864,128]{1,0:T(8,128)(2,1)S(1)}, u32[]{:S(2)}, u32[]{:S(2)}) collective-permute-start(bf16[864,128]{1,0:T(8,128)(2,1)S(1)} %collective-permute-done.8.refs_4_), channel_id=1, source_target_pairs={{4,0},{6,2},{12,4},{14,6},{0,8},{2,10},{8,12},{10,14},{5,1},{7,3},... | collective-permute-start | bytes 663560 | tf_op jit(solution)/shard_map/ppermute | solution.py:469
  27.5 0.5 collective-permute-start.2
  28.0 0.8 collective-permute-done.2
  28.9 0.5 copy-done.31
  29.3 0.2 copy-done.23
  29.5 0.2 copy-done
  29.7 2.3 %shard_map.235 = (f32[8,64,128]{2,1,0:T(8,128)}, f32[64,512]{1,0:T(8,128)}, f32[64,1]{1,0:T(8,128)}) custom-call(bf16[256,1024]{1,0:T(8,128)(2,1)} %shard_map.234.cols_m, bf16[256,1024]{1,0:T(8,128)(2,1)} %copy-done, f32[256,128]{1,0:T(8,128)} %dual_m.1, f32[256,128]{1,0:T(8,128)} %copy-done.23, f32[1,8]{1,0:T(1,128)} %bitcast.15, f32[1,8]{1,0:T(1,128)} %bitcast.17), custom_call_target="tpu_custom_call" | custom-call | tf_op jit(solution)/shard_map/pallas_call | solution.py:368
  32.0 3.6 %all-to-all-start = ((f32[8,64,128]{2,1,0:T(8,128)}), f32[8,64,128]{2,1,0:T(8,128)S(1)}, u32[]{:S(2)}, u32[]{:S(2)}) async-start(f32[8,64,128]{2,1,0:T(8,128)} %get-tuple-element.61), calls=%async_computation | async-start | bytes 524288 | tf_op jit(solution)/shard_map/all_to_all | solution.py:499
  35.6 3.0 %collective-permute-start.12 = (bf16[864,128]{1,0:T(8,128)(2,1)S(1)}, bf16[864,128]{1,0:T(8,128)(2,1)S(1)}, u32[]{:S(2)}, u32[]{:S(2)}) collective-permute-start(bf16[864,128]{1,0:T(8,128)(2,1)S(1)} %collective-permute-done.10.refs_8_), channel_id=1, source_target_pairs={{4,0},{6,2},{12,4},{14,6},{0,8},{2,10},{8,12},{10,14},{5,1},{7,3},... | collective-permute-start | bytes 663560 | tf_op jit(solution)/shard_map/ppermute | solution.py:469
  38.6 1.5 %collective-permute-start.5 = (bf16[864,128]{1,0:T(8,128)(2,1)S(1)}, bf16[864,128]{1,0:T(8,128)(2,1)S(1)}, u32[]{:S(2)}, u32[]{:S(2)}) collective-permute-start(bf16[864,128]{1,0:T(8,128)(2,1)S(1)} %copy-done.7), channel_id=1, source_target_pairs={{0,2},{2,0},{4,6},{6,4},{8,10},{10,8},{12,14},{14,12},{1,3},{3,1},... | collective-permute-start | bytes 663560 | tf_op jit(solution)/shard_map/ppermute | solution.py:472
  40.1 0.6 collective-permute-start.9
  40.7 0.7 copy.34.par
  41.4 0.7 copy.32.spans_ref
  42.1 2.7 %shard_map.236 = (f32[192,128]{1,0:T(8,128)}, f32[64,128]{1,0:T(8,128)}, f32[64,128]{1,0:T(8,128)}, f32[64,128]{1,0:T(8,128)}, f32[64,128]{1,0:T(8,128)}, /*inde...) custom-call(f32[64,4]{1,0:T(8,128)} %copy.34.par, s32[64,1]{1,0:T(8,128)} %copy.32.spans_ref, f32[64,128]{1,0:T(8,128)} %gen.1, ...), custom_call_target="tpu_custom_call" | custom-call | tf_op jit(solution)/shard_map/pallas_call | solution.py:368
  44.8 1.4 %shard_map.237.rows_m = f32[8,256]{1,0:T(8,128)} custom-call(f32[1,256]{1,0:T(1,128)} %bitcast.14, f32[1,64]{1,0:T(1,128)} %bitcast.12, f32[1,64]{1,0:T(1,128)} %bitcast.18), custom_call_target="tpu_custom_call" | custom-call | tf_op jit(solution)/shard_map/pallas_call | solution.py:368
  46.2 0.5 collective-permute-start.4
  46.7 0.2 collective-permute-done.12.refs_12_
  46.9 1.6 %collective-permute-start.11 = (bf16[864,128]{1,0:T(8,128)(2,1)S(1)}, bf16[864,128]{1,0:T(8,128)(2,1)S(1)}, u32[]{:S(2)}, u32[]{:S(2)}) collective-permute-start(bf16[864,128]{1,0:T(8,128)(2,1)S(1)} %collective-permute-done.10.refs_8_), channel_id=1, source_target_pairs={{0,2},{2,0},{4,6},{6,4},{8,10},{10,8},{12,14},{14,12},{1,3},{3,1},... | collective-permute-start | bytes 663560 | tf_op jit(solution)/shard_map/ppermute | solution.py:472
  48.6 0.4 collective-permute-start.13
  49.0 3.7 %collective-permute-done.9.refs_5_ = bf16[864,128]{1,0:T(8,128)(2,1)S(1)} collective-permute-done((bf16[864,128]{1,0:T(8,128)(2,1)S(1)}, bf16[864,128]{1,0:T(8,128)(2,1)S(1)}, u32[]{:S(2)}, u32[]{:S(2)}) %collective-permute-start.9) | collective-permute-done | bytes 221216 | tf_op jit(solution)/shard_map/ppermute | solution.py:472
  52.7 0.5 collective-permute-start.7
  53.2 0.1 collective-permute-start.14
  53.3 0.0 copy-done.21
  53.3 0.5 copy-done.24
  53.8 0.7 copy-done.1
  54.5 1.9 %shard_map.238 = (bf16[8,64,128]{2,1,0:T(8,128)(2,1)}, f32[2,64,128]{2,1,0:T(8,128)}) custom-call(f32[8,64,128]{2,1,0:T(8,128)} %copy-done.1, f32[192,128]{1,0:T(8,128)} %get-tuple-element.65.pack_m, f32[192,128]{1,0:T(8,128)} %copy-done.24, f32[8,256]{1,0:T(8,128)} %shard_map.237.rows_m, f32[8,256]{1,0:T(8,128)} %copy-done.21), custom_call_target="tpu_custom_call" | custom-call | tf_op jit(solution)/shard_map/pallas_call | solution.py:368
  56.4 0.9 collective-permute-done.11.refs_9_
  57.4 3.7 %collective-permute-done.13.refs_13_ = bf16[864,128]{1,0:T(8,128)(2,1)S(1)} collective-permute-done((bf16[864,128]{1,0:T(8,128)(2,1)S(1)}, bf16[864,128]{1,0:T(8,128)(2,1)S(1)}, u32[]{:S(2)}, u32[]{:S(2)}) %collective-permute-start.13) | collective-permute-done | bytes 221216 | tf_op jit(solution)/shard_map/ppermute | solution.py:472
  61.1 0.5 collective-permute-start.17
  61.6 0.1 collective-permute-start.19
  61.7 0.4 collective-permute-start.16
  62.2 0.1 collective-permute-start.18
  62.2 3.7 %all-to-all-start.1 = ((bf16[8,64,128]{2,1,0:T(8,128)(2,1)}), bf16[8,64,128]{2,1,0:T(8,128)(2,1)S(1)}, u32[]{:S(2)}, u32[]{:S(2)}) async-start(bf16[8,64,128]{2,1,0:T(8,128)(2,1)} %get-tuple-element.66), calls=%async_computation.1 | async-start | bytes 262144 | tf_op jit(solution)/shard_map/all_to_all | solution.py:519
  66.1 0.5 copy-done.18
  66.6 0.1 copy-done.19
  66.7 0.1 copy-done.20
  66.8 7.5 %shard_map.239 = (f32[64,256]{1,0:T(8,128)}, f32[64,256]{1,0:T(8,128)}, f32[8,128]{1,0:T(8,128)}) custom-call(bf16[256,13824]{1,0:T(8,128)(2,1)} %ptdf.5, bf16[864,128]{1,0:T(8,128)(2,1)} %refs_0_.1, bf16[864,128]{1,0:T(8,128)(2,1)} %copy-done.11, bf16[864,128]{1,0:T(8,128)(2,1)} %copy-done.15, bf16[864,128]{1,0:T(8,128)(2,1)} %copy-done.16, ...), custom_call_target="tpu_custom_call" | custom-call | flops 905969664 | bytes 10616832 | tf_op jit(solution)/shard_map/pallas_call | solution.py:418
  74.3 0.2 collective-permute-start.20
  74.5 1.3 %collective-permute-done.20.flow_o = f32[64,256]{1,0:T(8,128)S(1)} collective-permute-done((f32[64,256]{1,0:T(8,128)}, f32[64,256]{1,0:T(8,128)S(1)}, u32[]{:S(2)}, u32[]{:S(2)}) %collective-permute-start.20) | collective-permute-done | bytes 65568 | tf_op jit(solution)/shard_map/ppermute | solution.py:383
  75.8 0.6 copy-done.5
  76.5 2.8 %shard_map.240 = (f32[8,64,128]{2,1,0:T(8,128)}, f32[64,512]{1,0:T(8,128)}, f32[64,1]{1,0:T(8,128)}) custom-call(bf16[8,64,128]{2,1,0:T(8,128)(2,1)} %copy-done.3, bf16[256,1024]{1,0:T(8,128)(2,1)} %shard_map.234.cols_m, bf16[256,1024]{1,0:T(8,128)(2,1)} %copy-done, f32[64,256]{1,0:T(8,128)} %get-tuple-element.75.flow_m, f32[64,256]{1,0:T(8,128)} %copy-done.5, ...), custom_call_target="tpu_custom_call" | custom-call | tf_op jit(solution)/shard_map/pallas_call | solution.py:368
  79.2 6.0 %all-to-all-start.2 = ((f32[8,64,128]{2,1,0:T(8,128)}), f32[8,64,128]{2,1,0:T(8,128)S(1)}, u32[]{:S(2)}, u32[]{:S(2)}) async-start(f32[8,64,128]{2,1,0:T(8,128)} %get-tuple-element.80), calls=%async_computation.2 | async-start | bytes 524288 | tf_op jit(solution)/shard_map/all_to_all | solution.py:535
  85.2 0.1 collective-permute-start.21
  85.3 1.2 %collective-permute-done.21.state_o = f32[2,64,128]{2,1,0:T(8,128)S(1)} collective-permute-done((f32[2,64,128]{2,1,0:T(8,128)S(1)}, f32[2,64,128]{2,1,0:T(8,128)S(1)}, u32[]{:S(2)}, u32[]{:S(2)}) %collective-permute-start.21) | collective-permute-done | bytes 65568 | tf_op jit(solution)/shard_map/ppermute | solution.py:383
  86.6 0.6 copy-done.26
  87.2 1.9 %shard_map.241 = (f32[64,128]{1,0:T(8,128)}, f32[64,128]{1,0:T(8,128)}, f32[64,128]{1,0:T(8,128)}, f32[64,128]{1,0:T(8,128)}, f32[64,128]{1,0:T(8,128)}, /*index=5*/f32[64,128]{1,0:T(8,128)}) custom-call(f32[64,4]{1,0:T(8,128)} %copy.34.par, f32[2,64,128]{2,1,0:T(8,128)} %get-tuple-element.90.state_m.state, f32[2,64,128]{2,1,0:T(8,128)} %copy-done.26, ...), custom_call_target="tpu_custom_call" | custom-call | tf_op jit(solution)/shard_map/pallas_call | solution.py:368
  89.0 5.4 %all-to-all-done.2.parts = f32[8,64,128]{2,1,0:T(8,128)S(1)} async-done(((f32[8,64,128]{2,1,0:T(8,128)}), f32[8,64,128]{2,1,0:T(8,128)S(1)}, u32[]{:S(2)}, u32[]{:S(2)}) %all-to-all-start.2) | async-done | bytes 262176 | tf_op jit(solution)/shard_map/all_to_all | solution.py:535
  94.5 0.7 copy-done.2
  95.2 1.7 %shard_map.242 = (bf16[8,64,128]{2,1,0:T(8,128)(2,1)}, f32[64,128]{1,0:T(8,128)}) custom-call(f32[8,64,128]{2,1,0:T(8,128)} %copy-done.2, f32[2,64,128]{2,1,0:T(8,128)} %get-tuple-element.90.state_m.state, f32[8,256]{1,0:T(8,128)} %shard_map.237.rows_m, f32[8,256]{1,0:T(8,128)} %copy-done.21), custom_call_target="tpu_custom_call" | custom-call | tf_op jit(solution)/shard_map/pallas_call | solution.py:368
  96.9 3.6 %all-to-all-start.3 = ((bf16[8,64,128]{2,1,0:T(8,128)(2,1)}), bf16[8,64,128]{2,1,0:T(8,128)(2,1)S(1)}, u32[]{:S(2)}, u32[]{:S(2)}) async-start(bf16[8,64,128]{2,1,0:T(8,128)(2,1)} %get-tuple-element.98), calls=%async_computation.3 | async-start | bytes 262144 | tf_op jit(solution)/shard_map/all_to_all | solution.py:546
  100.5 1.4 %collective-permute-done.22.gen_o = f32[64,128]{1,0:T(8,128)S(1)} collective-permute-done((f32[64,128]{1,0:T(8,128)}, f32[64,128]{1,0:T(8,128)S(1)}, u32[]{:S(2)}, u32[]{:S(2)}) %collective-permute-start.22) | collective-permute-done | bytes 32800 | tf_op jit(solution)/shard_map/ppermute | solution.py:383
  101.9 0.6 copy-done.27
  102.5 1.7 %shard_map.243 = (f32[64,128]{1,0:T(8,128)}, f32[64,128]{1,0:T(8,128)}) custom-call(f32[64,4]{1,0:T(8,128)} %copy.34.par, f32[64,128]{1,0:T(8,128)} %get-tuple-element.91.gen_m, f32[64,128]{1,0:T(8,128)} %copy-done.27, f32[64,128]{1,0:T(8,128)} %get-tuple-element.92.gen1, f32[64,128]{1,0:T(8,128)} %get-tuple-element.93.cap1, ...), custom_call_target="tpu_custom_call" | custom-call | tf_op jit(solution)/shard_map/pallas_call | solution.py:368
  104.2 3.7 %all-to-all-done.3.bars = bf16[8,64,128]{2,1,0:T(8,128)(2,1)S(1)} async-done(((bf16[8,64,128]{2,1,0:T(8,128)(2,1)}), bf16[8,64,128]{2,1,0:T(8,128)(2,1)S(1)}, u32[]{:S(2)}, u32[]{:S(2)}) %all-to-all-start.3) | async-done | bytes 131104 | tf_op jit(solution)/shard_map/all_to_all | solution.py:546
  107.8 0.7 copy-done.4
  108.5 2.5 %shard_map.244 = (f32[72,256]{1,0:T(8,128)}, f32[72,256]{1,0:T(8,128)}) custom-call(bf16[8,64,128]{2,1,0:T(8,128)(2,1)} %copy-done.4, bf16[256,1024]{1,0:T(8,128)(2,1)} %shard_map.234.cols_m, bf16[256,1024]{1,0:T(8,128)(2,1)} %copy-done, f32[64,256]{1,0:T(8,128)} %get-tuple-element.75.flow_m, f32[64,256]{1,0:T(8,128)} %copy-done.5, ...), custom_call_target="tpu_custom_call" | custom-call | tf_op jit(solution)/shard_map/pallas_call | solution.py:368
  110.9 1.5 %collective-permute-done.23.other = f32[72,256]{1,0:T(8,128)S(1)} collective-permute-done((f32[72,256]{1,0:T(8,128)}, f32[72,256]{1,0:T(8,128)S(1)}, u32[]{:S(2)}, u32[]{:S(2)}) %collective-permute-start.23) | collective-permute-done | bytes 73760 | tf_op jit(solution)/shard_map/ppermute | solution.py:383
  112.4 0.6 copy-done.25
  113.0 1.8 %shard_map.245 = (f32[256,128]{1,0:T(8,128)}, f32[1,8]{1,0:T(1,128)}) custom-call(f32[72,256]{1,0:T(8,128)} %get-tuple-element.103.mine, f32[72,256]{1,0:T(8,128)} %copy-done.25), custom_call_target="tpu_custom_call" | custom-call | tf_op jit(solution)/shard_map/pallas_call | solution.py:368
  (78 shorter events, 0.2 us)
Async XLA Ops:
  7.4 7.7 %copy-start.7 = (bf16[864,128]{1,0:T(8,128)(2,1)S(1)}, bf16[864,128]{1,0:T(8,128)(2,1)}, u32[]{:S(2)}) copy-start(bf16[864,128]{1,0:T(8,128)(2,1)} %refs_0_.1) | copy-start | bytes 663556
  7.4 20.1 %copy-start.22 = (f32[256,128]{1,0:T(8,128)S(1)}, f32[256,128]{1,0:T(8,128)}, u32[]{:S(2)}) copy-start(f32[256,128]{1,0:T(8,128)} %dual_m.1) | copy-start | bytes 393220
  7.4 20.1 %copy-start.29 = (f32[8]{0:T(128)S(1)}, f32[8]{0:T(128)}, u32[]{:S(2)}) copy-start(f32[8]{0:T(128)} %param.32) | copy-start | bytes 100
  7.4 33.2 %copy-start.28 = (f32[64]{0:T(128)S(1)}, f32[64]{0:T(128)}, u32[]{:S(2)}) copy-start(f32[64]{0:T(128)} %param.22) | copy-start | bytes 772
  7.4 33.2 %copy-start.32 = (f32[64]{0:T(128)S(1)}, f32[64]{0:T(128)}, u32[]{:S(2)}) copy-start(f32[64]{0:T(128)} %param.26) | copy-start | bytes 772
  7.5 33.2 %copy-start.33 = (f32[64]{0:T(128)S(1)}, f32[64]{0:T(128)}, u32[]{:S(2)}) copy-start(f32[64]{0:T(128)} %param.25) | copy-start | bytes 772
  7.5 33.2 %copy-start.34 = (f32[64]{0:T(128)S(1)}, f32[64]{0:T(128)}, u32[]{:S(2)}) copy-start(f32[64]{0:T(128)} %param.24) | copy-start | bytes 772
  7.5 33.9 %copy-start.30 = (s32[64]{0:T(128)S(1)}, s32[64]{0:T(128)}, u32[]{:S(2)}) copy-start(s32[64]{0:T(128)} %param.21) | copy-start | bytes 772
  14.7 14.2 %collective-permute-start = (bf16[256,1024]{1,0:T(8,128)(2,1)}, bf16[256,1024]{1,0:T(8,128)(2,1)S(1)}, u32[]{:S(2)}, u32[]{:S(2)}) collective-permute-start(bf16[256,1024]{1,0:T(8,128)(2,1)} %shard_map.234.cols_m), channel_id=1, source_target_pairs={{0,1},{1,0},{2,3},{3,2},{4,5},{5,4},{6,7},{7,6},{8,9},{9,8},{10,11... | collective-permute-start | bytes 1572872 | tf_op jit(solution)/shard_map/ppermute | solution.py:383
  15.2 8.9 %collective-permute-start.8 = (bf16[864,128]{1,0:T(8,128)(2,1)S(1)}, bf16[864,128]{1,0:T(8,128)(2,1)S(1)}, u32[]{:S(2)}, u32[]{:S(2)}) collective-permute-start(bf16[864,128]{1,0:T(8,128)(2,1)S(1)} %copy-done.7), channel_id=1, source_target_pairs={{4,0},{6,2},{12,4},{14,6},{0,8},{2,10},{8,12},{10,14},{5,1},{7,3},... | collective-permute-start | bytes 663560 | tf_op jit(solution)/shard_map/ppermute | solution.py:469
  24.1 41.9 %copy-start.8 = (bf16[864,128]{1,0:T(8,128)(2,1)}, bf16[864,128]{1,0:T(8,128)(2,1)S(1)}, u32[]{:S(2)}) copy-start(bf16[864,128]{1,0:T(8,128)(2,1)S(1)} %collective-permute-done.8.refs_4_) | copy-start | bytes 663556
  24.1 11.5 %collective-permute-start.10 = (bf16[864,128]{1,0:T(8,128)(2,1)S(1)}, bf16[864,128]{1,0:T(8,128)(2,1)S(1)}, u32[]{:S(2)}, u32[]{:S(2)}) collective-permute-start(bf16[864,128]{1,0:T(8,128)(2,1)S(1)} %collective-permute-done.8.refs_4_), channel_id=1, source_target_pairs={{4,0},{6,2},{12,4},{14,6},{0,8},{2,10},{8,12},{10,14},{5,1},{7,3},... | collective-permute-start | bytes 663560 | tf_op jit(solution)/shard_map/ppermute | solution.py:469
  27.5 1.4 %collective-permute-start.1 = (f32[256,128]{1,0:T(8,128)S(1)}, f32[256,128]{1,0:T(8,128)S(1)}, u32[]{:S(2)}, u32[]{:S(2)}) collective-permute-start(f32[256,128]{1,0:T(8,128)S(1)} %copy-done.22), channel_id=1, source_target_pairs={{0,1},{1,0},{2,3},{3,2},{4,5},{5,4},{6,7},{7,6},{8,9},{9,8},{10,11... | collective-permute-start | bytes 393224 | tf_op jit(solution)/shard_map/ppermute | solution.py:383
  27.5 1.3 %collective-permute-start.2 = (f32[8]{0:T(128)S(1)}, f32[8]{0:T(128)S(1)}, u32[]{:S(2)}, u32[]{:S(2)}) collective-permute-start(f32[8]{0:T(128)S(1)} %copy-done.29), channel_id=1, source_target_pairs={{0,1},{1,0},{2,3},{3,2},{4,5},{5,4},{6,7},{7,6},{8,9},{9,8},{10,11... | collective-permute-start | bytes 104 | tf_op jit(solution)/shard_map/ppermute | solution.py:383
  28.8 0.5 copy-start.31
  28.8 0.7 copy-start.23
  28.8 0.8 copy-start
  32.0 21.2 %all-to-all-start = ((f32[8,64,128]{2,1,0:T(8,128)}), f32[8,64,128]{2,1,0:T(8,128)S(1)}, u32[]{:S(2)}, u32[]{:S(2)}) async-start(f32[8,64,128]{2,1,0:T(8,128)} %get-tuple-element.61), calls=%async_computation | async-start | bytes 524288 | tf_op jit(solution)/shard_map/all_to_all | solution.py:499
  35.6 30.4 %copy-start.9 = (bf16[864,128]{1,0:T(8,128)(2,1)}, bf16[864,128]{1,0:T(8,128)(2,1)S(1)}, u32[]{:S(2)}) copy-start(bf16[864,128]{1,0:T(8,128)(2,1)S(1)} %collective-permute-done.10.refs_8_) | copy-start | bytes 663556
  35.6 11.3 %collective-permute-start.12 = (bf16[864,128]{1,0:T(8,128)(2,1)S(1)}, bf16[864,128]{1,0:T(8,128)(2,1)S(1)}, u32[]{:S(2)}, u32[]{:S(2)}) collective-permute-start(bf16[864,128]{1,0:T(8,128)(2,1)S(1)} %collective-permute-done.10.refs_8_), channel_id=1, source_target_pairs={{4,0},{6,2},{12,4},{14,6},{0,8},{2,10},{8,12},{10,14},{5,1},{7,3},... | collective-permute-start | bytes 663560 | tf_op jit(solution)/shard_map/ppermute | solution.py:469
  38.6 10.0 %collective-permute-start.5 = (bf16[864,128]{1,0:T(8,128)(2,1)S(1)}, bf16[864,128]{1,0:T(8,128)(2,1)S(1)}, u32[]{:S(2)}, u32[]{:S(2)}) collective-permute-start(bf16[864,128]{1,0:T(8,128)(2,1)S(1)} %copy-done.7), channel_id=1, source_target_pairs={{0,2},{2,0},{4,6},{6,4},{8,10},{10,8},{12,14},{14,12},{1,3},{3,1},... | collective-permute-start | bytes 663560 | tf_op jit(solution)/shard_map/ppermute | solution.py:472
  40.1 12.6 %collective-permute-start.9 = (bf16[864,128]{1,0:T(8,128)(2,1)S(1)}, bf16[864,128]{1,0:T(8,128)(2,1)S(1)}, u32[]{:S(2)}, u32[]{:S(2)}) collective-permute-start(bf16[864,128]{1,0:T(8,128)(2,1)S(1)} %collective-permute-done.8.refs_4_), channel_id=1, source_target_pairs={{0,2},{2,0},{4,6},{6,4},{8,10},{10,8},{12,14},{14,12},{1,3},{3,1},... | collective-permute-start | bytes 663560 | tf_op jit(solution)/shard_map/ppermute | solution.py:472
  44.8 8.4 %collective-permute-start.3 = (f32[192,128]{1,0:T(8,128)}, f32[192,128]{1,0:T(8,128)S(1)}, u32[]{:S(2)}, u32[]{:S(2)}) collective-permute-start(f32[192,128]{1,0:T(8,128)} %get-tuple-element.65.pack_m), channel_id=1, source_target_pairs={{0,1},{1,0},{2,3},{3,2},{4,5},{5,4},{6,7},{7,6},{8,9},{9,8},{10,11... | collective-permute-start | bytes 294920 | tf_op jit(solution)/shard_map/ppermute | solution.py:383
  46.2 6.4 %collective-permute-start.4 = (f32[8,256]{1,0:T(8,128)}, f32[8,256]{1,0:T(8,128)S(1)}, u32[]{:S(2)}, u32[]{:S(2)}) collective-permute-start(f32[8,256]{1,0:T(8,128)} %shard_map.237.rows_m), channel_id=1, source_target_pairs={{0,1},{1,0},{2,3},{3,2},{4,5},{5,4},{6,7},{7,6},{8,9},{9,8},{10,11... | collective-permute-start | bytes 24584 | tf_op jit(solution)/shard_map/ppermute | solution.py:383
  46.9 19.1 %copy-start.10 = (bf16[864,128]{1,0:T(8,128)(2,1)}, bf16[864,128]{1,0:T(8,128)(2,1)S(1)}, u32[]{:S(2)}) copy-start(bf16[864,128]{1,0:T(8,128)(2,1)S(1)} %collective-permute-done.12.refs_12_) | copy-start | bytes 663556
  46.9 10.4 %collective-permute-start.11 = (bf16[864,128]{1,0:T(8,128)(2,1)S(1)}, bf16[864,128]{1,0:T(8,128)(2,1)S(1)}, u32[]{:S(2)}, u32[]{:S(2)}) collective-permute-start(bf16[864,128]{1,0:T(8,128)(2,1)S(1)} %collective-permute-done.10.refs_8_), channel_id=1, source_target_pairs={{0,2},{2,0},{4,6},{6,4},{8,10},{10,8},{12,14},{14,12},{1,3},{3,1},... | collective-permute-start | bytes 663560 | tf_op jit(solution)/shard_map/ppermute | solution.py:472
  48.6 17.5 %copy-start.11 = (bf16[864,128]{1,0:T(8,128)(2,1)}, bf16[864,128]{1,0:T(8,128)(2,1)S(1)}, u32[]{:S(2)}) copy-start(bf16[864,128]{1,0:T(8,128)(2,1)S(1)} %collective-permute-done.5.refs_1_) | copy-start | bytes 663556
  48.6 12.6 %collective-permute-start.13 = (bf16[864,128]{1,0:T(8,128)(2,1)S(1)}, bf16[864,128]{1,0:T(8,128)(2,1)S(1)}, u32[]{:S(2)}, u32[]{:S(2)}) collective-permute-start(bf16[864,128]{1,0:T(8,128)(2,1)S(1)} %collective-permute-done.12.refs_12_), channel_id=1, source_target_pairs={{0,2},{2,0},{4,6},{6,4},{8,10},{10,8},{12,14},{14,12},{1,3},{3,1},... | collective-permute-start | bytes 663560 | tf_op jit(solution)/shard_map/ppermute | solution.py:472
  52.7 13.4 %copy-start.12 = (bf16[864,128]{1,0:T(8,128)(2,1)}, bf16[864,128]{1,0:T(8,128)(2,1)S(1)}, u32[]{:S(2)}) copy-start(bf16[864,128]{1,0:T(8,128)(2,1)S(1)} %collective-permute-done.9.refs_5_) | copy-start | bytes 663556
  52.7 9.0 %collective-permute-start.6 = (bf16[864,128]{1,0:T(8,128)(2,1)S(1)}, bf16[864,128]{1,0:T(8,128)(2,1)S(1)}, u32[]{:S(2)}, u32[]{:S(2)}) collective-permute-start(bf16[864,128]{1,0:T(8,128)(2,1)S(1)} %copy-done.7), channel_id=1, source_target_pairs={{0,1},{1,0},{2,3},{3,2},{4,5},{5,4},{6,7},{7,6},{8,9},{9,8},{10,11... | collective-permute-start | bytes 663560 | tf_op jit(solution)/shard_map/ppermute | solution.py:383
  52.7 0.7 copy-start.21
  52.7 9.0 %collective-permute-start.7 = (bf16[864,128]{1,0:T(8,128)(2,1)S(1)}, bf16[864,128]{1,0:T(8,128)(2,1)S(1)}, u32[]{:S(2)}, u32[]{:S(2)}) collective-permute-start(bf16[864,128]{1,0:T(8,128)(2,1)S(1)} %collective-permute-done.5.refs_1_), channel_id=1, source_target_pairs={{0,1},{1,0},{2,3},{3,2},{4,5},{5,4},{6,7},{7,6},{8,9},{9,8},{10,11... | collective-permute-start | bytes 663560 | tf_op jit(solution)/shard_map/ppermute | solution.py:383
  53.2 0.6 copy-start.24
  53.2 9.0 %collective-permute-start.14 = (bf16[864,128]{1,0:T(8,128)(2,1)S(1)}, bf16[864,128]{1,0:T(8,128)(2,1)S(1)}, u32[]{:S(2)}, u32[]{:S(2)}) collective-permute-start(bf16[864,128]{1,0:T(8,128)(2,1)S(1)} %collective-permute-done.8.refs_4_), channel_id=1, source_target_pairs={{0,1},{1,0},{2,3},{3,2},{4,5},{5,4},{6,7},{7,6},{8,9},{9,8},{10,11... | collective-permute-start | bytes 663560 | tf_op jit(solution)/shard_map/ppermute | solution.py:383
  53.8 0.7 copy-start.1
  56.4 28.8 %copy-start.6 = (f32[2,64,128]{2,1,0:T(8,128)S(1)}, f32[2,64,128]{2,1,0:T(8,128)}, u32[]{:S(2)}) copy-start(f32[2,64,128]{2,1,0:T(8,128)} %get-tuple-element.90.state_m.state) | copy-start | bytes 196612
  57.4 8.7 %copy-start.13 = (bf16[864,128]{1,0:T(8,128)(2,1)}, bf16[864,128]{1,0:T(8,128)(2,1)S(1)}, u32[]{:S(2)}) copy-start(bf16[864,128]{1,0:T(8,128)(2,1)S(1)} %collective-permute-done.11.refs_9_) | copy-start | bytes 663556
  61.1 5.0 %copy-start.14 = (bf16[864,128]{1,0:T(8,128)(2,1)}, bf16[864,128]{1,0:T(8,128)(2,1)S(1)}, u32[]{:S(2)}) copy-start(bf16[864,128]{1,0:T(8,128)(2,1)S(1)} %collective-permute-done.13.refs_13_) | copy-start | bytes 663556
  61.1 4.8 %collective-permute-start.15 = (bf16[864,128]{1,0:T(8,128)(2,1)S(1)}, bf16[864,128]{1,0:T(8,128)(2,1)S(1)}, u32[]{:S(2)}, u32[]{:S(2)}) collective-permute-start(bf16[864,128]{1,0:T(8,128)(2,1)S(1)} %collective-permute-done.9.refs_5_), channel_id=1, source_target_pairs={{0,1},{1,0},{2,3},{3,2},{4,5},{5,4},{6,7},{7,6},{8,9},{9,8},{10,11... | collective-permute-start | bytes 663560 | tf_op jit(solution)/shard_map/ppermute | solution.py:383
  61.1 4.8 %collective-permute-start.17 = (bf16[864,128]{1,0:T(8,128)(2,1)S(1)}, bf16[864,128]{1,0:T(8,128)(2,1)S(1)}, u32[]{:S(2)}, u32[]{:S(2)}) collective-permute-start(bf16[864,128]{1,0:T(8,128)(2,1)S(1)} %collective-permute-done.11.refs_9_), channel_id=1, source_target_pairs={{0,1},{1,0},{2,3},{3,2},{4,5},{5,4},{6,7},{7,6},{8,9},{9,8},{10,11... | collective-permute-start | bytes 663560 | tf_op jit(solution)/shard_map/ppermute | solution.py:383
  61.6 4.5 %copy-start.15 = (bf16[864,128]{1,0:T(8,128)(2,1)}, bf16[864,128]{1,0:T(8,128)(2,1)S(1)}, u32[]{:S(2)}) copy-start(bf16[864,128]{1,0:T(8,128)(2,1)S(1)} %collective-permute-done.6.refs_2_) | copy-start | bytes 663556
  61.6 4.4 %collective-permute-start.19 = (bf16[864,128]{1,0:T(8,128)(2,1)S(1)}, bf16[864,128]{1,0:T(8,128)(2,1)S(1)}, u32[]{:S(2)}, u32[]{:S(2)}) collective-permute-start(bf16[864,128]{1,0:T(8,128)(2,1)S(1)} %collective-permute-done.13.refs_13_), channel_id=1, source_target_pairs={{0,1},{1,0},{2,3},{3,2},{4,5},{5,4},{6,7},{7,6},{8,9},{9,8},{10,11... | collective-permute-start | bytes 663560 | tf_op jit(solution)/shard_map/ppermute | solution.py:383
  61.7 4.4 %copy-start.16 = (bf16[864,128]{1,0:T(8,128)(2,1)}, bf16[864,128]{1,0:T(8,128)(2,1)S(1)}, u32[]{:S(2)}) copy-start(bf16[864,128]{1,0:T(8,128)(2,1)S(1)} %collective-permute-done.7.refs_3_) | copy-start | bytes 663556
  61.7 4.3 %collective-permute-start.16 = (bf16[864,128]{1,0:T(8,128)(2,1)S(1)}, bf16[864,128]{1,0:T(8,128)(2,1)}, u32[]{:S(2)}, u32[]{:S(2)}) collective-permute-start(bf16[864,128]{1,0:T(8,128)(2,1)S(1)} %collective-permute-done.10.refs_8_), channel_id=1, source_target_pairs={{0,1},{1,0},{2,3},{3,2},{4,5},{5,4},{6,7},{7,6},{8,9},{9,8},{10,11... | collective-permute-start | bytes 663560 | tf_op jit(solution)/shard_map/ppermute | solution.py:383
  62.2 4.0 %copy-start.17 = (bf16[864,128]{1,0:T(8,128)(2,1)}, bf16[864,128]{1,0:T(8,128)(2,1)S(1)}, u32[]{:S(2)}) copy-start(bf16[864,128]{1,0:T(8,128)(2,1)S(1)} %collective-permute-done.14.refs_6_) | copy-start | bytes 663556
  62.2 3.9 %collective-permute-start.18 = (bf16[864,128]{1,0:T(8,128)(2,1)S(1)}, bf16[864,128]{1,0:T(8,128)(2,1)}, u32[]{:S(2)}, u32[]{:S(2)}) collective-permute-start(bf16[864,128]{1,0:T(8,128)(2,1)S(1)} %collective-permute-done.12.refs_12_), channel_id=1, source_target_pairs={{0,1},{1,0},{2,3},{3,2},{4,5},{5,4},{6,7},{7,6},{8,9},{9,8},{10,11... | collective-permute-start | bytes 663560 | tf_op jit(solution)/shard_map/ppermute | solution.py:383
  62.2 12.3 %all-to-all-start.1 = ((bf16[8,64,128]{2,1,0:T(8,128)(2,1)}), bf16[8,64,128]{2,1,0:T(8,128)(2,1)S(1)}, u32[]{:S(2)}, u32[]{:S(2)}) async-start(bf16[8,64,128]{2,1,0:T(8,128)(2,1)} %get-tuple-element.66), calls=%async_computation.1 | async-start | bytes 262144 | tf_op jit(solution)/shard_map/all_to_all | solution.py:519
  66.0 0.7 copy-start.18
  66.0 0.8 copy-start.19
  66.0 0.8 copy-start.20
  74.3 1.5 %collective-permute-start.20 = (f32[64,256]{1,0:T(8,128)}, f32[64,256]{1,0:T(8,128)S(1)}, u32[]{:S(2)}, u32[]{:S(2)}) collective-permute-start(f32[64,256]{1,0:T(8,128)} %get-tuple-element.76), channel_id=1, source_target_pairs={{0,1},{1,0},{2,3},{3,2},{4,5},{5,4},{6,7},{7,6},{8,9},{9,8},{10,11... | collective-permute-start | bytes 196616 | tf_op jit(solution)/shard_map/ppermute | solution.py:383
  74.5 1.3 %copy-start.3 = (bf16[8,64,128]{2,1,0:T(8,128)(2,1)}, bf16[8,64,128]{2,1,0:T(8,128)(2,1)S(1)}, u32[]{:S(2)}) copy-start(bf16[8,64,128]{2,1,0:T(8,128)(2,1)S(1)} %all-to-all-done.1.bars) | copy-start | bytes 393220
  75.8 0.6 copy-start.5
  79.2 15.2 %all-to-all-start.2 = ((f32[8,64,128]{2,1,0:T(8,128)}), f32[8,64,128]{2,1,0:T(8,128)S(1)}, u32[]{:S(2)}, u32[]{:S(2)}) async-start(f32[8,64,128]{2,1,0:T(8,128)} %get-tuple-element.80), calls=%async_computation.2 | async-start | bytes 524288 | tf_op jit(solution)/shard_map/all_to_all | solution.py:535
  85.2 1.3 %collective-permute-start.21 = (f32[2,64,128]{2,1,0:T(8,128)S(1)}, f32[2,64,128]{2,1,0:T(8,128)S(1)}, u32[]{:S(2)}, u32[]{:S(2)}) collective-permute-start(f32[2,64,128]{2,1,0:T(8,128)S(1)} %copy-done.6), channel_id=1, source_target_pairs={{0,1},{1,0},{2,3},{3,2},{4,5},{5,4},{6,7},{7,6},{8,9},{9,8},{10,11... | collective-permute-start | bytes 196616 | tf_op jit(solution)/shard_map/ppermute | solution.py:383
  86.6 0.6 copy-start.26
  94.5 0.7 copy-start.2
  96.9 10.9 %all-to-all-start.3 = ((bf16[8,64,128]{2,1,0:T(8,128)(2,1)}), bf16[8,64,128]{2,1,0:T(8,128)(2,1)S(1)}, u32[]{:S(2)}, u32[]{:S(2)}) async-start(bf16[8,64,128]{2,1,0:T(8,128)(2,1)} %get-tuple-element.98), calls=%async_computation.3 | async-start | bytes 262144 | tf_op jit(solution)/shard_map/all_to_all | solution.py:546
  100.5 1.4 %collective-permute-start.22 = (f32[64,128]{1,0:T(8,128)}, f32[64,128]{1,0:T(8,128)S(1)}, u32[]{:S(2)}, u32[]{:S(2)}) collective-permute-start(f32[64,128]{1,0:T(8,128)} %get-tuple-element.91.gen_m), channel_id=1, source_target_pairs={{0,1},{1,0},{2,3},{3,2},{4,5},{5,4},{6,7},{7,6},{8,9},{9,8},{10,11... | collective-permute-start | bytes 98312 | tf_op jit(solution)/shard_map/ppermute | solution.py:383
  101.9 0.6 copy-start.27
  107.8 0.7 copy-start.4
  110.9 1.5 %collective-permute-start.23 = (f32[72,256]{1,0:T(8,128)}, f32[72,256]{1,0:T(8,128)S(1)}, u32[]{:S(2)}, u32[]{:S(2)}) collective-permute-start(f32[72,256]{1,0:T(8,128)} %get-tuple-element.104), channel_id=1, source_target_pairs={{0,1},{1,0},{2,3},{3,2},{4,5},{5,4},{6,7},{7,6},{8,9},{9,8},{10,11... | collective-permute-start | bytes 221192 | tf_op jit(solution)/shard_map/ppermute | solution.py:383
  112.4 0.6 copy-start.25

commit v4 on v3

v4 whole, which is shorter than its diff:
```python
import jax
import jax.numpy as jnp
from jax import lax
from jax.experimental import pallas as pl
from jax.experimental.pallas import tpu as pltpu
from jax.sharding import Mesh, PartitionSpec as P

TAU = 0.05
SIGMA = 0.5
SPAN_BITS = 5

F32 = jnp.float32
BF16 = jnp.bfloat16
LINE = ("chip", "core")
SWAP = [(0, 1), (1, 0)]
VMEM = pl.BlockSpec(memory_space=pltpu.VMEM)
HBM = pl.BlockSpec(memory_space=pltpu.HBM)


def shift_right(values, amount):
    lanes = lax.broadcasted_iota(jnp.int32, values.shape, 1)
    return jnp.where(lanes >= amount, pltpu.roll(values, amount, 1), 0.0)


def shift_left(values, amount):
    periods = values.shape[1]
    lanes = lax.broadcasted_iota(jnp.int32, values.shape, 1)
    return jnp.where(lanes < periods - amount, pltpu.roll(values, periods - amount, 1), 0.0)


def window_sum(values, spans, shift):
    block = values
    total = jnp.zeros_like(values)
    for bit in range(SPAN_BITS):
        chosen = (lax.shift_right_logical(spans, bit) & 1) == 1
        total = jnp.where(chosen, block + shift(total, 1 << bit), total)
        if bit + 1 < SPAN_BITS:
            block = block + shift(block, 1 << bit)
    return total


def diagonal(rows, columns):
    shape = (rows, columns)
    return lax.broadcasted_iota(jnp.int32, shape, 0) == lax.broadcasted_iota(jnp.int32, shape, 1)


def to_column(row):
    size = row.shape[1]
    return jnp.sum(jnp.where(diagonal(size, size), row, 0.0), axis=1, keepdims=True)


def to_row(column):
    size = column.shape[0]
    return jnp.sum(jnp.where(diagonal(size, size), column, 0.0), axis=0, keepdims=True)


def half_of(values, core):
    half = values.shape[0] // 2
    return jnp.where(core == 0, values[:half], values[half:])


def by_core(mine, other, core):
    return jnp.where(
        core == 0,
        jnp.concatenate([mine, other], axis=1),
        jnp.concatenate([other, mine], axis=1),
    )


def packed_row(mine, other, index):
    at = mine.shape[0] - 8 + index
    return mine[at:at + 1] + other[at:at + 1]


def packed_limits(mine, other, lines):
    rows = []
    for pack in (mine, other):
        for i in range(lines // pack.shape[1]):
            at = pack.shape[0] - 6 + i
            rows.append(pack[at:at + 1])
    return jnp.concatenate(rows, axis=1)


def ahead_kernel(par, gen_row, cost_row, limit, gen, commit, startup, cap, start, window,
                 pack, startup2, hold):
    gen_max, cost_commit, cost_start, init = (par[:, i:i + 1] for i in range(4))
    spans = jnp.broadcast_to(par[:, 4:5].astype(jnp.int32), commit.shape)
    lanes = lax.broadcasted_iota(jnp.int32, commit.shape, 1)
    c0, s0, sd0, wd0 = commit[...], startup[...], start[...], window[...]
    grad_c = cost_commit - gen_max * cap[...] + sd0 - shift_left(sd0, 1) - wd0
    grad_s = cost_start - sd0 + window_sum(wd0, spans, shift_left)
    c1 = jnp.clip(c0 - TAU * grad_c, 0.0, 1.0)
    s1 = jnp.clip(s0 - TAU * grad_s, 0.0, 1.0)
    bc1 = 2.0 * c1 - c0
    bs1 = 2.0 * s1 - s0
    before = jnp.where(lanes == 0, init, pltpu.roll(bc1, 1, 1))
    sd1 = jnp.maximum(0.0, sd0 + SIGMA * (bc1 - before - bs1))
    wd1 = jnp.maximum(0.0, wd0 + SIGMA * (window_sum(bs1, spans, shift_right) - bc1))
    grad_s2 = cost_start - sd1 + window_sum(wd1, spans, shift_left)
    s2 = jnp.clip(s1 - TAU * grad_s2, 0.0, 1.0)
    bs2 = 2.0 * s2 - s1
    units = gen.shape[0]
    pack[0:units] = gen[...]
    pack[units:2 * units] = cap[...]
    pack[2 * units:3 * units] = bc1
    core, wide = lax.axis_index("core"), pack.shape[1]
    blank = jnp.zeros((1, wide - units), F32)
    table = [pltpu.roll(jnp.concatenate([row[...], blank], axis=1), core * units, 1)
             for row in (gen_row, cost_row)]
    table += [limit[:, i:i + wide] for i in range(0, limit.shape[1], wide)]
    table += [jnp.zeros((1, wide), F32)] * (8 - len(table))
    pack[3 * units:] = jnp.concatenate(table, axis=0)
    startup2[...] = s2
    hold[0] = c1
    hold[1] = cost_commit + sd1 - shift_left(sd1, 1) - wd1
    hold[2] = sd1 - SIGMA * bs2
    hold[3] = wd1 + SIGMA * window_sum(bs2, spans, shift_right)


def columns_kernel(bus, ptdf, cols, acc):
    step = pl.program_id(0)
    depth = ptdf.shape[1]
    here = bus[...] - step * depth
    places = lax.broadcasted_iota(jnp.int32, (depth, bus.shape[1]), 0)
    hot = jnp.where(places == here, 1.0, 0.0).astype(BF16)
    part = jnp.dot(ptdf[...], hot, preferred_element_type=F32)

    @pl.when(step == 0)
    def _():
        acc[...] = part

    @pl.when(step > 0)
    def _():
        acc[...] += part

    @pl.when(step == pl.num_programs(0) - 1)
    def _():
        cols[...] = acc[...].astype(BF16)


def put_parts(part, dual, cols_m, cols_o, balance):
    lines = cols_m.shape[0]
    half = dual.astype(BF16)
    total = jnp.dot(half[:, :lines], cols_m[...], preferred_element_type=F32)
    total += jnp.dot(half[:, lines:], cols_o[...], preferred_element_type=F32)
    total += balance
    wide = part.shape[2]
    for i in range(part.shape[0]):
        part[i] = total[:, i * wide:(i + 1) * wide]


def adjoint_kernel(cols_m, cols_o, dual_m, dual_o, balance_m, balance_o, part, dual_t, balance):
    core, chip = lax.axis_index("core"), lax.axis_index("chip")
    periods = dual_m.shape[1]
    dual = jnp.concatenate([half_of(dual_m[...].T, core), half_of(dual_o[...].T, core)], axis=1)
    dual_t[...] = dual
    own = balance_m.shape[1]
    mine, other = balance_m[...], balance_o[...]
    rest = jnp.zeros((1, periods - 2 * own), F32)
    row = jnp.concatenate([by_core(mine, other, core), rest], axis=1)
    row = pltpu.roll(row, 2 * chip * own, 1)
    column = half_of(to_column(row), core)
    balance[...] = column
    put_parts(part, dual, cols_m, cols_o, column)


def gen_step(parts, gen, cap, pack_m, pack_o):
    weighted = parts[0]
    for i in range(1, parts.shape[0]):
        weighted = weighted + parts[i]
    gen_max = packed_row(pack_m, pack_o, 0)
    cost_gen = packed_row(pack_m, pack_o, 1)
    g1 = jnp.clip(gen - TAU * (cost_gen + (weighted + cap)), 0.0, gen_max)
    return g1, 2.0 * g1 - gen, gen_max


def gen1_kernel(parts, pack_m, pack_o, spread, state):
    core = lax.axis_index("core")
    units = (pack_m.shape[0] - 8) // 3

    def turned(i):
        rows = slice(i * units, (i + 1) * units)
        return by_core(half_of(pack_m[rows].T, core), half_of(pack_o[rows].T, core), core)

    cap = turned(1)
    g1, bar, gen_max = gen_step(parts, turned(0), cap, pack_m, pack_o)
    half = bar.astype(BF16)
    for i in range(spread.shape[0]):
        spread[i] = half
    state[0] = g1
    state[1] = jnp.maximum(0.0, cap + SIGMA * (bar - gen_max * turned(2)))


def gen2_kernel(parts, state, pack_m, pack_o, spread, gen_out):
    g2, bar, _ = gen_step(parts, state[0], state[1], pack_m, pack_o)
    half = bar.astype(BF16)
    for i in range(spread.shape[0]):
        spread[i] = half
    gen_out[...] = g2


def own_units(mine, other, core):
    units = mine.shape[1] // 2
    here, there = mine.T, other.T
    here = jnp.where(core == 0, here[:units], here[units:])
    there = jnp.where(core == 0, there[:units], there[units:])
    return by_core(here, there, core)


def late_kernel(par, state_m, state_o, keep, other, hold,
                gen1, cap1, bar_commit, dual, balance, commit_out, start_out, window_out):
    core = lax.axis_index("core")
    gen_max, init = par[:, 0:1], par[:, 3:4]
    cap = own_units(state_m[1], state_o[1], core)
    gen1[...] = own_units(state_m[0], state_o[0], core)
    half = dual.shape[1] // 2
    dual[...] = by_core(keep[0:half].T, other[0:half].T, core)
    own = balance.shape[1]
    first = (2 * lax.axis_index("chip") + core) * own
    side = first // half
    row = jnp.where(core == side, keep[half:half + 1], other[half:half + 1])
    wide = row.shape[1]
    row = pltpu.roll(row, lax.rem(wide - (first - side * half), wide), 1)
    balance[...] = row[:, :own]
    cap1[...] = cap
    c1, grad, start, window = (hold[i] for i in range(4))
    lanes = lax.broadcasted_iota(jnp.int32, c1.shape, 1)
    c2 = jnp.clip(c1 - TAU * (grad - gen_max * cap), 0.0, 1.0)
    bc2 = 2.0 * c2 - c1
    before = jnp.where(lanes == 0, init, pltpu.roll(bc2, 1, 1))
    commit_out[...] = c2
    bar_commit[...] = bc2
    start_out[...] = jnp.maximum(0.0, start + SIGMA * (bc2 - before))
    window_out[...] = jnp.maximum(0.0, window - SIGMA * bc2)


def units_kernel(par, gen_m, gen_o, gen1, cap1, bar_commit, gen_out, cap_out):
    g2 = own_units(gen_m[...], gen_o[...], lax.axis_index("core"))
    gen_out[...] = g2
    bar = 2.0 * g2 - gen1[...]
    cap_out[...] = jnp.maximum(0.0, cap1[...] + SIGMA * (bar - par[:, 0:1] * bar_commit[...]))


def load_kernel(ptdf, load, keep, send, demand, flow):
    step = pl.program_id(0)
    block = load[...]
    part = jnp.dot(ptdf[...], block, preferred_element_type=F32)
    rows = jnp.sum(block.astype(F32).reshape(-1, 8, block.shape[1]), axis=0)

    @pl.when(step == 0)
    def _():
        flow[...] = part
        demand[...] = rows

    @pl.when(step > 0)
    def _():
        flow[...] += part
        demand[...] += rows

    @pl.when(step == pl.num_programs(0) - 1)
    def _():
        turned = flow[...].T
        core = lax.axis_index("core")
        keep[...] = half_of(turned, core)
        send[...] = half_of(turned, 1 - core)


def slab_kernel(ptdf, *refs):
    pieces, (keep, send, demand, total, slab, buffers, sems) = refs[:-7], refs[-7:]
    core, chip = lax.axis_index("core"), lax.axis_index("chip")
    side, here = chip % 2, chip // 2
    depth = slab.shape[0]
    copies = []
    for i in range(len(pieces) // 4):
        start = pl.multiple_of(jnp.bitwise_xor(here, i) * depth, depth)
        copies.append(
            pltpu.make_async_copy(ptdf.at[:, pl.ds(start, depth)], buffers.at[i], sems.at[i])
        )
        copies[i].start()
    flow, rows = 0.0, 0.0
    for i in range(len(pieces) // 4):
        near, across, swapped, far = (ref[...] for ref in pieces[4 * i:4 * i + 4])
        bus_dev, periods = near.shape
        for yy in range(2):
            for kk in range(2):
                chosen = jnp.where(
                    side == yy,
                    jnp.where(core == kk, near, swapped),
                    jnp.where(core == kk, across, far),
                )
                at = (2 * yy + kk) * bus_dev
                slab[at:at + bus_dev] = chosen
                rows += jnp.sum(chosen.astype(F32).reshape(-1, 8, periods), axis=0)
        copies[i].wait()
        flow += jnp.dot(buffers[i], slab[...], preferred_element_type=F32)
    total[...] = flow
    turned = flow.T
    keep[...] = half_of(turned, core)
    send[...] = half_of(turned, 1 - core)
    demand[...] = rows


def line_step(flows, dual, bound):
    shifted = dual + SIGMA * flows
    return shifted - SIGMA * jnp.clip(shifted / SIGMA, -bound, bound)


def balance_change(bar, demand, units):
    totals = jnp.sum(bar.astype(F32), axis=1, keepdims=True)
    return (totals - demand) / units


TURN = (((1,), (1,)), ((), ()))


def line1_kernel(bars, cols_m, cols_o, flow_m, flow_o, dual, pack_m, pack_o, demand,
                 balance, part, keep, send, held):
    core, chip = lax.axis_index("core"), lax.axis_index("chip")
    lines, units = cols_m.shape
    wide = bars.shape[2]
    for i in range(bars.shape[0]):
        held[:, i * wide:(i + 1) * wide] = bars[i]
    bar = held[...]
    mine = lax.dot_general(bar, cols_m[...], TURN, preferred_element_type=F32) - flow_m[...]
    other = lax.dot_general(bar, cols_o[...], TURN, preferred_element_type=F32) - flow_o[...]
    flows = jnp.concatenate([mine, other], axis=1)
    new = line_step(flows, dual[...], packed_limits(pack_m, pack_o, lines))
    wanted = half_of(to_column(jnp.sum(demand[...], axis=0, keepdims=True)), core)
    moved = balance[...] + balance_change(bar, wanted, units)
    periods = moved.shape[0]
    own = 2 * periods // part.shape[0]
    rows = lax.broadcasted_iota(jnp.int32, moved.shape, 0) + core * periods
    moved = jnp.where((rows >= chip * own) & (rows < (chip + 1) * own), moved, 0.0)
    put_parts(part, new, cols_m, cols_o, moved)
    row = jnp.concatenate([to_row(moved), jnp.zeros((1, lines - periods), F32)], axis=1)
    extra = jnp.broadcast_to(row, (8, lines))
    keep[0:periods] = new[:, :lines]
    keep[periods:] = extra
    send[0:periods] = new[:, lines:]
    send[periods:] = extra


def line2_kernel(bars_m, bars_o, cols, flow, dual, limit, demand, balance, dual_out, balance_out,
                 held):
    core, chip = lax.axis_index("core"), lax.axis_index("chip")
    half, wide = bars_m.shape[1:]
    for i in range(bars_m.shape[0]):
        here, there = bars_m[i], bars_o[i]
        held[0:half, i * wide:(i + 1) * wide] = jnp.where(core == 0, here, there)
        held[half:, i * wide:(i + 1) * wide] = jnp.where(core == 0, there, here)
    bar = held[...]
    flows = lax.dot_general(cols[...], bar, TURN, preferred_element_type=F32) - flow[...]
    dual_out[...] = line_step(flows, dual[...], limit[...])
    wanted = to_column(jnp.sum(demand[...], axis=0, keepdims=True))
    change = to_row(balance_change(bar, wanted, cols.shape[1]))
    own = balance_out.shape[1]
    first = (2 * chip + core) * own
    wide = change.shape[1]
    change = pltpu.roll(change, lax.rem(wide - first, wide), 1)
    balance_out[...] = balance[...] + change[:, :own]


def work(flops, moved):
    return pl.CostEstimate(flops=flops, bytes_accessed=moved, transcendentals=0)


def room(mib):
    return pltpu.CompilerParams(vmem_limit_bytes=mib << 20)


def call(kernel, outs, *args, scratch=(), cost=None):
    shapes = [jax.ShapeDtypeStruct(shape, dtype) for shape, dtype in outs]
    return pl.pallas_call(
        kernel,
        out_shape=shapes,
        in_specs=[VMEM] * len(args),
        out_specs=[VMEM] * len(shapes),
        scratch_shapes=scratch,
        cost_estimate=cost,
        compiler_params=room(8),
    )(*args)


def block_depth(buses, most):
    return max(d for d in range(128, most + 1, 128) if buses % d == 0)


def swap(values):
    return lax.ppermute(values, "core", SWAP)


def gathered_product(ptdf, every_load):
    lines, buses = ptdf.shape
    periods = every_load.shape[1]
    half = periods // 2
    depth = block_depth(buses, 4608)
    return pl.pallas_call(
        load_kernel,
        grid=(buses // depth,),
        out_shape=[
            jax.ShapeDtypeStruct((half, lines), F32),
            jax.ShapeDtypeStruct((half, lines), F32),
            jax.ShapeDtypeStruct((8, periods), F32),
            jax.ShapeDtypeStruct((lines, periods), F32),
        ],
        in_specs=[
            pl.BlockSpec((lines, depth), lambda k: (0, k)),
            pl.BlockSpec((depth, periods), lambda k: (k, 0)),
        ],
        out_specs=[
            pl.BlockSpec((half, lines), lambda k: (0, 0)),
            pl.BlockSpec((half, lines), lambda k: (0, 0)),
            pl.BlockSpec((8, periods), lambda k: (0, 0)),
            pl.BlockSpec((lines, periods), lambda k: (0, 0)),
        ],
        cost_estimate=work(2 * periods * lines * buses, ptdf.size * 2 + every_load.size * 2),
    )(ptdf, every_load)


def slab_product(ptdf, pieces):
    lines, buses = ptdf.shape
    bus_dev, periods = pieces[0].shape
    shapes = [((periods // 2, lines), F32)] * 2 + [((8, periods), F32), ((lines, periods), F32)]
    return pl.pallas_call(
        slab_kernel,
        out_shape=[jax.ShapeDtypeStruct(*shape) for shape in shapes],
        in_specs=[HBM] + [VMEM] * len(pieces),
        out_specs=[VMEM] * len(shapes),
        scratch_shapes=[
            pltpu.VMEM((4 * bus_dev, periods), BF16),
            pltpu.VMEM((len(pieces) // 4, lines, 4 * bus_dev), BF16),
            pltpu.SemaphoreType.DMA((len(pieces) // 4,)),
        ],
        cost_estimate=work(2 * lines * periods * buses, buses * (lines + periods) * 2),
        compiler_params=room(16),
    )(ptdf, *pieces)


def unit_columns(ptdf, unit_bus):
    lines, buses = ptdf.shape
    units = unit_bus.shape[0]
    depth = block_depth(buses, 2304)
    return pl.pallas_call(
        columns_kernel,
        grid=(buses // depth,),
        out_shape=jax.ShapeDtypeStruct((lines, units), BF16),
        in_specs=[
            pl.BlockSpec((1, units), lambda k: (0, 0)),
            pl.BlockSpec((lines, depth), lambda k: (0, k)),
        ],
        out_specs=pl.BlockSpec((lines, units), lambda k: (0, 0)),
        scratch_shapes=[pltpu.VMEM((lines, units), F32)],
        cost_estimate=work(2 * units * lines * buses, ptdf.size * 2),
        compiler_params=room(24),
    )(unit_bus[None], ptdf)


def on_device(
    ptdf, load, unit_bus, min_up, gen_max, cost_gen, cost_commit, cost_start, init_commit,
    line_limit, gen, commit, startup, line_dual, balance_dual, cap_dual, start_dual, window_dual,
):
    unit_dev, periods = gen.shape
    lines, _ = ptdf.shape
    units = unit_bus.shape[0]
    chips = lax.axis_size("chip")
    half = periods // 2
    unit_chip = 2 * unit_dev
    across = [(i, i ^ 1) for i in range(chips)]
    by_slab = chips == 8 and 4 * load.shape[0] % 128 == 0
    after = lax.optimization_barrier

    def along(turn):
        pairs = [(i, i ^ 2 * turn) for i in range(chips)]
        return lax.ppermute(load, "chip", pairs)

    def cross(piece):
        return lax.ppermute(piece, "chip", across)

    if by_slab:
        near = [load, along(1), along(2), along(3)]
        far = [cross(load)]
    else:
        every_load = lax.all_gather(load, LINE, axis=0, tiled=True)
    dual_o, balance_o = swap(line_dual), swap(balance_dual)
    ptdf = pltpu.with_memory_space_constraint(ptdf, pltpu.HBM)

    cols_m = unit_columns(ptdf, unit_bus)
    if by_slab:
        near[1] = after((near[1], cols_m))[0]
        far.append(cross(near[1]))
    cols_o = swap(cols_m)

    blocks = (chips, half, unit_chip)
    parts, dual0, balance0 = call(
        adjoint_kernel, [(blocks, F32), ((half, 2 * lines), F32), ((half, 1), F32)],
        cols_m, cols_o, line_dual, dual_o, balance_dual[None], balance_o[None],
    )
    commit, startup, gen_max, min_up, parts = after((commit, startup, gen_max, min_up, parts))
    sums = lax.all_to_all(parts, "chip", 0, 0)
    if by_slab:
        near[2:] = after((*near[2:], parts))[:2]
        far.append(cross(near[2]))
        far.append(cross(near[3]))
    par = jnp.stack(
        [gen_max, cost_commit, cost_start, init_commit, min_up.astype(F32)], axis=1
    )
    square = (unit_dev, periods)
    pack_m, startup2, hold = call(
        ahead_kernel,
        [((3 * unit_dev + 8, periods), F32), (square, F32), ((4, *square), F32)], par,
        gen_max[None], cost_gen[None], line_limit[None], gen, commit, startup, cap_dual, start_dual, window_dual,
    )
    pack_o = swap(pack_m)
    spread, state_m = call(
        gen1_kernel, [(blocks, BF16), ((2, half, unit_chip), F32)],
        sums, pack_m, pack_o,
    )

    bars = lax.all_to_all(spread, "chip", 0, 0)
    if by_slab:
        far[2:] = after((*far[2:], spread))[:2]
        near_o = [swap(piece) for piece in near]
        far_o = [swap(piece) for piece in far[:2]]
        far_o += [swap(piece) for piece in far[2:]]
        pieces = [list(four) for four in zip(near, far, near_o, far_o)]
        flow_m, send, demand, flow = slab_product(ptdf, sum(pieces, []))
    else:
        flow_m, send, demand, flow = gathered_product(ptdf, every_load)
    flow_o = swap(send)

    parts, keep, send = call(
        line1_kernel, [(blocks, F32)] + [((half + 8, lines), F32)] * 2,
        bars, cols_m, cols_o, flow_m, flow_o, dual0, pack_m, pack_o, demand, balance0,
        scratch=[pltpu.VMEM((half, units), BF16)],
    )
    sums = lax.all_to_all(parts, "chip", 0, 0)
    state, par, line_limit, parts = after((state_m, par, line_limit, parts))
    limit = line_limit[:, None]
    small = ((1, balance_dual.shape[0]), F32)
    state_o, dual_o = swap(state), swap(send)
    gen1, cap1, bar_commit2, dual1, balance1, commit2, start2, window2 = call(
        late_kernel,
        [(square, F32)] * 3 + [((lines, periods), F32), small] + [(square, F32)] * 3,
        par, state, state_o, keep, dual_o, hold,
    )
    state_m, bar_commit2, limit = after((state_m, bar_commit2, limit))
    spread, gen2_m = call(
        gen2_kernel, [(blocks, BF16), ((half, unit_chip), F32)], sums, state_m, pack_m, pack_o,
    )
    bars = lax.all_to_all(spread, "chip", 0, 0)
    gen2_o = swap(gen2_m)
    gen2, cap2 = call(
        units_kernel, [(square, F32)] * 2, par, gen2_m, gen2_o, gen1, cap1, bar_commit2
    )
    dual1, cap2 = after((dual1, cap2))
    dual2, balance2 = call(
        line2_kernel, [((lines, periods), F32), small],
        bars, swap(bars), cols_m, flow, dual1, limit, demand, balance1,
        scratch=[pltpu.VMEM((periods, units), BF16)],
    )
    return (gen2, commit2, startup2, dual2, balance2[0], cap2, start2, window2)


def solution(mesh):
    groups, lines = mesh.devices.shape
    mesh = Mesh(mesh.devices.reshape(groups, lines // 2, 2), ("grp", *LINE))
    wide = P(LINE, "grp")
    unit = P(LINE)
    both = P(("grp", *LINE))
    in_specs = (
        P(LINE, None), wide, P(), unit, unit, unit, unit, unit, unit, unit,
        wide, wide, wide, wide, both, wide, wide, wide,
    )
    out_specs = (wide, wide, wide, wide, both, wide, wide, wide)

    return jax.shard_map(
        on_device, mesh=mesh, in_specs=in_specs, out_specs=out_specs, check_vma=False
    )
```

time: 116 us -> 101 us (0.87)
  Pallas kernels: 42.1 us -> 25 us
  blocking collectives: 0 us -> 10.7 us
  starting transfers between devices: 34.4 us -> 30.9 us
  waiting for transfers between devices: 29.3 us -> 26.4 us
  local copies, waits for them, and re-layouts: 8.11 us -> 5.87 us
    pallas_call x10 -> x8, Pallas kernels: 20.6 us -> 7.49 us  [call(): pl.pallas_call(kernel, out_shape=shapes, in_specs=[VMEM] * len(args), out...]
    all_to_all x0 -> x1, blocking collectives: none -> 10.7 us  [on_device(): bars = lax.all_to_all(spread, 'chip', 0, 0)]
    all_to_all x2, waiting for transfers between devices: 5.42 us -> 10.5 us  [on_device(): sums = lax.all_to_all(parts, 'chip', 0, 0)]
    all_to_all x2 -> x1, waiting for transfers between devices: 3.66 us -> 0.01 us  [on_device(): bars = lax.all_to_all(spread, 'chip', 0, 0)]
    pallas_call x2 -> x1, Pallas kernels: 14 us -> 10.6 us  [unit_columns(): pl.pallas_call(columns_kernel, grid=(buses // depth,), out_shape=jax.Shap...]
    ppermute x17, waiting for transfers between devices: 6.3 us -> 3.52 us  [swap(): return lax.ppermute(values, 'core', SWAP)]
    all_to_all x2 -> x1, starting transfers between devices: 7.29 us -> 5.13 us  [on_device(): bars = lax.all_to_all(spread, 'chip', 0, 0)]
    ppermute x3, starting transfers between devices: 9.97 us -> 7.87 us  [along(): return lax.ppermute(load, 'chip', pairs)]
  transfers between devices with their start and end apart: 28 -> 27, of which waited for: 12 -> 9; matrix products, arithmetic and copies ran while one was open for 1% -> 1% of each run, Pallas kernels for 17% -> 12%
where the time goes in v4:
time: 101 us; the launch traced here: 99.9 us
  starting transfers between devices  30.9 us (31%)
  waiting for transfers between devices  26.4 us (26%)
  Pallas kernels  25 us (25%)
  blocking collectives  10.7 us (11%)
  local copies, waits for them, and re-layouts  5.87 us (6%)
    all_to_all x1, blocking collectives, on_device(): bars = lax.all_to_all(spread, 'chip', 0, 0)  10.7 us
    pallas_call x1, Pallas kernels, unit_columns(): pl.pallas_call(columns_kernel, grid=(buses // depth,), out_shape=jax.Shap...  10.6 us
    all_to_all x2, waiting for transfers between devices, on_device(): sums = lax.all_to_all(parts, 'chip', 0, 0)  10.5 us
    all_to_all x2, starting transfers between devices, on_device(): sums = lax.all_to_all(parts, 'chip', 0, 0)  9.41 us
    ppermute x3, starting transfers between devices, along(): return lax.ppermute(load, 'chip', pairs)  7.87 us
    pallas_call x8, Pallas kernels, call(): pl.pallas_call(kernel, out_shape=shapes, in_specs=[VMEM] * len(args), out...  7.49 us
    pallas_call x1, Pallas kernels, slab_product(): pl.pallas_call(slab_kernel, out_shape=[jax.ShapeDtypeStruct(*shape) for s...  6.99 us
    ppermute x4, waiting for transfers between devices, cross(): return lax.ppermute(piece, 'chip', across)  6.29 us
  transfers between devices with their start and end apart: 27, of which 9 were waited for; matrix products, arithmetic and copies ran while one was open for 1% of the time, Pallas kernels for 12%

profile of v4, /device:TPU:0, one launch (start us, length us, event | category | flops | bytes accessed | tf_op | source)
XLA Modules:
  0.0 99.9 jit_solution(3914536395108394083)
XLA Ops:
  0.7 0.7 copy-done.19
  1.5 10.6 %shard_map.233.cols_m.cols = bf16[256,1024]{1,0:T(8,128)(2,1)S(1)} custom-call(s32[1,1024]{1,0:T(1,128)S(1)} %bitcast.21, bf16[256,13824]{1,0:T(8,128)(2,1)} %ptdf.3), custom_call_target="tpu_custom_call" | custom-call | flops 7247757312 | bytes 7077888 | tf_op jit(solution)/shard_map/pallas_call | solution.py:443
  12.0 0.6 collective-permute-start
  12.6 2.6 %collective-permute-start.7 = (bf16[864,128]{1,0:T(8,128)(2,1)S(1)}, bf16[864,128]{1,0:T(8,128)(2,1)S(1)}, u32[]{:S(2)}, u32[]{:S(2)}) collective-permute-start(bf16[864,128]{1,0:T(8,128)(2,1)S(1)} %copy-done), channel_id=1, source_target_pairs={{0,4},{2,6},{4,0},{6,2},{8,12},{10,14},{12,8},{14,10},{1,5},{3,7},... | collective-permute-start | bytes 663560 | tf_op jit(solution)/shard_map/ppermute | solution.py:474
  15.2 0.1 collective-permute-start.1
  15.4 2.6 %collective-permute-start.11 = (bf16[864,128]{1,0:T(8,128)(2,1)S(1)}, bf16[864,128]{1,0:T(8,128)(2,1)S(1)}, u32[]{:S(2)}, u32[]{:S(2)}) collective-permute-start(bf16[864,128]{1,0:T(8,128)(2,1)S(1)} %copy-done), channel_id=1, source_target_pairs={{0,8},{2,10},{4,12},{6,14},{8,0},{10,2},{12,4},{14,6},{1,9},{3,11}... | collective-permute-start | bytes 663560 | tf_op jit(solution)/shard_map/ppermute | solution.py:474
  18.0 1.5 %collective-permute-start.4 = (bf16[864,128]{1,0:T(8,128)(2,1)S(1)}, bf16[864,128]{1,0:T(8,128)(2,1)S(1)}, u32[]{:S(2)}, u32[]{:S(2)}) collective-permute-start(bf16[864,128]{1,0:T(8,128)(2,1)S(1)} %copy-done), channel_id=1, source_target_pairs={{0,2},{2,0},{4,6},{6,4},{8,10},{10,8},{12,14},{14,12},{1,3},{3,1},... | collective-permute-start | bytes 663560 | tf_op jit(solution)/shard_map/ppermute | solution.py:477
  19.5 6.0 %collective-permute-done.7.refs_4_ = bf16[864,128]{1,0:T(8,128)(2,1)S(1)} collective-permute-done((bf16[864,128]{1,0:T(8,128)(2,1)S(1)}, bf16[864,128]{1,0:T(8,128)(2,1)S(1)}, u32[]{:S(2)}, u32[]{:S(2)}) %collective-permute-start.7) | collective-permute-done | bytes 221216 | tf_op jit(solution)/shard_map/ppermute | solution.py:474
  25.5 0.0 collective-permute-start.2
  25.5 1.2 %collective-permute-done.2 = f32[8]{0:T(128)S(1)} collective-permute-done((f32[8]{0:T(128)S(1)}, f32[8]{0:T(128)S(1)}, u32[]{:S(2)}, u32[]{:S(2)}) %collective-permute-start.2) | collective-permute-done | bytes 64 | tf_op jit(solution)/shard_map/ppermute | solution.py:389
  26.7 2.6 %collective-permute-start.12 = (bf16[864,128]{1,0:T(8,128)(2,1)S(1)}, bf16[864,128]{1,0:T(8,128)(2,1)S(1)}, u32[]{:S(2)}, u32[]{:S(2)}) collective-permute-start(bf16[864,128]{1,0:T(8,128)(2,1)S(1)} %copy-done), channel_id=1, source_target_pairs={{0,12},{2,14},{4,8},{6,10},{8,4},{10,6},{12,0},{14,2},{1,13},{3,15... | collective-permute-start | bytes 663560 | tf_op jit(solution)/shard_map/ppermute | solution.py:474
  29.3 0.0 collective-permute-done.1.dual_o
  29.3 1.5 %collective-permute-start.8 = (bf16[864,128]{1,0:T(8,128)(2,1)S(1)}, bf16[864,128]{1,0:T(8,128)(2,1)S(1)}, u32[]{:S(2)}, u32[]{:S(2)}) collective-permute-start(bf16[864,128]{1,0:T(8,128)(2,1)S(1)} %collective-permute-done.7.refs_4_), channel_id=1, source_target_pairs={{0,2},{2,0},{4,6},{6,4},{8,10},{10,8},{12,14},{14,12},{1,3},{3,1},... | collective-permute-start | bytes 663560 | tf_op jit(solution)/shard_map/ppermute | solution.py:477
  30.8 0.0 collective-permute-done.cols_o
  30.8 1.1 %shard_map.234 = (f32[8,64,128]{2,1,0:T(8,128)}, f32[64,512]{1,0:T(8,128)S(1)}, f32[64,1]{1,0:T(8,128)S(1)}) custom-call(bf16[256,1024]{1,0:T(8,128)(2,1)S(1)} %shard_map.233.cols_m.cols, bf16[256,1024]{1,0:T(8,128)(2,1)S(1)} %collective-permute-done.cols_o, f32[256,128]{1,0:T(8,128)S(1)} %copy-done.1, f32[256,128]{1,0:T(8,128)S(1)} %collective-permute-done.1.dual_o, ...), custom_call_target="tpu_custom_call" | custom-call | tf_op jit(solution)/shard_map/pallas_call | solution.py:373
  31.9 0.6 copy-done.2
  32.6 3.4 %all-to-all-start = ((f32[8,64,128]{2,1,0:T(8,128)}), f32[8,64,128]{2,1,0:T(8,128)S(1)}, u32[]{:S(2)}, u32[]{:S(2)}) async-start(f32[8,64,128]{2,1,0:T(8,128)} %get-tuple-element.56), calls=%async_computation | async-start | bytes 524288 | tf_op jit(solution)/shard_map/all_to_all | solution.py:499
  36.1 0.1 copy.37.par
  36.2 0.5 copy-done.20
  36.7 1.8 %shard_map.235 = (f32[200,128]{1,0:T(8,128)S(1)}, f32[64,128]{1,0:T(8,128)}, f32[4,64,128]{2,1,0:T(8,128)S(1)}) custom-call(f32[64,5]{1,0:T(8,128)S(1)} %copy.37.par, f32[1,64]{1,0:T(1,128)S(1)} %bitcast.17, f32[1,64]{1,0:T(1,128)S(1)} %bitcast.19, f32[1,256]{1,0:T(1,128)S(1)} %bitcast.14, f32[64,128]{1,0:T(8,128)S(1)} %copy-done.7, ...), custom_call_target="tpu_custom_call" | custom-call | tf_op jit(solution)/shard_map/pallas_call | solution.py:373
  38.5 2.0 %collective-permute-start.13 = (bf16[864,128]{1,0:T(8,128)(2,1)S(1)}, bf16[864,128]{1,0:T(8,128)(2,1)S(1)}, u32[]{:S(2)}, u32[]{:S(2)}) collective-permute-start(bf16[864,128]{1,0:T(8,128)(2,1)S(1)} %collective-permute-done.11.refs_8_), channel_id=1, source_target_pairs={{0,2},{2,0},{4,6},{6,4},{8,10},{10,8},{12,14},{14,12},{1,3},{3,1},... | collective-permute-start | bytes 663560 | tf_op jit(solution)/shard_map/ppermute | solution.py:477
  40.5 0.1 collective-permute-start.14
  40.6 0.0 collective-permute-done.4.refs_1_
  40.6 0.1 collective-permute-start.5
  40.7 0.0 collective-permute-done.8.refs_5_
  40.7 0.4 collective-permute-start.6
  41.1 0.0 collective-permute-done.3.pack_o
  41.1 0.1 collective-permute-start.9
  41.2 3.7 %all-to-all-done.parts = f32[8,64,128]{2,1,0:T(8,128)S(1)} async-done(((f32[8,64,128]{2,1,0:T(8,128)}), f32[8,64,128]{2,1,0:T(8,128)S(1)}, u32[]{:S(2)}, u32[]{:S(2)}) %all-to-all-start) | async-done | bytes 262176 | tf_op jit(solution)/shard_map/all_to_all | solution.py:499
  45.0 0.3 shard_map.236
  45.2 0.0 copy-start.6
  45.3 0.6 copy-done.6
  45.9 1.9 %collective-permute-done.13.refs_9_ = bf16[864,128]{1,0:T(8,128)(2,1)S(1)} collective-permute-done((bf16[864,128]{1,0:T(8,128)(2,1)S(1)}, bf16[864,128]{1,0:T(8,128)(2,1)S(1)}, u32[]{:S(2)}, u32[]{:S(2)}) %collective-permute-start.13) | collective-permute-done | bytes 221216 | tf_op jit(solution)/shard_map/ppermute | solution.py:477
  47.8 0.0 collective-permute-start.10
  47.8 4.4 %collective-permute-done.14.refs_13_ = bf16[864,128]{1,0:T(8,128)(2,1)S(1)} collective-permute-done((bf16[864,128]{1,0:T(8,128)(2,1)S(1)}, bf16[864,128]{1,0:T(8,128)(2,1)S(1)}, u32[]{:S(2)}, u32[]{:S(2)}) %collective-permute-start.14) | collective-permute-done | bytes 221216 | tf_op jit(solution)/shard_map/ppermute | solution.py:477
  52.2 0.0 collective-permute-start.15
  52.2 0.0 collective-permute-done.5.refs_2_
  52.2 0.5 collective-permute-start.17
  52.7 0.0 collective-permute-done.6.refs_3_
  52.7 0.1 collective-permute-start.16
  52.8 0.0 collective-permute-done.9.refs_6_
  52.8 0.4 collective-permute-start.18
  53.2 5.1 %all-to-all-start.1 = ((bf16[8,64,128]{2,1,0:T(8,128)(2,1)}), bf16[8,64,128]{2,1,0:T(8,128)(2,1)S(1)}, u32[]{:S(2)}, u32[]{:S(2)}) async-start(bf16[8,64,128]{2,1,0:T(8,128)(2,1)} %copy-done.6), calls=%async_computation.1 | async-start | bytes 262144 | tf_op jit(solution)/shard_map/all_to_all | solution.py:519
  58.4 0.0 collective-permute-done.10.refs_7_
  58.4 0.0 collective-permute-done.16.refs_11_
  58.4 7.0 %shard_map.237 = (f32[64,256]{1,0:T(8,128)S(1)}, f32[64,256]{1,0:T(8,128)}, f32[8,128]{1,0:T(8,128)S(1)}, f32[256,128]{1,0:T(8,128)S(1)}) custom-call(bf16[256,13824]{1,0:T(8,128)(2,1)} %ptdf.3, bf16[864,128]{1,0:T(8,128)(2,1)S(1)} %copy-done, bf16[864,128]{1,0:T(8,128)(2,1)S(1)} %collective-permute-done.4.refs_1_, ...), custom_call_target="tpu_custom_call" | custom-call | flops 905969664 | bytes 10616832 | tf_op jit(solution)/shard_map/pallas_call | solution.py:424
  65.4 0.6 copy-done.4
  66.1 0.0 collective-permute-start.19
  66.1 1.5 %collective-permute-done.19.flow_o = f32[64,256]{1,0:T(8,128)S(1)} collective-permute-done((f32[64,256]{1,0:T(8,128)}, f32[64,256]{1,0:T(8,128)S(1)}, u32[]{:S(2)}, u32[]{:S(2)}) %collective-permute-start.19) | collective-permute-done | bytes 65568 | tf_op jit(solution)/shard_map/ppermute | solution.py:389
  67.5 0.8 copy-done.14
  68.3 1.4 %shard_map.238 = (f32[8,64,128]{2,1,0:T(8,128)}, f32[72,256]{1,0:T(8,128)S(1)}, f32[72,256]{1,0:T(8,128)S(1)}) custom-call(bf16[8,64,128]{2,1,0:T(8,128)(2,1)S(1)} %all-to-all-done.1.bars, bf16[256,1024]{1,0:T(8,128)(2,1)S(1)} %shard_map.233.cols_m.cols, bf16[256,1024]{1,0:T(8,128)(2,1)S(1)} %collective-permute-done.cols_o, ...), custom_call_target="tpu_custom_call" | custom-call | tf_op jit(solution)/shard_map/pallas_call | solution.py:373
  69.7 6.0 %all-to-all-start.2 = ((f32[8,64,128]{2,1,0:T(8,128)}), f32[8,64,128]{2,1,0:T(8,128)S(1)}, u32[]{:S(2)}, u32[]{:S(2)}) async-start(f32[8,64,128]{2,1,0:T(8,128)} %get-tuple-element.74), calls=%async_computation.2 | async-start | bytes 524288 | tf_op jit(solution)/shard_map/all_to_all | solution.py:536
  75.7 0.5 collective-permute-start.20
  76.2 0.8 copy.39.par
  77.0 0.1 collective-permute-done.20.state_o
  77.1 1.0 %shard_map.239 = (f32[64,128]{1,0:T(8,128)S(1)}, f32[64,128]{1,0:T(8,128)S(1)}, f32[64,128]{1,0:T(8,128)S(1)}, f32[256,128]{1,0:T(8,128)S(1)}, f32[1,8]{1,0:T(1,...) custom-call(f32[64,5]{1,0:T(8,128)S(1)} %copy.39.par, ...), custom_call_target="tpu_custom_call" | custom-call | tf_op jit(solution)/shard_map/pallas_call | solution.py:373
  78.2 6.8 %all-to-all-done.2.parts = f32[8,64,128]{2,1,0:T(8,128)S(1)} async-done(((f32[8,64,128]{2,1,0:T(8,128)}), f32[8,64,128]{2,1,0:T(8,128)S(1)}, u32[]{:S(2)}, u32[]{:S(2)}) %all-to-all-start.2) | async-done | bytes 262176 | tf_op jit(solution)/shard_map/all_to_all | solution.py:536
  85.0 10.7 %all_to_all.20.bars_m = bf16[8,64,128]{2,1,0:T(8,128)(2,1)S(1)} all-to-all(bf16[8,64,128]{2,1,0:T(8,128)(2,1)S(1)} %get-tuple-element.90), channel_id=1, replica_groups=mesh['grp'=2,'chip'=8,'core'=2] {'chip'}, dimensions={0} | all-to-all | bytes 262144 | tf_op jit(solution)/shard_map/all_to_all | solution.py:550
  95.7 0.5 collective-permute-start.22
  96.2 0.1 copy.40.limit
  96.4 0.7 collective-permute-done.22.gen_o
  97.1 0.8 shard_map.241
  97.9 0.9 copy-done.5
  98.8 1.1 %shard_map.242 = (f32[256,128]{1,0:T(8,128)}, f32[1,8]{1,0:T(1,128)}) custom-call(bf16[8,64,128]{2,1,0:T(8,128)(2,1)S(1)} %all_to_all.20.bars_m, bf16[8,64,128]{2,1,0:T(8,128)(2,1)S(1)} %collective-permute-done.23.bars_o, bf16[256,1024]{1,0:T(8,128)(2,1)S(1)} %shard_map.233.cols_m.cols, f32[256,128]{1,0:T(8,128)S(1)} %copy-done.5, ...), custom_call_target="tpu_custom_call" | custom-call | tf_op jit(solution)/shard_map/pallas_call | solution.py:373
  (56 shorter events, 0.2 us)
Async XLA Ops:
  0.6 0.7 copy-start.19
  1.3 11.2 %copy-start = (bf16[864,128]{1,0:T(8,128)(2,1)S(1)}, bf16[864,128]{1,0:T(8,128)(2,1)}, u32[]{:S(2)}) copy-start(bf16[864,128]{1,0:T(8,128)(2,1)} %refs_0_.1) | copy-start | bytes 663556
  1.3 13.9 %copy-start.1 = (f32[256,128]{1,0:T(8,128)S(1)}, f32[256,128]{1,0:T(8,128)}, u32[]{:S(2)}) copy-start(f32[256,128]{1,0:T(8,128)} %dual_m.1) | copy-start | bytes 393220
  1.3 24.2 %copy-start.17 = (f32[8]{0:T(128)S(1)}, f32[8]{0:T(128)}, u32[]{:S(2)}) copy-start(f32[8]{0:T(128)} %param.32) | copy-start | bytes 100
  1.3 34.6 %copy-start.24 = (s32[64]{0:T(128)S(1)}, s32[64]{0:T(128)}, u32[]{:S(2)}) copy-start(s32[64]{0:T(128)} %param.21) | copy-start | bytes 772
  1.3 34.7 %copy-start.16 = (f32[64]{0:T(128)S(1)}, f32[64]{0:T(128)}, u32[]{:S(2)}) copy-start(f32[64]{0:T(128)} %param.22) | copy-start | bytes 772
  1.4 34.7 %copy-start.21 = (f32[64]{0:T(128)S(1)}, f32[64]{0:T(128)}, u32[]{:S(2)}) copy-start(f32[64]{0:T(128)} %param.24) | copy-start | bytes 772
  1.4 34.7 %copy-start.22 = (f32[64]{0:T(128)S(1)}, f32[64]{0:T(128)}, u32[]{:S(2)}) copy-start(f32[64]{0:T(128)} %param.25) | copy-start | bytes 772
  1.4 34.7 %copy-start.23 = (f32[64]{0:T(128)S(1)}, f32[64]{0:T(128)}, u32[]{:S(2)}) copy-start(f32[64]{0:T(128)} %param.26) | copy-start | bytes 772
  1.4 35.3 %copy-start.7 = (f32[64,128]{1,0:T(8,128)S(1)}, f32[64,128]{1,0:T(8,128)}, u32[]{:S(2)}) copy-start(f32[64,128]{1,0:T(8,128)} %gen.1) | copy-start | bytes 98308
  1.4 35.3 %copy-start.8 = (f32[64,128]{1,0:T(8,128)S(1)}, f32[64,128]{1,0:T(8,128)}, u32[]{:S(2)}) copy-start(f32[64,128]{1,0:T(8,128)} %commit) | copy-start | bytes 98308
  1.4 35.3 %copy-start.9 = (f32[64,128]{1,0:T(8,128)S(1)}, f32[64,128]{1,0:T(8,128)}, u32[]{:S(2)}) copy-start(f32[64,128]{1,0:T(8,128)} %startup) | copy-start | bytes 98308
  1.4 35.3 %copy-start.10 = (f32[64,128]{1,0:T(8,128)S(1)}, f32[64,128]{1,0:T(8,128)}, u32[]{:S(2)}) copy-start(f32[64,128]{1,0:T(8,128)} %cap.1) | copy-start | bytes 98308
  1.4 35.2 %copy-start.11 = (f32[64,128]{1,0:T(8,128)S(1)}, f32[64,128]{1,0:T(8,128)}, u32[]{:S(2)}) copy-start(f32[64,128]{1,0:T(8,128)} %start.1) | copy-start | bytes 98308
  1.4 35.2 %copy-start.12 = (f32[64,128]{1,0:T(8,128)S(1)}, f32[64,128]{1,0:T(8,128)}, u32[]{:S(2)}) copy-start(f32[64,128]{1,0:T(8,128)} %window.1) | copy-start | bytes 98308
  1.4 35.2 %copy-start.15 = (f32[256]{0:T(256)S(1)}, f32[256]{0:T(256)}, u32[]{:S(2)}) copy-start(f32[256]{0:T(256)} %param.27) | copy-start | bytes 3076
  1.4 35.2 %copy-start.18 = (f32[64]{0:T(128)S(1)}, f32[64]{0:T(128)}, u32[]{:S(2)}) copy-start(f32[64]{0:T(128)} %param.23) | copy-start | bytes 772
  12.0 18.8 %collective-permute-start = (bf16[256,1024]{1,0:T(8,128)(2,1)S(1)}, bf16[256,1024]{1,0:T(8,128)(2,1)S(1)}, u32[]{:S(2)}, u32[]{:S(2)}) collective-permute-start(bf16[256,1024]{1,0:T(8,128)(2,1)S(1)} %shard_map.233.cols_m.cols), channel_id=1, source_target_pairs={{0,1},{1,0},{2,3},{3,2},{4,5},{5,4},{6,7},{7,6},{8,9},{9,8},{10,11... | collective-permute-start | bytes 1572872 | tf_op jit(solution)/shard_map/ppermute | solution.py:389
  12.6 12.9 %collective-permute-start.7 = (bf16[864,128]{1,0:T(8,128)(2,1)S(1)}, bf16[864,128]{1,0:T(8,128)(2,1)S(1)}, u32[]{:S(2)}, u32[]{:S(2)}) collective-permute-start(bf16[864,128]{1,0:T(8,128)(2,1)S(1)} %copy-done), channel_id=1, source_target_pairs={{0,4},{2,6},{4,0},{6,2},{8,12},{10,14},{12,8},{14,10},{1,5},{3,7},... | collective-permute-start | bytes 663560 | tf_op jit(solution)/shard_map/ppermute | solution.py:474
  15.2 14.1 %collective-permute-start.1 = (f32[256,128]{1,0:T(8,128)S(1)}, f32[256,128]{1,0:T(8,128)S(1)}, u32[]{:S(2)}, u32[]{:S(2)}) collective-permute-start(f32[256,128]{1,0:T(8,128)S(1)} %copy-done.1), channel_id=1, source_target_pairs={{0,1},{1,0},{2,3},{3,2},{4,5},{5,4},{6,7},{7,6},{8,9},{9,8},{10,11... | collective-permute-start | bytes 393224 | tf_op jit(solution)/shard_map/ppermute | solution.py:389
  15.4 23.1 %collective-permute-start.11 = (bf16[864,128]{1,0:T(8,128)(2,1)S(1)}, bf16[864,128]{1,0:T(8,128)(2,1)S(1)}, u32[]{:S(2)}, u32[]{:S(2)}) collective-permute-start(bf16[864,128]{1,0:T(8,128)(2,1)S(1)} %copy-done), channel_id=1, source_target_pairs={{0,8},{2,10},{4,12},{6,14},{8,0},{10,2},{12,4},{14,6},{1,9},{3,11}... | collective-permute-start | bytes 663560 | tf_op jit(solution)/shard_map/ppermute | solution.py:474
  18.0 22.7 %collective-permute-start.4 = (bf16[864,128]{1,0:T(8,128)(2,1)S(1)}, bf16[864,128]{1,0:T(8,128)(2,1)S(1)}, u32[]{:S(2)}, u32[]{:S(2)}) collective-permute-start(bf16[864,128]{1,0:T(8,128)(2,1)S(1)} %copy-done), channel_id=1, source_target_pairs={{0,2},{2,0},{4,6},{6,4},{8,10},{10,8},{12,14},{14,12},{1,3},{3,1},... | collective-permute-start | bytes 663560 | tf_op jit(solution)/shard_map/ppermute | solution.py:477
  25.5 1.2 %collective-permute-start.2 = (f32[8]{0:T(128)S(1)}, f32[8]{0:T(128)S(1)}, u32[]{:S(2)}, u32[]{:S(2)}) collective-permute-start(f32[8]{0:T(128)S(1)} %copy-done.17), channel_id=1, source_target_pairs={{0,1},{1,0},{2,3},{3,2},{4,5},{5,4},{6,7},{7,6},{8,9},{9,8},{10,11... | collective-permute-start | bytes 104 | tf_op jit(solution)/shard_map/ppermute | solution.py:389
  26.7 11.9 %collective-permute-start.12 = (bf16[864,128]{1,0:T(8,128)(2,1)S(1)}, bf16[864,128]{1,0:T(8,128)(2,1)S(1)}, u32[]{:S(2)}, u32[]{:S(2)}) collective-permute-start(bf16[864,128]{1,0:T(8,128)(2,1)S(1)} %copy-done), channel_id=1, source_target_pairs={{0,12},{2,14},{4,8},{6,10},{8,4},{10,6},{12,0},{14,2},{1,13},{3,15... | collective-permute-start | bytes 663560 | tf_op jit(solution)/shard_map/ppermute | solution.py:474
  29.3 11.4 %collective-permute-start.8 = (bf16[864,128]{1,0:T(8,128)(2,1)S(1)}, bf16[864,128]{1,0:T(8,128)(2,1)S(1)}, u32[]{:S(2)}, u32[]{:S(2)}) collective-permute-start(bf16[864,128]{1,0:T(8,128)(2,1)S(1)} %collective-permute-done.7.refs_4_), channel_id=1, source_target_pairs={{0,2},{2,0},{4,6},{6,4},{8,10},{10,8},{12,14},{14,12},{1,3},{3,1},... | collective-permute-start | bytes 663560 | tf_op jit(solution)/shard_map/ppermute | solution.py:477
  31.9 0.6 copy-start.2
  32.6 3.6 %copy-start.13 = (f32[64,1]{1,0:T(8,128)}, f32[64,1]{1,0:T(8,128)S(1)}, u32[]{:S(2)}) copy-start(f32[64,1]{1,0:T(8,128)S(1)} %get-tuple-element.73.balance) | copy-start | bytes 772
  32.6 12.4 %all-to-all-start = ((f32[8,64,128]{2,1,0:T(8,128)}), f32[8,64,128]{2,1,0:T(8,128)S(1)}, u32[]{:S(2)}, u32[]{:S(2)}) async-start(f32[8,64,128]{2,1,0:T(8,128)} %get-tuple-element.56), calls=%async_computation | async-start | bytes 524288 | tf_op jit(solution)/shard_map/all_to_all | solution.py:499
  36.1 0.6 copy-start.20
  38.5 2.6 %collective-permute-start.3 = (f32[200,128]{1,0:T(8,128)S(1)}, f32[200,128]{1,0:T(8,128)S(1)}, u32[]{:S(2)}, u32[]{:S(2)}) collective-permute-start(f32[200,128]{1,0:T(8,128)S(1)} %get-tuple-element.61.pack_m), channel_id=1, source_target_pairs={{0,1},{1,0},{2,3},{3,2},{4,5},{5,4},{6,7},{7,6},{8,9},{9,8},{10,11... | collective-permute-start | bytes 307208 | tf_op jit(solution)/shard_map/ppermute | solution.py:389
  38.5 9.3 %collective-permute-start.13 = (bf16[864,128]{1,0:T(8,128)(2,1)S(1)}, bf16[864,128]{1,0:T(8,128)(2,1)S(1)}, u32[]{:S(2)}, u32[]{:S(2)}) collective-permute-start(bf16[864,128]{1,0:T(8,128)(2,1)S(1)} %collective-permute-done.11.refs_8_), channel_id=1, source_target_pairs={{0,2},{2,0},{4,6},{6,4},{8,10},{10,8},{12,14},{14,12},{1,3},{3,1},... | collective-permute-start | bytes 663560 | tf_op jit(solution)/shard_map/ppermute | solution.py:477
  40.5 11.7 %collective-permute-start.14 = (bf16[864,128]{1,0:T(8,128)(2,1)S(1)}, bf16[864,128]{1,0:T(8,128)(2,1)S(1)}, u32[]{:S(2)}, u32[]{:S(2)}) collective-permute-start(bf16[864,128]{1,0:T(8,128)(2,1)S(1)} %collective-permute-done.12.refs_12_), channel_id=1, source_target_pairs={{0,2},{2,0},{4,6},{6,4},{8,10},{10,8},{12,14},{14,12},{1,3},{3,1},... | collective-permute-start | bytes 663560 | tf_op jit(solution)/shard_map/ppermute | solution.py:477
  40.6 11.6 %collective-permute-start.5 = (bf16[864,128]{1,0:T(8,128)(2,1)S(1)}, bf16[864,128]{1,0:T(8,128)(2,1)}, u32[]{:S(2)}, u32[]{:S(2)}) collective-permute-start(bf16[864,128]{1,0:T(8,128)(2,1)S(1)} %copy-done), channel_id=1, source_target_pairs={{0,1},{1,0},{2,3},{3,2},{4,5},{5,4},{6,7},{7,6},{8,9},{9,8},{10,11... | collective-permute-start | bytes 663560 | tf_op jit(solution)/shard_map/ppermute | solution.py:389
  40.7 12.0 %collective-permute-start.6 = (bf16[864,128]{1,0:T(8,128)(2,1)S(1)}, bf16[864,128]{1,0:T(8,128)(2,1)}, u32[]{:S(2)}, u32[]{:S(2)}) collective-permute-start(bf16[864,128]{1,0:T(8,128)(2,1)S(1)} %collective-permute-done.4.refs_1_), channel_id=1, source_target_pairs={{0,1},{1,0},{2,3},{3,2},{4,5},{5,4},{6,7},{7,6},{8,9},{9,8},{10,11... | collective-permute-start | bytes 663560 | tf_op jit(solution)/shard_map/ppermute | solution.py:389
  41.1 11.6 %collective-permute-start.9 = (bf16[864,128]{1,0:T(8,128)(2,1)S(1)}, bf16[864,128]{1,0:T(8,128)(2,1)}, u32[]{:S(2)}, u32[]{:S(2)}) collective-permute-start(bf16[864,128]{1,0:T(8,128)(2,1)S(1)} %collective-permute-done.7.refs_4_), channel_id=1, source_target_pairs={{0,1},{1,0},{2,3},{3,2},{4,5},{5,4},{6,7},{7,6},{8,9},{9,8},{10,11... | collective-permute-start | bytes 663560 | tf_op jit(solution)/shard_map/ppermute | solution.py:389
  45.2 0.7 copy-start.6
  45.9 21.6 %copy-start.3 = (f32[64,512]{1,0:T(8,128)S(1)}, f32[64,512]{1,0:T(8,128)}, u32[]{:S(2)}) copy-start(f32[64,512]{1,0:T(8,128)} %copy-done.2) | copy-start | bytes 393220
  47.8 10.6 %collective-permute-start.10 = (bf16[864,128]{1,0:T(8,128)(2,1)S(1)}, bf16[864,128]{1,0:T(8,128)(2,1)}, u32[]{:S(2)}, u32[]{:S(2)}) collective-permute-start(bf16[864,128]{1,0:T(8,128)(2,1)S(1)} %collective-permute-done.8.refs_5_), channel_id=1, source_target_pairs={{0,1},{1,0},{2,3},{3,2},{4,5},{5,4},{6,7},{7,6},{8,9},{9,8},{10,11... | collective-permute-start | bytes 663560 | tf_op jit(solution)/shard_map/ppermute | solution.py:389
  52.2 6.2 %collective-permute-start.15 = (bf16[864,128]{1,0:T(8,128)(2,1)S(1)}, bf16[864,128]{1,0:T(8,128)(2,1)}, u32[]{:S(2)}, u32[]{:S(2)}) collective-permute-start(bf16[864,128]{1,0:T(8,128)(2,1)S(1)} %collective-permute-done.11.refs_8_), channel_id=1, source_target_pairs={{0,1},{1,0},{2,3},{3,2},{4,5},{5,4},{6,7},{7,6},{8,9},{9,8},{10,11... | collective-permute-start | bytes 663560 | tf_op jit(solution)/shard_map/ppermute | solution.py:389
  52.2 6.2 %collective-permute-start.17 = (bf16[864,128]{1,0:T(8,128)(2,1)S(1)}, bf16[864,128]{1,0:T(8,128)(2,1)}, u32[]{:S(2)}, u32[]{:S(2)}) collective-permute-start(bf16[864,128]{1,0:T(8,128)(2,1)S(1)} %collective-permute-done.12.refs_12_), channel_id=1, source_target_pairs={{0,1},{1,0},{2,3},{3,2},{4,5},{5,4},{6,7},{7,6},{8,9},{9,8},{10,11... | collective-permute-start | bytes 663560 | tf_op jit(solution)/shard_map/ppermute | solution.py:389
  52.7 5.7 %collective-permute-start.16 = (bf16[864,128]{1,0:T(8,128)(2,1)S(1)}, bf16[864,128]{1,0:T(8,128)(2,1)}, u32[]{:S(2)}, u32[]{:S(2)}) collective-permute-start(bf16[864,128]{1,0:T(8,128)(2,1)S(1)} %collective-permute-done.13.refs_9_), channel_id=1, source_target_pairs={{0,1},{1,0},{2,3},{3,2},{4,5},{5,4},{6,7},{7,6},{8,9},{9,8},{10,11... | collective-permute-start | bytes 663560 | tf_op jit(solution)/shard_map/ppermute | solution.py:389
  52.8 5.6 %collective-permute-start.18 = (bf16[864,128]{1,0:T(8,128)(2,1)S(1)}, bf16[864,128]{1,0:T(8,128)(2,1)}, u32[]{:S(2)}, u32[]{:S(2)}) collective-permute-start(bf16[864,128]{1,0:T(8,128)(2,1)S(1)} %collective-permute-done.14.refs_13_), channel_id=1, source_target_pairs={{0,1},{1,0},{2,3},{3,2},{4,5},{5,4},{6,7},{7,6},{8,9},{9,8},{10,11... | collective-permute-start | bytes 663560 | tf_op jit(solution)/shard_map/ppermute | solution.py:389
  53.2 12.8 %all-to-all-start.1 = ((bf16[8,64,128]{2,1,0:T(8,128)(2,1)}), bf16[8,64,128]{2,1,0:T(8,128)(2,1)S(1)}, u32[]{:S(2)}, u32[]{:S(2)}) async-start(bf16[8,64,128]{2,1,0:T(8,128)(2,1)} %copy-done.6), calls=%async_computation.1 | async-start | bytes 262144 | tf_op jit(solution)/shard_map/all_to_all | solution.py:519
  65.4 0.7 copy-start.4
  66.1 1.5 %collective-permute-start.19 = (f32[64,256]{1,0:T(8,128)}, f32[64,256]{1,0:T(8,128)S(1)}, u32[]{:S(2)}, u32[]{:S(2)}) collective-permute-start(f32[64,256]{1,0:T(8,128)} %get-tuple-element.70), channel_id=1, source_target_pairs={{0,1},{1,0},{2,3},{3,2},{4,5},{5,4},{6,7},{7,6},{8,9},{9,8},{10,11... | collective-permute-start | bytes 196616 | tf_op jit(solution)/shard_map/ppermute | solution.py:389
  67.5 0.8 copy-start.14
  69.7 15.2 %all-to-all-start.2 = ((f32[8,64,128]{2,1,0:T(8,128)}), f32[8,64,128]{2,1,0:T(8,128)S(1)}, u32[]{:S(2)}, u32[]{:S(2)}) async-start(f32[8,64,128]{2,1,0:T(8,128)} %get-tuple-element.74), calls=%async_computation.2 | async-start | bytes 524288 | tf_op jit(solution)/shard_map/all_to_all | solution.py:536
  75.7 1.4 %collective-permute-start.21 = (f32[72,256]{1,0:T(8,128)S(1)}, f32[72,256]{1,0:T(8,128)S(1)}, u32[]{:S(2)}, u32[]{:S(2)}) collective-permute-start(f32[72,256]{1,0:T(8,128)S(1)} %get-tuple-element.78), channel_id=1, source_target_pairs={{0,1},{1,0},{2,3},{3,2},{4,5},{5,4},{6,7},{7,6},{8,9},{9,8},{10,11... | collective-permute-start | bytes 221192 | tf_op jit(solution)/shard_map/ppermute | solution.py:389
  75.7 1.4 %collective-permute-start.20 = (f32[2,64,128]{2,1,0:T(8,128)S(1)}, f32[2,64,128]{2,1,0:T(8,128)S(1)}, u32[]{:S(2)}, u32[]{:S(2)}) collective-permute-start(f32[2,64,128]{2,1,0:T(8,128)S(1)} %get-tuple-element.82.state_m.state), channel_id=1, source_target_pairs={{0,1},{1,0},{2,3},{3,2},{4,5},{5,4},{6,7},{7,6},{8,9},{9,8},{10,11... | collective-permute-start | bytes 196616 | tf_op jit(solution)/shard_map/ppermute | solution.py:389
  95.7 2.2 %collective-permute-start.23 = (bf16[8,64,128]{2,1,0:T(8,128)(2,1)S(1)}, bf16[8,64,128]{2,1,0:T(8,128)(2,1)S(1)}, u32[]{:S(2)}, u32[]{:S(2)}) collective-permute-start(bf16[8,64,128]{2,1,0:T(8,128)(2,1)S(1)} %all_to_all.20.bars_m), channel_id=1, source_target_pairs={{0,1},{1,0},{2,3},{3,2},{4,5},{5,4},{6,7},{7,6},{8,9},{9,8},{10,11... | collective-permute-start | bytes 393224 | tf_op jit(solution)/shard_map/ppermute | solution.py:389
  95.7 1.4 %collective-permute-start.22 = (f32[64,128]{1,0:T(8,128)S(1)}, f32[64,128]{1,0:T(8,128)S(1)}, u32[]{:S(2)}, u32[]{:S(2)}) collective-permute-start(f32[64,128]{1,0:T(8,128)S(1)} %get-tuple-element.83.gen_m), channel_id=1, source_target_pairs={{0,1},{1,0},{2,3},{3,2},{4,5},{5,4},{6,7},{7,6},{8,9},{9,8},{10,11... | collective-permute-start | bytes 98312 | tf_op jit(solution)/shard_map/ppermute | solution.py:389
  97.9 0.9 copy-start.5

commit v5 on v4

--- a/solution.py
+++ b/solution.py
@@ -81,7 +81,7 @@
     return jnp.concatenate(rows, axis=1)
 
 
-def ahead_kernel(par, gen_row, cost_row, limit, gen, commit, startup, cap, start, window,
+def ahead_kernel(par, gen_row, cost_row, limit, balance, gen, commit, startup, cap, start, window,
                  pack, startup2, hold):
     gen_max, cost_commit, cost_start, init = (par[:, i:i + 1] for i in range(4))
     spans = jnp.broadcast_to(par[:, 4:5].astype(jnp.int32), commit.shape)
@@ -108,6 +108,9 @@
     table = [pltpu.roll(jnp.concatenate([row[...], blank], axis=1), core * units, 1)
              for row in (gen_row, cost_row)]
     table += [limit[:, i:i + wide] for i in range(0, limit.shape[1], wide)]
+    own = balance.shape[1]
+    row = jnp.concatenate([balance[...], jnp.zeros((1, wide - own), F32)], axis=1)
+    table.append(pltpu.roll(row, (2 * lax.axis_index("chip") + core) * own, 1))
     table += [jnp.zeros((1, wide), F32)] * (8 - len(table))
     pack[3 * units:] = jnp.concatenate(table, axis=0)
     startup2[...] = s2
@@ -149,18 +152,19 @@
         part[i] = total[:, i * wide:(i + 1) * wide]
 
 
-def adjoint_kernel(cols_m, cols_o, dual_m, dual_o, balance_m, balance_o, part, dual_t, balance):
+def balance_column(mine, other, periods):
     core, chip = lax.axis_index("core"), lax.axis_index("chip")
-    periods = dual_m.shape[1]
+    own = mine.shape[1]
+    rest = jnp.zeros((1, periods - 2 * own), F32)
+    row = jnp.concatenate([by_core(mine[...], other[...], core), rest], axis=1)
+    return half_of(to_column(pltpu.roll(row, 2 * chip * own, 1)), core)
+
+
+def adjoint_kernel(cols_m, cols_o, dual_m, dual_o, balance_m, balance_o, part, dual_t):
+    core = lax.axis_index("core")
     dual = jnp.concatenate([half_of(dual_m[...].T, core), half_of(dual_o[...].T, core)], axis=1)
     dual_t[...] = dual
-    own = balance_m.shape[1]
-    mine, other = balance_m[...], balance_o[...]
-    rest = jnp.zeros((1, periods - 2 * own), F32)
-    row = jnp.concatenate([by_core(mine, other, core), rest], axis=1)
-    row = pltpu.roll(row, 2 * chip * own, 1)
-    column = half_of(to_column(row), core)
-    balance[...] = column
+    column = balance_column(balance_m, balance_o, dual_m.shape[1])
     put_parts(part, dual, cols_m, cols_o, column)
 
 
@@ -207,12 +211,13 @@
     return by_core(here, there, core)
 
 
-def late_kernel(par, state_m, state_o, keep, other, hold,
-                gen1, cap1, bar_commit, dual, balance, commit_out, start_out, window_out):
+def late_kernel(par, state_m, state_o, keep, other, hold, flow_m, flow_s,
+                flow, gen1, cap1, bar_commit, dual, balance, commit_out, start_out, window_out):
     core = lax.axis_index("core")
     gen_max, init = par[:, 0:1], par[:, 3:4]
     cap = own_units(state_m[1], state_o[1], core)
     gen1[...] = own_units(state_m[0], state_o[0], core)
+    flow[...] = by_core(flow_m[...].T, flow_s[...].T, core)
     half = dual.shape[1] // 2
     dual[...] = by_core(keep[0:half].T, other[0:half].T, core)
     own = balance.shape[1]
@@ -266,19 +271,20 @@
 
 
 def slab_kernel(ptdf, *refs):
-    pieces, (keep, send, demand, total, slab, buffers, sems) = refs[:-7], refs[-7:]
+    pieces, (keep, send, demand, slab, buffers, sems) = refs[:-6], refs[-6:]
+    count = buffers.shape[0]
     core, chip = lax.axis_index("core"), lax.axis_index("chip")
     side, here = chip % 2, chip // 2
     depth = slab.shape[0]
     copies = []
-    for i in range(len(pieces) // 4):
+    for i in range(count):
         start = pl.multiple_of(jnp.bitwise_xor(here, i) * depth, depth)
         copies.append(
             pltpu.make_async_copy(ptdf.at[:, pl.ds(start, depth)], buffers.at[i], sems.at[i])
         )
         copies[i].start()
     flow, rows = 0.0, 0.0
-    for i in range(len(pieces) // 4):
+    for i in range(count):
         near, across, swapped, far = (ref[...] for ref in pieces[4 * i:4 * i + 4])
         bus_dev, periods = near.shape
         for yy in range(2):
@@ -293,7 +299,6 @@
                 rows += jnp.sum(chosen.astype(F32).reshape(-1, 8, periods), axis=0)
         copies[i].wait()
         flow += jnp.dot(buffers[i], slab[...], preferred_element_type=F32)
-    total[...] = flow
     turned = flow.T
     keep[...] = half_of(turned, core)
     send[...] = half_of(turned, 1 - core)
@@ -314,7 +319,7 @@
 
 
 def line1_kernel(bars, cols_m, cols_o, flow_m, flow_o, dual, pack_m, pack_o, demand,
-                 balance, part, keep, send, held):
+                 part, keep, send, held):
     core, chip = lax.axis_index("core"), lax.axis_index("chip")
     lines, units = cols_m.shape
     wide = bars.shape[2]
@@ -326,7 +331,9 @@
     flows = jnp.concatenate([mine, other], axis=1)
     new = line_step(flows, dual[...], packed_limits(pack_m, pack_o, lines))
     wanted = half_of(to_column(jnp.sum(demand[...], axis=0, keepdims=True)), core)
-    moved = balance[...] + balance_change(bar, wanted, units)
+    row = packed_row(pack_m, pack_o, 2 + lines // demand.shape[1])
+    balance = half_of(to_column(row), core)
+    moved = balance + balance_change(bar, wanted, units)
     periods = moved.shape[0]
     own = 2 * periods // part.shape[0]
     rows = lax.broadcasted_iota(jnp.int32, moved.shape, 0) + core * periods
@@ -364,6 +371,10 @@
     return pl.CostEstimate(flops=flops, bytes_accessed=moved, transcendentals=0)
 
 
+def near_core(values):
+    return pltpu.with_memory_space_constraint(values, pltpu.VMEM)
+
+
 def room(mib):
     return pltpu.CompilerParams(vmem_limit_bytes=mib << 20)
 
@@ -401,7 +412,6 @@
             jax.ShapeDtypeStruct((half, lines), F32),
             jax.ShapeDtypeStruct((half, lines), F32),
             jax.ShapeDtypeStruct((8, periods), F32),
-            jax.ShapeDtypeStruct((lines, periods), F32),
         ],
         in_specs=[
             pl.BlockSpec((lines, depth), lambda k: (0, k)),
@@ -411,27 +421,29 @@
             pl.BlockSpec((half, lines), lambda k: (0, 0)),
             pl.BlockSpec((half, lines), lambda k: (0, 0)),
             pl.BlockSpec((8, periods), lambda k: (0, 0)),
-            pl.BlockSpec((lines, periods), lambda k: (0, 0)),
         ],
+        scratch_shapes=[pltpu.VMEM((lines, periods), F32)],
         cost_estimate=work(2 * periods * lines * buses, ptdf.size * 2 + every_load.size * 2),
     )(ptdf, every_load)
 
 
 def slab_product(ptdf, pieces):
-    lines, buses = ptdf.shape
+    lines = ptdf.shape[0]
     bus_dev, periods = pieces[0].shape
-    shapes = [((periods // 2, lines), F32)] * 2 + [((8, periods), F32), ((lines, periods), F32)]
+    count, depth = len(pieces) // 4, 4 * bus_dev
+    shapes = [(periods // 2, lines)] * 2 + [(8, periods)]
+    moved = count * depth * (lines + periods) * 2
     return pl.pallas_call(
         slab_kernel,
-        out_shape=[jax.ShapeDtypeStruct(*shape) for shape in shapes],
+        out_shape=[jax.ShapeDtypeStruct(shape, F32) for shape in shapes],
         in_specs=[HBM] + [VMEM] * len(pieces),
         out_specs=[VMEM] * len(shapes),
         scratch_shapes=[
-            pltpu.VMEM((4 * bus_dev, periods), BF16),
-            pltpu.VMEM((len(pieces) // 4, lines, 4 * bus_dev), BF16),
-            pltpu.SemaphoreType.DMA((len(pieces) // 4,)),
+            pltpu.VMEM((depth, periods), BF16),
+            pltpu.VMEM((count, lines, depth), BF16),
+            pltpu.SemaphoreType.DMA((count,)),
         ],
-        cost_estimate=work(2 * lines * periods * buses, buses * (lines + periods) * 2),
+        cost_estimate=work(2 * lines * periods * count * depth, moved),
         compiler_params=room(16),
     )(ptdf, *pieces)
 
@@ -469,15 +481,15 @@
     by_slab = chips == 8 and 4 * load.shape[0] % 128 == 0
     after = lax.optimization_barrier
 
-    def along(turn):
+    def along(turn, piece):
         pairs = [(i, i ^ 2 * turn) for i in range(chips)]
-        return lax.ppermute(load, "chip", pairs)
+        return lax.ppermute(piece, "chip", pairs)
 
     def cross(piece):
         return lax.ppermute(piece, "chip", across)
 
     if by_slab:
-        near = [load, along(1), along(2), along(3)]
+        near = [load, along(1, load), along(2, load)]
         far = [cross(load)]
     else:
         every_load = lax.all_gather(load, LINE, axis=0, tiled=True)
@@ -486,51 +498,56 @@
 
     cols_m = unit_columns(ptdf, unit_bus)
     if by_slab:
-        near[1] = after((near[1], cols_m))[0]
+        late_load, near[1], near[2] = after((load, near[1], near[2], cols_m))[:3]
+        near.append(along(3, late_load))
         far.append(cross(near[1]))
+        far.append(cross(near[2]))
     cols_o = swap(cols_m)
 
     blocks = (chips, half, unit_chip)
-    parts, dual0, balance0 = call(
-        adjoint_kernel, [(blocks, F32), ((half, 2 * lines), F32), ((half, 1), F32)],
+    parts, dual0 = call(
+        adjoint_kernel, [(blocks, F32), ((half, 2 * lines), F32)],
         cols_m, cols_o, line_dual, dual_o, balance_dual[None], balance_o[None],
     )
     commit, startup, gen_max, min_up, parts = after((commit, startup, gen_max, min_up, parts))
     sums = lax.all_to_all(parts, "chip", 0, 0)
     if by_slab:
-        near[2:] = after((*near[2:], parts))[:2]
-        far.append(cross(near[2]))
+        near[3] = after((near[3], parts))[0]
         far.append(cross(near[3]))
     par = jnp.stack(
         [gen_max, cost_commit, cost_start, init_commit, min_up.astype(F32)], axis=1
     )
     square = (unit_dev, periods)
+    states = [
+        pltpu.with_memory_space_constraint(state, pltpu.HBM)
+        for state in (gen, commit, startup, cap_dual, start_dual, window_dual)
+    ]
     pack_m, startup2, hold = call(
         ahead_kernel,
         [((3 * unit_dev + 8, periods), F32), (square, F32), ((4, *square), F32)], par,
-        gen_max[None], cost_gen[None], line_limit[None], gen, commit, startup, cap_dual, start_dual, window_dual,
+        gen_max[None], cost_gen[None], line_limit[None], balance_dual[None], *states,
     )
     pack_o = swap(pack_m)
     spread, state_m = call(
-        gen1_kernel, [(blocks, BF16), ((2, half, unit_chip), F32)],
-        sums, pack_m, pack_o,
+        gen1_kernel, [(blocks, BF16), ((2, half, unit_chip), F32)], sums, pack_m, pack_o,
     )
 
     bars = lax.all_to_all(spread, "chip", 0, 0)
     if by_slab:
-        far[2:] = after((*far[2:], spread))[:2]
+        far[3] = after((far[3], spread))[0]
         near_o = [swap(piece) for piece in near]
-        far_o = [swap(piece) for piece in far[:2]]
-        far_o += [swap(piece) for piece in far[2:]]
+        far_o = [swap(piece) for piece in far[:3]]
+        far_o.append(swap(far[3]))
+        near_o, far_o = ([near_core(piece) for piece in some] for some in (near_o, far_o))
         pieces = [list(four) for four in zip(near, far, near_o, far_o)]
-        flow_m, send, demand, flow = slab_product(ptdf, sum(pieces, []))
+        flow_m, flow_s, demand = slab_product(ptdf, sum(pieces, []))
     else:
-        flow_m, send, demand, flow = gathered_product(ptdf, every_load)
-    flow_o = swap(send)
+        flow_m, flow_s, demand = gathered_product(ptdf, every_load)
+    flow_o = swap(flow_s)
 
     parts, keep, send = call(
         line1_kernel, [(blocks, F32)] + [((half + 8, lines), F32)] * 2,
-        bars, cols_m, cols_o, flow_m, flow_o, dual0, pack_m, pack_o, demand, balance0,
+        bars, cols_m, cols_o, flow_m, flow_o, near_core(dual0), pack_m, pack_o, demand,
         scratch=[pltpu.VMEM((half, units), BF16)],
     )
     sums = lax.all_to_all(parts, "chip", 0, 0)
@@ -538,10 +555,11 @@
     limit = line_limit[:, None]
     small = ((1, balance_dual.shape[0]), F32)
     state_o, dual_o = swap(state), swap(send)
-    gen1, cap1, bar_commit2, dual1, balance1, commit2, start2, window2 = call(
+    flow, gen1, cap1, bar_commit2, dual1, balance1, commit2, start2, window2 = call(
         late_kernel,
-        [(square, F32)] * 3 + [((lines, periods), F32), small] + [(square, F32)] * 3,
-        par, state, state_o, keep, dual_o, hold,
+        [((lines, periods), F32)] + [(square, F32)] * 3 + [((lines, periods), F32), small]
+        + [(square, F32)] * 3,
+        par, state, state_o, keep, dual_o, hold, flow_m, flow_s,
     )
     state_m, bar_commit2, limit = after((state_m, bar_commit2, limit))
     spread, gen2_m = call(
@@ -555,7 +573,7 @@
     dual1, cap2 = after((dual1, cap2))
     dual2, balance2 = call(
         line2_kernel, [((lines, periods), F32), small],
-        bars, swap(bars), cols_m, flow, dual1, limit, demand, balance1,
+        bars, swap(bars), cols_m, near_core(flow), dual1, limit, demand, balance1,
         scratch=[pltpu.VMEM((periods, units), BF16)],
     )
     return (gen2, commit2, startup2, dual2, balance2[0], cap2, start2, window2)

time: 101 us -> 103 us (1.020)
  local copies, waits for them, and re-layouts: 5.87 us -> 3.06 us
  waiting for transfers between devices: 26.4 us -> 29.2 us
  Pallas kernels: 25 us -> 26.7 us
    all_to_all x2, waiting for transfers between devices: 10.5 us -> 5.84 us  [on_device(): sums = lax.all_to_all(parts, 'chip', 0, 0)]
    ppermute x4, waiting for transfers between devices: 6.29 us -> 10.7 us  [cross(): return lax.ppermute(piece, 'chip', across)]
    ppermute x3, waiting for transfers between devices: 6.02 us -> 9.47 us  [along(): return lax.ppermute(piece, 'chip', pairs)]
    unnamed x50 -> x30, local copies, waits for them, and re-layouts: 4.84 us -> 2.03 us
    pallas_call x8, Pallas kernels: 7.49 us -> 9.22 us  [call(): pl.pallas_call(kernel, out_shape=shapes, in_specs=[VMEM] * len(args), out...]
  transfers between devices with their start and end apart: 27 -> 27, of which waited for: 9 -> 11; matrix products, arithmetic and copies ran while one was open for 1% -> 1% of each run, Pallas kernels for 12% -> 13%
where the time goes in v5:
time: 103 us; the launch traced here: 102 us
  starting transfers between devices  31.5 us (31%)
  waiting for transfers between devices  29.2 us (28%)
  Pallas kernels  26.7 us (26%)
  blocking collectives  10.7 us (10%)
  local copies, waits for them, and re-layouts  3.06 us (3%)
    ppermute x4, waiting for transfers between devices, cross(): return lax.ppermute(piece, 'chip', across)  10.7 us
    all_to_all x1, blocking collectives, on_device(): bars = lax.all_to_all(spread, 'chip', 0, 0)  10.7 us
    pallas_call x1, Pallas kernels, unit_columns(): pl.pallas_call(columns_kernel, grid=(buses // depth,), out_shape=jax.Shap...  10.5 us
    ppermute x3, waiting for transfers between devices, along(): return lax.ppermute(piece, 'chip', pairs)  9.47 us
    all_to_all x2, starting transfers between devices, on_device(): sums = lax.all_to_all(parts, 'chip', 0, 0)  9.4 us
    pallas_call x8, Pallas kernels, call(): pl.pallas_call(kernel, out_shape=shapes, in_specs=[VMEM] * len(args), out...  9.22 us
    ppermute x3, starting transfers between devices, along(): return lax.ppermute(piece, 'chip', pairs)  8.48 us
    pallas_call x1, Pallas kernels, slab_product(): pl.pallas_call(slab_kernel, out_shape=[jax.ShapeDtypeStruct(shape, F32) f...  7 us
  transfers between devices with their start and end apart: 27, of which 11 were waited for; matrix products, arithmetic and copies ran while one was open for 1% of the time, Pallas kernels for 13%

profile of v5, /device:TPU:0, one launch (start us, length us, event | category | flops | bytes accessed | tf_op | source)
XLA Modules:
  0.0 102.2 jit_solution(3169647591980337381)
XLA Ops:
  0.6 0.7 copy-done.9
  1.4 10.5 %shard_map.233.cols_m.cols = bf16[256,1024]{1,0:T(8,128)(2,1)S(1)} custom-call(s32[1,1024]{1,0:T(1,128)S(1)} %bitcast.22, bf16[256,13824]{1,0:T(8,128)(2,1)} %ptdf.3), custom_call_target="tpu_custom_call" | custom-call | flops 7247757312 | bytes 7077888 | tf_op jit(solution)/shard_map/pallas_call | solution.py:455
  11.9 0.6 collective-permute-start
  12.5 3.7 %collective-permute-start.8 = (bf16[864,128]{1,0:T(8,128)(2,1)S(1)}, bf16[864,128]{1,0:T(8,128)(2,1)S(1)}, u32[]{:S(2)}, u32[]{:S(2)}) collective-permute-start(bf16[864,128]{1,0:T(8,128)(2,1)S(1)} %copy-done), channel_id=1, source_target_pairs={{0,8},{2,10},{4,12},{6,14},{8,0},{10,2},{12,4},{14,6},{1,9},{3,11}... | collective-permute-start | bytes 663560 | tf_op jit(solution)/shard_map/ppermute | solution.py:486
  16.1 1.6 %collective-permute-start.7 = (bf16[864,128]{1,0:T(8,128)(2,1)S(1)}, bf16[864,128]{1,0:T(8,128)(2,1)S(1)}, u32[]{:S(2)}, u32[]{:S(2)}) collective-permute-start(bf16[864,128]{1,0:T(8,128)(2,1)S(1)} %copy-done), channel_id=1, source_target_pairs={{0,4},{2,6},{4,0},{6,2},{8,12},{10,14},{12,8},{14,10},{1,5},{3,7},... | collective-permute-start | bytes 663560 | tf_op jit(solution)/shard_map/ppermute | solution.py:486
  17.7 9.3 %collective-permute-done.8.refs_8_ = bf16[864,128]{1,0:T(8,128)(2,1)S(1)} collective-permute-done((bf16[864,128]{1,0:T(8,128)(2,1)S(1)}, bf16[864,128]{1,0:T(8,128)(2,1)S(1)}, u32[]{:S(2)}, u32[]{:S(2)}) %collective-permute-start.8) | collective-permute-done | bytes 221216 | tf_op jit(solution)/shard_map/ppermute | solution.py:486
  27.0 0.2 collective-permute-done.7.refs_4_
  27.2 3.2 %collective-permute-start.15 = (bf16[864,128]{1,0:T(8,128)(2,1)S(1)}, bf16[864,128]{1,0:T(8,128)(2,1)S(1)}, u32[]{:S(2)}, u32[]{:S(2)}) collective-permute-start(bf16[864,128]{1,0:T(8,128)(2,1)S(1)} %copy-done), channel_id=1, source_target_pairs={{0,12},{2,14},{4,8},{6,10},{8,4},{10,6},{12,0},{14,2},{1,13},{3,15... | collective-permute-start | bytes 663560 | tf_op jit(solution)/shard_map/ppermute | solution.py:486
  30.4 0.0 collective-permute-start.1
  30.5 1.5 %collective-permute-start.4 = (bf16[864,128]{1,0:T(8,128)(2,1)S(1)}, bf16[864,128]{1,0:T(8,128)(2,1)S(1)}, u32[]{:S(2)}, u32[]{:S(2)}) collective-permute-start(bf16[864,128]{1,0:T(8,128)(2,1)S(1)} %copy-done), channel_id=1, source_target_pairs={{0,2},{2,0},{4,6},{6,4},{8,10},{10,8},{12,14},{14,12},{1,3},{3,1},... | collective-permute-start | bytes 663560 | tf_op jit(solution)/shard_map/ppermute | solution.py:489
  32.0 0.2 collective-permute-start.2
  32.2 0.9 collective-permute-done.2
  33.1 0.0 collective-permute-done.1.dual_o
  33.1 0.0 collective-permute-done.cols_o
  33.1 1.1 %shard_map.234 = (f32[8,64,128]{2,1,0:T(8,128)}, f32[64,512]{1,0:T(8,128)S(1)}) custom-call(bf16[256,1024]{1,0:T(8,128)(2,1)S(1)} %shard_map.233.cols_m.cols, bf16[256,1024]{1,0:T(8,128)(2,1)S(1)} %collective-permute-done.cols_o, f32[256,128]{1,0:T(8,128)S(1)} %copy-done.1, f32[256,128]{1,0:T(8,128)S(1)} %collective-permute-done.1.dual_o, ...), custom_call_target="tpu_custom_call" | custom-call | tf_op jit(solution)/shard_map/pallas_call | solution.py:384
  34.2 3.4 %all-to-all-start = ((f32[8,64,128]{2,1,0:T(8,128)}), f32[8,64,128]{2,1,0:T(8,128)S(1)}, u32[]{:S(2)}, u32[]{:S(2)}) async-start(f32[8,64,128]{2,1,0:T(8,128)} %get-tuple-element.55), calls=%async_computation | async-start | bytes 524288 | tf_op jit(solution)/shard_map/all_to_all | solution.py:513
  37.6 0.0 collective-permute-done.15.refs_12_
  37.7 1.9 %collective-permute-start.16 = (bf16[864,128]{1,0:T(8,128)(2,1)S(1)}, bf16[864,128]{1,0:T(8,128)(2,1)S(1)}, u32[]{:S(2)}, u32[]{:S(2)}) collective-permute-start(bf16[864,128]{1,0:T(8,128)(2,1)S(1)} %collective-permute-done.15.refs_12_), channel_id=1, source_target_pairs={{0,2},{2,0},{4,6},{6,4},{8,10},{10,8},{12,14},{14,12},{1,3},{3,1},... | collective-permute-start | bytes 663560 | tf_op jit(solution)/shard_map/ppermute | solution.py:489
  39.6 0.1 copy.37.par
  39.7 2.6 %shard_map.235 = (f32[200,128]{1,0:T(8,128)S(1)}, f32[64,128]{1,0:T(8,128)}, f32[4,64,128]{2,1,0:T(8,128)S(1)}) custom-call(f32[64,5]{1,0:T(8,128)S(1)} %copy.37.par, f32[1,64]{1,0:T(1,128)S(1)} %bitcast.19, f32[1,64]{1,0:T(1,128)S(1)} %bitcast.20, f32[1,256]{1,0:T(1,128)S(1)} %bitcast.14, f32[1,8]{1,0:T(1,128)S(1)} %bitcast.17, f32[64,128]{1,0:T(8,128)} %gen.1, ...), custom_call_target="tpu_custom_call" | custom-call | tf_op jit(solution)/shard_map/pallas_call | solution.py:384
  42.3 0.7 copy-done.3
  43.0 0.0 collective-permute-start.3
  43.0 0.5 collective-permute-start.5
  43.5 0.2 collective-permute-start.9
  43.7 0.0 collective-permute-done.4.refs_1_
  43.7 1.8 %collective-permute-start.12 = (bf16[864,128]{1,0:T(8,128)(2,1)S(1)}, bf16[864,128]{1,0:T(8,128)(2,1)}, u32[]{:S(2)}, u32[]{:S(2)}) collective-permute-start(bf16[864,128]{1,0:T(8,128)(2,1)S(1)} %collective-permute-done.8.refs_8_), channel_id=1, source_target_pairs={{0,2},{2,0},{4,6},{6,4},{8,10},{10,8},{12,14},{14,12},{1,3},{3,1},... | collective-permute-start | bytes 663560 | tf_op jit(solution)/shard_map/ppermute | solution.py:489
  45.5 3.3 %collective-permute-done.16.refs_13_ = bf16[864,128]{1,0:T(8,128)(2,1)S(1)} collective-permute-done((bf16[864,128]{1,0:T(8,128)(2,1)S(1)}, bf16[864,128]{1,0:T(8,128)(2,1)S(1)}, u32[]{:S(2)}, u32[]{:S(2)}) %collective-permute-start.16) | collective-permute-done | bytes 221216 | tf_op jit(solution)/shard_map/ppermute | solution.py:489
  48.9 0.0 collective-permute-start.10
  48.9 0.0 all-to-all-done.parts
  48.9 0.3 shard_map.236
  49.1 0.0 copy-start.2
  49.1 0.6 copy-done.2
  49.8 0.5 collective-permute-start.13
  50.3 3.3 %collective-permute-done.9.refs_5_ = bf16[864,128]{1,0:T(8,128)(2,1)S(1)} collective-permute-done((bf16[864,128]{1,0:T(8,128)(2,1)S(1)}, bf16[864,128]{1,0:T(8,128)(2,1)S(1)}, u32[]{:S(2)}, u32[]{:S(2)}) %collective-permute-start.9) | collective-permute-done | bytes 221216 | tf_op jit(solution)/shard_map/ppermute | solution.py:489
  53.6 0.0 collective-permute-start.11
  53.6 4.1 %collective-permute-done.12.refs_9_ = bf16[864,128]{1,0:T(8,128)(2,1)} collective-permute-done((bf16[864,128]{1,0:T(8,128)(2,1)S(1)}, bf16[864,128]{1,0:T(8,128)(2,1)}, u32[]{:S(2)}, u32[]{:S(2)}) %collective-permute-start.12) | collective-permute-done | bytes 221216 | tf_op jit(solution)/shard_map/ppermute | solution.py:489
  57.7 0.0 collective-permute-start.14
  57.7 0.0 collective-permute-done.6.refs_3_
  57.7 0.5 collective-permute-start.17
  58.2 0.0 collective-permute-done.10.refs_6_
  58.2 0.1 collective-permute-start.18
  58.3 4.6 %all-to-all-start.1 = ((bf16[8,64,128]{2,1,0:T(8,128)(2,1)}), bf16[8,64,128]{2,1,0:T(8,128)(2,1)S(1)}, u32[]{:S(2)}, u32[]{:S(2)}) async-start(bf16[8,64,128]{2,1,0:T(8,128)(2,1)} %copy-done.2), calls=%async_computation.1 | async-start | bytes 262144 | tf_op jit(solution)/shard_map/all_to_all | solution.py:535
  62.9 0.0 collective-permute-done.13.refs_10_
  62.9 0.0 collective-permute-done.14.refs_11_
  62.9 0.0 collective-permute-done.17.refs_14_
  62.9 7.0 %shard_map.237 = (f32[64,256]{1,0:T(8,128)S(1)}, f32[64,256]{1,0:T(8,128)}, f32[8,128]{1,0:T(8,128)S(1)}) custom-call(bf16[256,13824]{1,0:T(8,128)(2,1)} %ptdf.3, bf16[864,128]{1,0:T(8,128)(2,1)S(1)} %copy-done, bf16[864,128]{1,0:T(8,128)(2,1)S(1)} %collective-permute-done.4.refs_1_, bf16[864,128]{1,0:T(8,128)(2,1)S(1)} %collective-permute-done.5.refs_2_, ...), custom_call_target="tpu_custom_call" | custom-call | flops 905969664 | bytes 10616832 | tf_op jit(solution)/shard_map/pallas_call | solution.py:436
  69.9 0.2 collective-permute-start.19
  70.1 0.3 all-to-all-done.1.bars
  70.5 1.0 collective-permute-done.19.flow_o
  71.4 1.4 %shard_map.238 = (f32[8,64,128]{2,1,0:T(8,128)}, f32[72,256]{1,0:T(8,128)S(1)}, f32[72,256]{1,0:T(8,128)S(1)}) custom-call(bf16[8,64,128]{2,1,0:T(8,128)(2,1)S(1)} %all-to-all-done.1.bars, bf16[256,1024]{1,0:T(8,128)(2,1)S(1)} %shard_map.233.cols_m.cols, bf16[256,1024]{1,0:T(8,128)(2,1)S(1)} %collective-permute-done.cols_o, ...), custom_call_target="tpu_custom_call" | custom-call | tf_op jit(solution)/shard_map/pallas_call | solution.py:384
  72.9 6.0 %all-to-all-start.2 = ((f32[8,64,128]{2,1,0:T(8,128)}), f32[8,64,128]{2,1,0:T(8,128)S(1)}, u32[]{:S(2)}, u32[]{:S(2)}) async-start(f32[8,64,128]{2,1,0:T(8,128)} %get-tuple-element.72), calls=%async_computation.2 | async-start | bytes 524288 | tf_op jit(solution)/shard_map/all_to_all | solution.py:553
  78.9 0.5 collective-permute-start.20
  79.4 0.8 copy.39.par
  80.2 0.1 collective-permute-done.20.state_o
  80.3 2.0 %shard_map.239 = (f32[256,128]{1,0:T(8,128)S(1)}, f32[64,128]{1,0:T(8,128)S(1)}, f32[64,128]{1,0:T(8,128)S(1)}, f32[64,128]{1,0:T(8,128)S(1)}, f32[256,128]{1,0:...) custom-call(f32[64,5]{1,0:T(8,128)S(1)} %copy.39.par, ...), custom_call_target="tpu_custom_call" | custom-call | tf_op jit(solution)/shard_map/pallas_call | solution.py:384
  82.3 5.8 %all-to-all-done.2.parts = f32[8,64,128]{2,1,0:T(8,128)S(1)} async-done(((f32[8,64,128]{2,1,0:T(8,128)}), f32[8,64,128]{2,1,0:T(8,128)S(1)}, u32[]{:S(2)}, u32[]{:S(2)}) %all-to-all-start.2) | async-done | bytes 262176 | tf_op jit(solution)/shard_map/all_to_all | solution.py:553
  88.1 10.7 %all_to_all.20.bars_m = bf16[8,64,128]{2,1,0:T(8,128)(2,1)S(1)} all-to-all(bf16[8,64,128]{2,1,0:T(8,128)(2,1)S(1)} %get-tuple-element.88), channel_id=1, replica_groups=mesh['grp'=2,'chip'=8,'core'=2] {'chip'}, dimensions={0} | all-to-all | bytes 262144 | tf_op jit(solution)/shard_map/all_to_all | solution.py:568
  98.9 0.0 collective-permute-start.23
  98.9 0.5 collective-permute-start.22
  99.4 0.1 copy.40.limit
  99.5 0.7 collective-permute-done.22.gen_o
  100.3 0.8 shard_map.241
  101.1 0.0 collective-permute-done.23.bars_o
  101.1 1.1 %shard_map.242 = (f32[256,128]{1,0:T(8,128)}, f32[1,8]{1,0:T(1,128)}) custom-call(bf16[8,64,128]{2,1,0:T(8,128)(2,1)S(1)} %all_to_all.20.bars_m, bf16[8,64,128]{2,1,0:T(8,128)(2,1)S(1)} %collective-permute-done.23.bars_o, bf16[256,1024]{1,0:T(8,128)(2,1)S(1)} %shard_map.233.cols_m.cols, f32[256,128]{1,0:T(8,128)S(1)} %get-tuple-element.89.flow, ...), custom_call_target="tpu_custom_call" | custom-call | tf_op jit(solution)/shard_map/pallas_call | solution.py:384
  (36 shorter events, 0.1 us)
Async XLA Ops:
  0.6 0.7 copy-start.9
  1.3 11.2 %copy-start = (bf16[864,128]{1,0:T(8,128)(2,1)S(1)}, bf16[864,128]{1,0:T(8,128)(2,1)}, u32[]{:S(2)}) copy-start(bf16[864,128]{1,0:T(8,128)(2,1)} %refs_0_.1) | copy-start | bytes 663556
  1.3 29.1 %copy-start.1 = (f32[256,128]{1,0:T(8,128)S(1)}, f32[256,128]{1,0:T(8,128)}, u32[]{:S(2)}) copy-start(f32[256,128]{1,0:T(8,128)} %dual_m.1) | copy-start | bytes 393220
  1.3 30.6 %copy-start.6 = (f32[8]{0:T(128)S(1)}, f32[8]{0:T(128)}, u32[]{:S(2)}) copy-start(f32[8]{0:T(128)} %param.32) | copy-start | bytes 100
  1.3 38.2 %copy-start.14 = (s32[64]{0:T(128)S(1)}, s32[64]{0:T(128)}, u32[]{:S(2)}) copy-start(s32[64]{0:T(128)} %param.21) | copy-start | bytes 772
  1.3 38.2 %copy-start.7 = (f32[64]{0:T(128)S(1)}, f32[64]{0:T(128)}, u32[]{:S(2)}) copy-start(f32[64]{0:T(128)} %param.22) | copy-start | bytes 772
  1.3 38.2 %copy-start.11 = (f32[64]{0:T(128)S(1)}, f32[64]{0:T(128)}, u32[]{:S(2)}) copy-start(f32[64]{0:T(128)} %param.24) | copy-start | bytes 772
  1.4 38.2 %copy-start.12 = (f32[64]{0:T(128)S(1)}, f32[64]{0:T(128)}, u32[]{:S(2)}) copy-start(f32[64]{0:T(128)} %param.25) | copy-start | bytes 772
  1.4 38.2 %copy-start.13 = (f32[64]{0:T(128)S(1)}, f32[64]{0:T(128)}, u32[]{:S(2)}) copy-start(f32[64]{0:T(128)} %param.26) | copy-start | bytes 772
  1.4 38.4 %copy-start.5 = (f32[256]{0:T(256)S(1)}, f32[256]{0:T(256)}, u32[]{:S(2)}) copy-start(f32[256]{0:T(256)} %param.27) | copy-start | bytes 3076
  1.4 38.3 %copy-start.8 = (f32[64]{0:T(128)S(1)}, f32[64]{0:T(128)}, u32[]{:S(2)}) copy-start(f32[64]{0:T(128)} %param.23) | copy-start | bytes 772
  11.9 21.2 %collective-permute-start = (bf16[256,1024]{1,0:T(8,128)(2,1)S(1)}, bf16[256,1024]{1,0:T(8,128)(2,1)S(1)}, u32[]{:S(2)}, u32[]{:S(2)}) collective-permute-start(bf16[256,1024]{1,0:T(8,128)(2,1)S(1)} %shard_map.233.cols_m.cols), channel_id=1, source_target_pairs={{0,1},{1,0},{2,3},{3,2},{4,5},{5,4},{6,7},{7,6},{8,9},{9,8},{10,11... | collective-permute-start | bytes 1572872 | tf_op jit(solution)/shard_map/ppermute | solution.py:400
  12.5 14.5 %collective-permute-start.8 = (bf16[864,128]{1,0:T(8,128)(2,1)S(1)}, bf16[864,128]{1,0:T(8,128)(2,1)S(1)}, u32[]{:S(2)}, u32[]{:S(2)}) collective-permute-start(bf16[864,128]{1,0:T(8,128)(2,1)S(1)} %copy-done), channel_id=1, source_target_pairs={{0,8},{2,10},{4,12},{6,14},{8,0},{10,2},{12,4},{14,6},{1,9},{3,11}... | collective-permute-start | bytes 663560 | tf_op jit(solution)/shard_map/ppermute | solution.py:486
  16.1 11.0 %collective-permute-start.7 = (bf16[864,128]{1,0:T(8,128)(2,1)S(1)}, bf16[864,128]{1,0:T(8,128)(2,1)S(1)}, u32[]{:S(2)}, u32[]{:S(2)}) collective-permute-start(bf16[864,128]{1,0:T(8,128)(2,1)S(1)} %copy-done), channel_id=1, source_target_pairs={{0,4},{2,6},{4,0},{6,2},{8,12},{10,14},{12,8},{14,10},{1,5},{3,7},... | collective-permute-start | bytes 663560 | tf_op jit(solution)/shard_map/ppermute | solution.py:486
  27.2 10.4 %collective-permute-start.15 = (bf16[864,128]{1,0:T(8,128)(2,1)S(1)}, bf16[864,128]{1,0:T(8,128)(2,1)S(1)}, u32[]{:S(2)}, u32[]{:S(2)}) collective-permute-start(bf16[864,128]{1,0:T(8,128)(2,1)S(1)} %copy-done), channel_id=1, source_target_pairs={{0,12},{2,14},{4,8},{6,10},{8,4},{10,6},{12,0},{14,2},{1,13},{3,15... | collective-permute-start | bytes 663560 | tf_op jit(solution)/shard_map/ppermute | solution.py:486
  30.4 2.7 %collective-permute-start.1 = (f32[256,128]{1,0:T(8,128)S(1)}, f32[256,128]{1,0:T(8,128)S(1)}, u32[]{:S(2)}, u32[]{:S(2)}) collective-permute-start(f32[256,128]{1,0:T(8,128)S(1)} %copy-done.1), channel_id=1, source_target_pairs={{0,1},{1,0},{2,3},{3,2},{4,5},{5,4},{6,7},{7,6},{8,9},{9,8},{10,11... | collective-permute-start | bytes 393224 | tf_op jit(solution)/shard_map/ppermute | solution.py:400
  30.5 13.2 %collective-permute-start.4 = (bf16[864,128]{1,0:T(8,128)(2,1)S(1)}, bf16[864,128]{1,0:T(8,128)(2,1)S(1)}, u32[]{:S(2)}, u32[]{:S(2)}) collective-permute-start(bf16[864,128]{1,0:T(8,128)(2,1)S(1)} %copy-done), channel_id=1, source_target_pairs={{0,2},{2,0},{4,6},{6,4},{8,10},{10,8},{12,14},{14,12},{1,3},{3,1},... | collective-permute-start | bytes 663560 | tf_op jit(solution)/shard_map/ppermute | solution.py:489
  32.0 1.2 %collective-permute-start.2 = (f32[8]{0:T(128)S(1)}, f32[8]{0:T(128)S(1)}, u32[]{:S(2)}, u32[]{:S(2)}) collective-permute-start(f32[8]{0:T(128)S(1)} %copy-done.6), channel_id=1, source_target_pairs={{0,1},{1,0},{2,3},{3,2},{4,5},{5,4},{6,7},{7,6},{8,9},{9,8},{10,11... | collective-permute-start | bytes 104 | tf_op jit(solution)/shard_map/ppermute | solution.py:400
  34.2 14.6 %all-to-all-start = ((f32[8,64,128]{2,1,0:T(8,128)}), f32[8,64,128]{2,1,0:T(8,128)S(1)}, u32[]{:S(2)}, u32[]{:S(2)}) async-start(f32[8,64,128]{2,1,0:T(8,128)} %get-tuple-element.55), calls=%async_computation | async-start | bytes 524288 | tf_op jit(solution)/shard_map/all_to_all | solution.py:513
  37.7 11.2 %collective-permute-start.16 = (bf16[864,128]{1,0:T(8,128)(2,1)S(1)}, bf16[864,128]{1,0:T(8,128)(2,1)S(1)}, u32[]{:S(2)}, u32[]{:S(2)}) collective-permute-start(bf16[864,128]{1,0:T(8,128)(2,1)S(1)} %collective-permute-done.15.refs_12_), channel_id=1, source_target_pairs={{0,2},{2,0},{4,6},{6,4},{8,10},{10,8},{12,14},{14,12},{1,3},{3,1},... | collective-permute-start | bytes 663560 | tf_op jit(solution)/shard_map/ppermute | solution.py:489
  39.6 9.2 %copy-start.10 = (f32[64,5]{0,1:T(8,128)}, f32[64,5]{0,1:T(8,128)S(1)}, u32[]{:S(2)}) copy-start(f32[64,5]{0,1:T(8,128)S(1)} %stack.23) | copy-start | bytes 3844
  42.3 0.7 copy-start.3
  43.0 2.5 %collective-permute-start.3 = (f32[200,128]{1,0:T(8,128)S(1)}, f32[200,128]{1,0:T(8,128)S(1)}, u32[]{:S(2)}, u32[]{:S(2)}) collective-permute-start(f32[200,128]{1,0:T(8,128)S(1)} %get-tuple-element.60.pack_m), channel_id=1, source_target_pairs={{0,1},{1,0},{2,3},{3,2},{4,5},{5,4},{6,7},{7,6},{8,9},{9,8},{10,11... | collective-permute-start | bytes 307208 | tf_op jit(solution)/shard_map/ppermute | solution.py:400
  43.0 6.8 %collective-permute-start.5 = (bf16[864,128]{1,0:T(8,128)(2,1)S(1)}, bf16[864,128]{1,0:T(8,128)(2,1)S(1)}, u32[]{:S(2)}, u32[]{:S(2)}) collective-permute-start(bf16[864,128]{1,0:T(8,128)(2,1)S(1)} %copy-done), channel_id=1, source_target_pairs={{0,1},{1,0},{2,3},{3,2},{4,5},{5,4},{6,7},{7,6},{8,9},{9,8},{10,11... | collective-permute-start | bytes 663560 | tf_op jit(solution)/shard_map/ppermute | solution.py:400
  43.5 10.1 %collective-permute-start.9 = (bf16[864,128]{1,0:T(8,128)(2,1)S(1)}, bf16[864,128]{1,0:T(8,128)(2,1)S(1)}, u32[]{:S(2)}, u32[]{:S(2)}) collective-permute-start(bf16[864,128]{1,0:T(8,128)(2,1)S(1)} %collective-permute-done.7.refs_4_), channel_id=1, source_target_pairs={{0,2},{2,0},{4,6},{6,4},{8,10},{10,8},{12,14},{14,12},{1,3},{3,1},... | collective-permute-start | bytes 663560 | tf_op jit(solution)/shard_map/ppermute | solution.py:489
  43.7 14.0 %collective-permute-start.12 = (bf16[864,128]{1,0:T(8,128)(2,1)S(1)}, bf16[864,128]{1,0:T(8,128)(2,1)}, u32[]{:S(2)}, u32[]{:S(2)}) collective-permute-start(bf16[864,128]{1,0:T(8,128)(2,1)S(1)} %collective-permute-done.8.refs_8_), channel_id=1, source_target_pairs={{0,2},{2,0},{4,6},{6,4},{8,10},{10,8},{12,14},{14,12},{1,3},{3,1},... | collective-permute-start | bytes 663560 | tf_op jit(solution)/shard_map/ppermute | solution.py:489
  45.5 12.2 %collective-permute-start.6 = (bf16[864,128]{1,0:T(8,128)(2,1)S(1)}, bf16[864,128]{1,0:T(8,128)(2,1)}, u32[]{:S(2)}, u32[]{:S(2)}) collective-permute-start(bf16[864,128]{1,0:T(8,128)(2,1)S(1)} %collective-permute-done.4.refs_1_), channel_id=1, source_target_pairs={{0,1},{1,0},{2,3},{3,2},{4,5},{5,4},{6,7},{7,6},{8,9},{9,8},{10,11... | collective-permute-start | bytes 663560 | tf_op jit(solution)/shard_map/ppermute | solution.py:400
  48.9 9.4 %collective-permute-start.10 = (bf16[864,128]{1,0:T(8,128)(2,1)S(1)}, bf16[864,128]{1,0:T(8,128)(2,1)}, u32[]{:S(2)}, u32[]{:S(2)}) collective-permute-start(bf16[864,128]{1,0:T(8,128)(2,1)S(1)} %collective-permute-done.7.refs_4_), channel_id=1, source_target_pairs={{0,1},{1,0},{2,3},{3,2},{4,5},{5,4},{6,7},{7,6},{8,9},{9,8},{10,11... | collective-permute-start | bytes 663560 | tf_op jit(solution)/shard_map/ppermute | solution.py:400
  49.1 0.7 copy-start.2
  49.8 30.5 %copy-start.4 = (f32[4,64,128]{2,1,0:T(8,128)S(1)}, f32[4,64,128]{2,1,0:T(8,128)}, u32[]{:S(2)}) copy-start(f32[4,64,128]{2,1,0:T(8,128)} %copy-done.3) | copy-start | bytes 393220
  49.8 13.1 %collective-permute-start.13 = (bf16[864,128]{1,0:T(8,128)(2,1)S(1)}, bf16[864,128]{1,0:T(8,128)(2,1)}, u32[]{:S(2)}, u32[]{:S(2)}) collective-permute-start(bf16[864,128]{1,0:T(8,128)(2,1)S(1)} %collective-permute-done.8.refs_8_), channel_id=1, source_target_pairs={{0,1},{1,0},{2,3},{3,2},{4,5},{5,4},{6,7},{7,6},{8,9},{9,8},{10,11... | collective-permute-start | bytes 663560 | tf_op jit(solution)/shard_map/ppermute | solution.py:400
  53.6 9.3 %collective-permute-start.11 = (bf16[864,128]{1,0:T(8,128)(2,1)S(1)}, bf16[864,128]{1,0:T(8,128)(2,1)}, u32[]{:S(2)}, u32[]{:S(2)}) collective-permute-start(bf16[864,128]{1,0:T(8,128)(2,1)S(1)} %collective-permute-done.9.refs_5_), channel_id=1, source_target_pairs={{0,1},{1,0},{2,3},{3,2},{4,5},{5,4},{6,7},{7,6},{8,9},{9,8},{10,11... | collective-permute-start | bytes 663560 | tf_op jit(solution)/shard_map/ppermute | solution.py:400
  57.7 5.2 %collective-permute-start.14 = (bf16[864,128]{1,0:T(8,128)(2,1)}, bf16[864,128]{1,0:T(8,128)(2,1)}, u32[]{:S(2)}, u32[]{:S(2)}) collective-permute-start(bf16[864,128]{1,0:T(8,128)(2,1)} %collective-permute-done.12.refs_9_), channel_id=1, source_target_pairs={{0,1},{1,0},{2,3},{3,2},{4,5},{5,4},{6,7},{7,6},{8,9},{9,8},{10,11... | collective-permute-start | bytes 663560 | tf_op jit(solution)/shard_map/ppermute | solution.py:400
  57.7 5.2 %collective-permute-start.17 = (bf16[864,128]{1,0:T(8,128)(2,1)S(1)}, bf16[864,128]{1,0:T(8,128)(2,1)}, u32[]{:S(2)}, u32[]{:S(2)}) collective-permute-start(bf16[864,128]{1,0:T(8,128)(2,1)S(1)} %collective-permute-done.15.refs_12_), channel_id=1, source_target_pairs={{0,1},{1,0},{2,3},{3,2},{4,5},{5,4},{6,7},{7,6},{8,9},{9,8},{10,11... | collective-permute-start | bytes 663560 | tf_op jit(solution)/shard_map/ppermute | solution.py:400
  58.2 4.7 %collective-permute-start.18 = (bf16[864,128]{1,0:T(8,128)(2,1)S(1)}, bf16[864,128]{1,0:T(8,128)(2,1)}, u32[]{:S(2)}, u32[]{:S(2)}) collective-permute-start(bf16[864,128]{1,0:T(8,128)(2,1)S(1)} %collective-permute-done.16.refs_13_), channel_id=1, source_target_pairs={{0,1},{1,0},{2,3},{3,2},{4,5},{5,4},{6,7},{7,6},{8,9},{9,8},{10,11... | collective-permute-start | bytes 663560 | tf_op jit(solution)/shard_map/ppermute | solution.py:400
  58.3 12.2 %all-to-all-start.1 = ((bf16[8,64,128]{2,1,0:T(8,128)(2,1)}), bf16[8,64,128]{2,1,0:T(8,128)(2,1)S(1)}, u32[]{:S(2)}, u32[]{:S(2)}) async-start(bf16[8,64,128]{2,1,0:T(8,128)(2,1)} %copy-done.2), calls=%async_computation.1 | async-start | bytes 262144 | tf_op jit(solution)/shard_map/all_to_all | solution.py:535
  69.9 1.5 %collective-permute-start.19 = (f32[64,256]{1,0:T(8,128)}, f32[64,256]{1,0:T(8,128)S(1)}, u32[]{:S(2)}, u32[]{:S(2)}) collective-permute-start(f32[64,256]{1,0:T(8,128)} %get-tuple-element.69.flow_s), channel_id=1, source_target_pairs={{0,1},{1,0},{2,3},{3,2},{4,5},{5,4},{6,7},{7,6},{8,9},{9,8},{10,11... | collective-permute-start | bytes 196616 | tf_op jit(solution)/shard_map/ppermute | solution.py:400
  72.9 15.2 %all-to-all-start.2 = ((f32[8,64,128]{2,1,0:T(8,128)}), f32[8,64,128]{2,1,0:T(8,128)S(1)}, u32[]{:S(2)}, u32[]{:S(2)}) async-start(f32[8,64,128]{2,1,0:T(8,128)} %get-tuple-element.72), calls=%async_computation.2 | async-start | bytes 524288 | tf_op jit(solution)/shard_map/all_to_all | solution.py:553
  78.9 1.4 %collective-permute-start.21 = (f32[72,256]{1,0:T(8,128)S(1)}, f32[72,256]{1,0:T(8,128)S(1)}, u32[]{:S(2)}, u32[]{:S(2)}) collective-permute-start(f32[72,256]{1,0:T(8,128)S(1)} %get-tuple-element.76), channel_id=1, source_target_pairs={{0,1},{1,0},{2,3},{3,2},{4,5},{5,4},{6,7},{7,6},{8,9},{9,8},{10,11... | collective-permute-start | bytes 221192 | tf_op jit(solution)/shard_map/ppermute | solution.py:400
  78.9 1.4 %collective-permute-start.20 = (f32[2,64,128]{2,1,0:T(8,128)S(1)}, f32[2,64,128]{2,1,0:T(8,128)S(1)}, u32[]{:S(2)}, u32[]{:S(2)}) collective-permute-start(f32[2,64,128]{2,1,0:T(8,128)S(1)} %get-tuple-element.80.state_m.state), channel_id=1, source_target_pairs={{0,1},{1,0},{2,3},{3,2},{4,5},{5,4},{6,7},{7,6},{8,9},{9,8},{10,11... | collective-permute-start | bytes 196616 | tf_op jit(solution)/shard_map/ppermute | solution.py:400
  98.9 2.2 %collective-permute-start.23 = (bf16[8,64,128]{2,1,0:T(8,128)(2,1)S(1)}, bf16[8,64,128]{2,1,0:T(8,128)(2,1)S(1)}, u32[]{:S(2)}, u32[]{:S(2)}) collective-permute-start(bf16[8,64,128]{2,1,0:T(8,128)(2,1)S(1)} %all_to_all.20.bars_m), channel_id=1, source_target_pairs={{0,1},{1,0},{2,3},{3,2},{4,5},{5,4},{6,7},{7,6},{8,9},{9,8},{10,11... | collective-permute-start | bytes 393224 | tf_op jit(solution)/shard_map/ppermute | solution.py:400
  98.9 1.4 %collective-permute-start.22 = (f32[64,128]{1,0:T(8,128)S(1)}, f32[64,128]{1,0:T(8,128)S(1)}, u32[]{:S(2)}, u32[]{:S(2)}) collective-permute-start(f32[64,128]{1,0:T(8,128)S(1)} %get-tuple-element.81.gen_m), channel_id=1, source_target_pairs={{0,1},{1,0},{2,3},{3,2},{4,5},{5,4},{6,7},{7,6},{8,9},{9,8},{10,11... | collective-permute-start | bytes 98312 | tf_op jit(solution)/shard_map/ppermute | solution.py:400

commit v6 on v5

--- a/solution.py
+++ b/solution.py
@@ -275,7 +275,7 @@
     count = buffers.shape[0]
     core, chip = lax.axis_index("core"), lax.axis_index("chip")
     side, here = chip % 2, chip // 2
-    depth = slab.shape[0]
+    depth = slab.shape[1]
     copies = []
     for i in range(count):
         start = pl.multiple_of(jnp.bitwise_xor(here, i) * depth, depth)
@@ -283,7 +283,7 @@
             pltpu.make_async_copy(ptdf.at[:, pl.ds(start, depth)], buffers.at[i], sems.at[i])
         )
         copies[i].start()
-    flow, rows = 0.0, 0.0
+    rows = 0.0
     for i in range(count):
         near, across, swapped, far = (ref[...] for ref in pieces[4 * i:4 * i + 4])
         bus_dev, periods = near.shape
@@ -295,10 +295,12 @@
                     jnp.where(core == kk, across, far),
                 )
                 at = (2 * yy + kk) * bus_dev
-                slab[at:at + bus_dev] = chosen
+                slab[i, at:at + bus_dev] = chosen
                 rows += jnp.sum(chosen.astype(F32).reshape(-1, 8, periods), axis=0)
+    flow = 0.0
+    for i in range(count):
         copies[i].wait()
-        flow += jnp.dot(buffers[i], slab[...], preferred_element_type=F32)
+        flow += jnp.dot(buffers[i], slab[i], preferred_element_type=F32)
     turned = flow.T
     keep[...] = half_of(turned, core)
     send[...] = half_of(turned, 1 - core)
@@ -380,7 +382,7 @@
 
 
 def call(kernel, outs, *args, scratch=(), cost=None):
-    shapes = [jax.ShapeDtypeStruct(shape, dtype) for shape, dtype in outs]
+    shapes = [pltpu.HBM(shape, dtype) if dtype == BF16 else jax.ShapeDtypeStruct(shape, dtype) for shape, dtype in outs]
     return pl.pallas_call(
         kernel,
         out_shape=shapes,
@@ -439,19 +441,19 @@
         in_specs=[HBM] + [VMEM] * len(pieces),
         out_specs=[VMEM] * len(shapes),
         scratch_shapes=[
-            pltpu.VMEM((depth, periods), BF16),
+            pltpu.VMEM((count, depth, periods), BF16),
             pltpu.VMEM((count, lines, depth), BF16),
             pltpu.SemaphoreType.DMA((count,)),
         ],
         cost_estimate=work(2 * lines * periods * count * depth, moved),
-        compiler_params=room(16),
+        compiler_params=room(20),
     )(ptdf, *pieces)
 
 
 def unit_columns(ptdf, unit_bus):
     lines, buses = ptdf.shape
     units = unit_bus.shape[0]
-    depth = block_depth(buses, 2304)
+    depth = block_depth(buses, 4608)
     return pl.pallas_call(
         columns_kernel,
         grid=(buses // depth,),
@@ -463,8 +465,8 @@
         out_specs=pl.BlockSpec((lines, units), lambda k: (0, 0)),
         scratch_shapes=[pltpu.VMEM((lines, units), F32)],
         cost_estimate=work(2 * units * lines * buses, ptdf.size * 2),
-        compiler_params=room(24),
-    )(unit_bus[None], ptdf)
+        compiler_params=room(36),
+    )(pltpu.with_memory_space_constraint(unit_bus[None], pltpu.HBM), ptdf)
 
 
 def on_device(

time: 103 us -> 101 us (0.981)
  local copies, waits for them, and re-layouts: 3.06 us -> 1.94 us
  transfers between devices with their start and end apart: 27 -> 27, of which waited for: 11 -> 10; matrix products, arithmetic and copies ran while one was open for 1% -> 0% of each run, Pallas kernels for 13% -> 12%
where the time goes in v6:
time: 101 us
  starting transfers between devices  31.3 us (31%)
  waiting for transfers between devices  29.9 us (30%)
  Pallas kernels  25.7 us (25%)
  blocking collectives  10.9 us (11%)
  local copies, waits for them, and re-layouts  1.94 us (2%)
    all_to_all x1, blocking collectives, on_device(): bars = lax.all_to_all(spread, 'chip', 0, 0)  10.9 us
    ppermute x4, waiting for transfers between devices, cross(): return lax.ppermute(piece, 'chip', across)  10.8 us
    pallas_call x1, Pallas kernels, unit_columns(): pl.pallas_call(columns_kernel, grid=(buses // depth,), out_shape=jax.Shap...  10 us
    pallas_call x8, Pallas kernels, call(): pl.pallas_call(kernel, out_shape=shapes, in_specs=[VMEM] * len(args), out...  9.64 us
    ppermute x3, waiting for transfers between devices, along(): return lax.ppermute(piece, 'chip', pairs)  9.48 us
    all_to_all x2, starting transfers between devices, on_device(): sums = lax.all_to_all(parts, 'chip', 0, 0)  9.19 us
    ppermute x3, starting transfers between devices, along(): return lax.ppermute(piece, 'chip', pairs)  8.48 us
    pallas_call x1, Pallas kernels, slab_product(): pl.pallas_call(slab_kernel, out_shape=[jax.ShapeDtypeStruct(shape, F32) f...  6.01 us
  transfers between devices with their start and end apart: 27, of which 10 were waited for; matrix products, arithmetic and copies ran while one was open for 0% of the time, Pallas kernels for 12%

profile of v6, /device:TPU:0, one launch (start us, length us, event | category | flops | bytes accessed | tf_op | source)
XLA Modules:
  0.0 100.6 jit_solution(16494564345614144214)
XLA Ops:
  0.7 10.0 %shard_map.233.cols_m.cols = bf16[256,1024]{1,0:T(8,128)(2,1)S(1)} custom-call(s32[1,1024]{1,0:T(1,128)} %bitcast.25, bf16[256,13824]{1,0:T(8,128)(2,1)} %ptdf.3), custom_call_target="tpu_custom_call" | custom-call | flops 7247757312 | bytes 7077888 | tf_op jit(solution)/shard_map/pallas_call | solution.py:457
  10.8 0.6 collective-permute-start
  11.3 3.7 %collective-permute-start.8 = (bf16[864,128]{1,0:T(8,128)(2,1)S(1)}, bf16[864,128]{1,0:T(8,128)(2,1)S(1)}, u32[]{:S(2)}, u32[]{:S(2)}) collective-permute-start(bf16[864,128]{1,0:T(8,128)(2,1)S(1)} %copy-done), channel_id=1, source_target_pairs={{0,8},{2,10},{4,12},{6,14},{8,0},{10,2},{12,4},{14,6},{1,9},{3,11}... | collective-permute-start | bytes 663560 | tf_op jit(solution)/shard_map/ppermute | solution.py:488
  15.0 1.6 %collective-permute-start.7 = (bf16[864,128]{1,0:T(8,128)(2,1)S(1)}, bf16[864,128]{1,0:T(8,128)(2,1)S(1)}, u32[]{:S(2)}, u32[]{:S(2)}) collective-permute-start(bf16[864,128]{1,0:T(8,128)(2,1)S(1)} %copy-done), channel_id=1, source_target_pairs={{0,4},{2,6},{4,0},{6,2},{8,12},{10,14},{12,8},{14,10},{1,5},{3,7},... | collective-permute-start | bytes 663560 | tf_op jit(solution)/shard_map/ppermute | solution.py:488
  16.6 9.3 %collective-permute-done.8.refs_8_ = bf16[864,128]{1,0:T(8,128)(2,1)S(1)} collective-permute-done((bf16[864,128]{1,0:T(8,128)(2,1)S(1)}, bf16[864,128]{1,0:T(8,128)(2,1)S(1)}, u32[]{:S(2)}, u32[]{:S(2)}) %collective-permute-start.8) | collective-permute-done | bytes 221216 | tf_op jit(solution)/shard_map/ppermute | solution.py:488
  25.9 0.2 collective-permute-done.7.refs_4_
  26.1 3.2 %collective-permute-start.15 = (bf16[864,128]{1,0:T(8,128)(2,1)S(1)}, bf16[864,128]{1,0:T(8,128)(2,1)S(1)}, u32[]{:S(2)}, u32[]{:S(2)}) collective-permute-start(bf16[864,128]{1,0:T(8,128)(2,1)S(1)} %copy-done), channel_id=1, source_target_pairs={{0,12},{2,14},{4,8},{6,10},{8,4},{10,6},{12,0},{14,2},{1,13},{3,15... | collective-permute-start | bytes 663560 | tf_op jit(solution)/shard_map/ppermute | solution.py:488
  29.3 0.0 collective-permute-start.1
  29.3 1.5 %collective-permute-start.4 = (bf16[864,128]{1,0:T(8,128)(2,1)S(1)}, bf16[864,128]{1,0:T(8,128)(2,1)S(1)}, u32[]{:S(2)}, u32[]{:S(2)}) collective-permute-start(bf16[864,128]{1,0:T(8,128)(2,1)S(1)} %copy-done), channel_id=1, source_target_pairs={{0,2},{2,0},{4,6},{6,4},{8,10},{10,8},{12,14},{14,12},{1,3},{3,1},... | collective-permute-start | bytes 663560 | tf_op jit(solution)/shard_map/ppermute | solution.py:491
  30.8 0.2 collective-permute-start.2
  31.1 0.9 collective-permute-done.2
  32.0 0.0 collective-permute-done.1.dual_o
  32.0 0.0 collective-permute-done.cols_o
  32.0 1.1 %shard_map.234 = (f32[8,64,128]{2,1,0:T(8,128)}, f32[64,512]{1,0:T(8,128)S(1)}) custom-call(bf16[256,1024]{1,0:T(8,128)(2,1)S(1)} %shard_map.233.cols_m.cols, bf16[256,1024]{1,0:T(8,128)(2,1)S(1)} %collective-permute-done.cols_o, f32[256,128]{1,0:T(8,128)S(1)} %copy-done.1, f32[256,128]{1,0:T(8,128)S(1)} %collective-permute-done.1.dual_o, ...), custom_call_target="tpu_custom_call" | custom-call | tf_op jit(solution)/shard_map/pallas_call | solution.py:386
  33.1 3.4 %all-to-all-start = ((f32[8,64,128]{2,1,0:T(8,128)}), f32[8,64,128]{2,1,0:T(8,128)S(1)}, u32[]{:S(2)}, u32[]{:S(2)}) async-start(f32[8,64,128]{2,1,0:T(8,128)} %get-tuple-element.55), calls=%async_computation | async-start | bytes 524288 | tf_op jit(solution)/shard_map/all_to_all | solution.py:515
  36.5 0.0 collective-permute-done.15.refs_12_
  36.5 1.9 %collective-permute-start.16 = (bf16[864,128]{1,0:T(8,128)(2,1)S(1)}, bf16[864,128]{1,0:T(8,128)(2,1)S(1)}, u32[]{:S(2)}, u32[]{:S(2)}) collective-permute-start(bf16[864,128]{1,0:T(8,128)(2,1)S(1)} %collective-permute-done.15.refs_12_), channel_id=1, source_target_pairs={{0,2},{2,0},{4,6},{6,4},{8,10},{10,8},{12,14},{14,12},{1,3},{3,1},... | collective-permute-start | bytes 663560 | tf_op jit(solution)/shard_map/ppermute | solution.py:491
  38.5 0.1 copy.37.par
  38.6 2.6 %shard_map.235 = (f32[200,128]{1,0:T(8,128)S(1)}, f32[64,128]{1,0:T(8,128)}, f32[4,64,128]{2,1,0:T(8,128)S(1)}) custom-call(f32[64,5]{1,0:T(8,128)S(1)} %copy.37.par, f32[1,64]{1,0:T(1,128)S(1)} %bitcast.19, f32[1,64]{1,0:T(1,128)S(1)} %bitcast.20, f32[1,256]{1,0:T(1,128)S(1)} %bitcast.14, f32[1,8]{1,0:T(1,128)S(1)} %bitcast.17, f32[64,128]{1,0:T(8,128)} %gen.1, ...), custom_call_target="tpu_custom_call" | custom-call | tf_op jit(solution)/shard_map/pallas_call | solution.py:386
  41.2 0.6 copy-done.2
  41.8 0.0 collective-permute-start.3
  41.8 0.5 collective-permute-start.5
  42.3 0.2 collective-permute-start.9
  42.5 0.0 collective-permute-done.4.refs_1_
  42.5 1.8 %collective-permute-start.12 = (bf16[864,128]{1,0:T(8,128)(2,1)S(1)}, bf16[864,128]{1,0:T(8,128)(2,1)}, u32[]{:S(2)}, u32[]{:S(2)}) collective-permute-start(bf16[864,128]{1,0:T(8,128)(2,1)S(1)} %collective-permute-done.8.refs_8_), channel_id=1, source_target_pairs={{0,2},{2,0},{4,6},{6,4},{8,10},{10,8},{12,14},{14,12},{1,3},{3,1},... | collective-permute-start | bytes 663560 | tf_op jit(solution)/shard_map/ppermute | solution.py:491
  44.4 0.0 collective-permute-start.6
  44.4 3.4 %collective-permute-done.16.refs_13_ = bf16[864,128]{1,0:T(8,128)(2,1)S(1)} collective-permute-done((bf16[864,128]{1,0:T(8,128)(2,1)S(1)}, bf16[864,128]{1,0:T(8,128)(2,1)S(1)}, u32[]{:S(2)}, u32[]{:S(2)}) %collective-permute-start.16) | collective-permute-done | bytes 221216 | tf_op jit(solution)/shard_map/ppermute | solution.py:491
  47.7 0.0 collective-permute-start.10
  47.7 0.0 all-to-all-done.parts
  47.7 0.9 shard_map.236
  48.6 0.0 collective-permute-done.5.refs_2_
  48.6 0.5 collective-permute-start.13
  49.1 3.3 %collective-permute-done.9.refs_5_ = bf16[864,128]{1,0:T(8,128)(2,1)S(1)} collective-permute-done((bf16[864,128]{1,0:T(8,128)(2,1)S(1)}, bf16[864,128]{1,0:T(8,128)(2,1)S(1)}, u32[]{:S(2)}, u32[]{:S(2)}) %collective-permute-start.9) | collective-permute-done | bytes 221216 | tf_op jit(solution)/shard_map/ppermute | solution.py:491
  52.5 0.0 collective-permute-start.11
  52.5 4.1 %collective-permute-done.12.refs_9_ = bf16[864,128]{1,0:T(8,128)(2,1)} collective-permute-done((bf16[864,128]{1,0:T(8,128)(2,1)S(1)}, bf16[864,128]{1,0:T(8,128)(2,1)}, u32[]{:S(2)}, u32[]{:S(2)}) %collective-permute-start.12) | collective-permute-done | bytes 221216 | tf_op jit(solution)/shard_map/ppermute | solution.py:491
  56.6 0.5 collective-permute-start.17
  57.1 0.1 collective-permute-start.18
  57.1 4.6 %all-to-all-start.1 = ((bf16[8,64,128]{2,1,0:T(8,128)(2,1)}), bf16[8,64,128]{2,1,0:T(8,128)(2,1)S(1)}, u32[]{:S(2)}, u32[]{:S(2)}) async-start(bf16[8,64,128]{2,1,0:T(8,128)(2,1)} %get-tuple-element.62), calls=%async_computation.1 | async-start | bytes 262144 | tf_op jit(solution)/shard_map/all_to_all | solution.py:537
  61.7 0.0 collective-permute-done.13.refs_10_
  61.7 0.0 collective-permute-done.11.refs_7_
  61.8 0.0 collective-permute-done.17.refs_14_
  61.8 0.0 collective-permute-done.18.refs_15_
  61.8 6.0 %shard_map.237 = (f32[64,256]{1,0:T(8,128)S(1)}, f32[64,256]{1,0:T(8,128)S(1)}, f32[8,128]{1,0:T(8,128)S(1)}) custom-call(bf16[256,13824]{1,0:T(8,128)(2,1)} %ptdf.3, bf16[864,128]{1,0:T(8,128)(2,1)S(1)} %copy-done, bf16[864,128]{1,0:T(8,128)(2,1)S(1)} %collective-permute-done.4.refs_1_, bf16[864,128]{1,0:T(8,128)(2,1)S(1)} %collective-permute-done.5.refs_2_, ...), custom_call_target="tpu_custom_call" | custom-call | flops 905969664 | bytes 10616832 | tf_op jit(solution)/shard_map/pallas_call | solution.py:438
  67.8 0.2 collective-permute-start.19
  68.0 1.3 %all-to-all-done.1.bars = bf16[8,64,128]{2,1,0:T(8,128)(2,1)S(1)} async-done(((bf16[8,64,128]{2,1,0:T(8,128)(2,1)}), bf16[8,64,128]{2,1,0:T(8,128)(2,1)S(1)}, u32[]{:S(2)}, u32[]{:S(2)}) %all-to-all-start.1) | async-done | bytes 131104 | tf_op jit(solution)/shard_map/all_to_all | solution.py:537
  69.3 0.0 collective-permute-done.19.flow_o
  69.3 1.4 %shard_map.238 = (f32[8,64,128]{2,1,0:T(8,128)}, f32[72,256]{1,0:T(8,128)S(1)}, f32[72,256]{1,0:T(8,128)S(1)}) custom-call(bf16[8,64,128]{2,1,0:T(8,128)(2,1)S(1)} %all-to-all-done.1.bars, bf16[256,1024]{1,0:T(8,128)(2,1)S(1)} %shard_map.233.cols_m.cols, bf16[256,1024]{1,0:T(8,128)(2,1)S(1)} %collective-permute-done.cols_o, ...), custom_call_target="tpu_custom_call" | custom-call | tf_op jit(solution)/shard_map/pallas_call | solution.py:386
  70.7 5.8 %all-to-all-start.2 = ((f32[8,64,128]{2,1,0:T(8,128)}), f32[8,64,128]{2,1,0:T(8,128)S(1)}, u32[]{:S(2)}, u32[]{:S(2)}) async-start(f32[8,64,128]{2,1,0:T(8,128)} %get-tuple-element.72), calls=%async_computation.2 | async-start | bytes 524288 | tf_op jit(solution)/shard_map/all_to_all | solution.py:555
  76.5 0.0 collective-permute-start.21
  76.5 0.5 collective-permute-start.20
  77.0 0.1 copy.39.par
  77.1 0.8 collective-permute-done.20.state_o
  77.9 0.0 collective-permute-done.21.other
  77.9 0.9 copy-done.3
  78.8 1.1 %shard_map.239 = (f32[256,128]{1,0:T(8,128)S(1)}, f32[64,128]{1,0:T(8,128)S(1)}, f32[64,128]{1,0:T(8,128)S(1)}, f32[64,128]{1,0:T(8,128)S(1)}, f32[256,128]{1,0:...) custom-call(f32[64,5]{1,0:T(8,128)S(1)} %copy.39.par, ...), custom_call_target="tpu_custom_call" | custom-call | tf_op jit(solution)/shard_map/pallas_call | solution.py:386
  80.0 5.8 %all-to-all-done.2.parts = f32[8,64,128]{2,1,0:T(8,128)S(1)} async-done(((f32[8,64,128]{2,1,0:T(8,128)}), f32[8,64,128]{2,1,0:T(8,128)S(1)}, u32[]{:S(2)}, u32[]{:S(2)}) %all-to-all-start.2) | async-done | bytes 262176 | tf_op jit(solution)/shard_map/all_to_all | solution.py:555
  85.7 0.7 shard_map.240
  86.4 10.9 %all_to_all.20.bars_m = bf16[8,64,128]{2,1,0:T(8,128)(2,1)S(1)} all-to-all(bf16[8,64,128]{2,1,0:T(8,128)(2,1)} %get-tuple-element.88), channel_id=1, replica_groups=mesh['grp'=2,'chip'=8,'core'=2] {'chip'}, dimensions={0} | all-to-all | bytes 262144 | tf_op jit(solution)/shard_map/all_to_all | solution.py:570
  97.4 0.0 collective-permute-start.23
  97.4 0.5 collective-permute-start.22
  97.9 0.1 copy.40.limit
  98.0 0.7 collective-permute-done.22.gen_o
  98.8 0.8 shard_map.241
  99.6 1.1 %shard_map.242 = (f32[256,128]{1,0:T(8,128)}, f32[1,8]{1,0:T(1,128)}) custom-call(bf16[8,64,128]{2,1,0:T(8,128)(2,1)S(1)} %all_to_all.20.bars_m, bf16[8,64,128]{2,1,0:T(8,128)(2,1)S(1)} %collective-permute-done.23.bars_o, bf16[256,1024]{1,0:T(8,128)(2,1)S(1)} %shard_map.233.cols_m.cols, f32[256,128]{1,0:T(8,128)S(1)} %get-tuple-element.89.flow, ...), custom_call_target="tpu_custom_call" | custom-call | tf_op jit(solution)/shard_map/pallas_call | solution.py:386
  (30 shorter events, 0.1 us)
Async XLA Ops:
  0.6 10.7 %copy-start = (bf16[864,128]{1,0:T(8,128)(2,1)S(1)}, bf16[864,128]{1,0:T(8,128)(2,1)}, u32[]{:S(2)}) copy-start(bf16[864,128]{1,0:T(8,128)(2,1)} %refs_0_.1) | copy-start | bytes 663556
  0.6 28.7 %copy-start.1 = (f32[256,128]{1,0:T(8,128)S(1)}, f32[256,128]{1,0:T(8,128)}, u32[]{:S(2)}) copy-start(f32[256,128]{1,0:T(8,128)} %dual_m.1) | copy-start | bytes 393220
  0.7 30.2 %copy-start.5 = (f32[8]{0:T(128)S(1)}, f32[8]{0:T(128)}, u32[]{:S(2)}) copy-start(f32[8]{0:T(128)} %param.32) | copy-start | bytes 100
  0.7 37.8 %copy-start.11 = (s32[64]{0:T(128)S(1)}, s32[64]{0:T(128)}, u32[]{:S(2)}) copy-start(s32[64]{0:T(128)} %param.21) | copy-start | bytes 772
  0.7 37.8 %copy-start.6 = (f32[64]{0:T(128)S(1)}, f32[64]{0:T(128)}, u32[]{:S(2)}) copy-start(f32[64]{0:T(128)} %param.22) | copy-start | bytes 772
  0.7 37.8 %copy-start.8 = (f32[64]{0:T(128)S(1)}, f32[64]{0:T(128)}, u32[]{:S(2)}) copy-start(f32[64]{0:T(128)} %param.24) | copy-start | bytes 772
  0.7 37.7 %copy-start.9 = (f32[64]{0:T(128)S(1)}, f32[64]{0:T(128)}, u32[]{:S(2)}) copy-start(f32[64]{0:T(128)} %param.25) | copy-start | bytes 772
  0.7 37.7 %copy-start.10 = (f32[64]{0:T(128)S(1)}, f32[64]{0:T(128)}, u32[]{:S(2)}) copy-start(f32[64]{0:T(128)} %param.26) | copy-start | bytes 772
  0.7 37.9 %copy-start.4 = (f32[256]{0:T(256)S(1)}, f32[256]{0:T(256)}, u32[]{:S(2)}) copy-start(f32[256]{0:T(256)} %param.27) | copy-start | bytes 3076
  0.7 37.9 %copy-start.7 = (f32[64]{0:T(128)S(1)}, f32[64]{0:T(128)}, u32[]{:S(2)}) copy-start(f32[64]{0:T(128)} %param.23) | copy-start | bytes 772
  10.8 21.2 %collective-permute-start = (bf16[256,1024]{1,0:T(8,128)(2,1)S(1)}, bf16[256,1024]{1,0:T(8,128)(2,1)S(1)}, u32[]{:S(2)}, u32[]{:S(2)}) collective-permute-start(bf16[256,1024]{1,0:T(8,128)(2,1)S(1)} %shard_map.233.cols_m.cols), channel_id=1, source_target_pairs={{0,1},{1,0},{2,3},{3,2},{4,5},{5,4},{6,7},{7,6},{8,9},{9,8},{10,11... | collective-permute-start | bytes 1572872 | tf_op jit(solution)/shard_map/ppermute | solution.py:402
  11.3 14.5 %collective-permute-start.8 = (bf16[864,128]{1,0:T(8,128)(2,1)S(1)}, bf16[864,128]{1,0:T(8,128)(2,1)S(1)}, u32[]{:S(2)}, u32[]{:S(2)}) collective-permute-start(bf16[864,128]{1,0:T(8,128)(2,1)S(1)} %copy-done), channel_id=1, source_target_pairs={{0,8},{2,10},{4,12},{6,14},{8,0},{10,2},{12,4},{14,6},{1,9},{3,11}... | collective-permute-start | bytes 663560 | tf_op jit(solution)/shard_map/ppermute | solution.py:488
  15.0 11.1 %collective-permute-start.7 = (bf16[864,128]{1,0:T(8,128)(2,1)S(1)}, bf16[864,128]{1,0:T(8,128)(2,1)S(1)}, u32[]{:S(2)}, u32[]{:S(2)}) collective-permute-start(bf16[864,128]{1,0:T(8,128)(2,1)S(1)} %copy-done), channel_id=1, source_target_pairs={{0,4},{2,6},{4,0},{6,2},{8,12},{10,14},{12,8},{14,10},{1,5},{3,7},... | collective-permute-start | bytes 663560 | tf_op jit(solution)/shard_map/ppermute | solution.py:488
  26.1 10.4 %collective-permute-start.15 = (bf16[864,128]{1,0:T(8,128)(2,1)S(1)}, bf16[864,128]{1,0:T(8,128)(2,1)S(1)}, u32[]{:S(2)}, u32[]{:S(2)}) collective-permute-start(bf16[864,128]{1,0:T(8,128)(2,1)S(1)} %copy-done), channel_id=1, source_target_pairs={{0,12},{2,14},{4,8},{6,10},{8,4},{10,6},{12,0},{14,2},{1,13},{3,15... | collective-permute-start | bytes 663560 | tf_op jit(solution)/shard_map/ppermute | solution.py:488
  29.3 2.7 %collective-permute-start.1 = (f32[256,128]{1,0:T(8,128)S(1)}, f32[256,128]{1,0:T(8,128)S(1)}, u32[]{:S(2)}, u32[]{:S(2)}) collective-permute-start(f32[256,128]{1,0:T(8,128)S(1)} %copy-done.1), channel_id=1, source_target_pairs={{0,1},{1,0},{2,3},{3,2},{4,5},{5,4},{6,7},{7,6},{8,9},{9,8},{10,11... | collective-permute-start | bytes 393224 | tf_op jit(solution)/shard_map/ppermute | solution.py:402
  29.3 13.2 %collective-permute-start.4 = (bf16[864,128]{1,0:T(8,128)(2,1)S(1)}, bf16[864,128]{1,0:T(8,128)(2,1)S(1)}, u32[]{:S(2)}, u32[]{:S(2)}) collective-permute-start(bf16[864,128]{1,0:T(8,128)(2,1)S(1)} %copy-done), channel_id=1, source_target_pairs={{0,2},{2,0},{4,6},{6,4},{8,10},{10,8},{12,14},{14,12},{1,3},{3,1},... | collective-permute-start | bytes 663560 | tf_op jit(solution)/shard_map/ppermute | solution.py:491
  30.8 1.2 %collective-permute-start.2 = (f32[8]{0:T(128)S(1)}, f32[8]{0:T(128)S(1)}, u32[]{:S(2)}, u32[]{:S(2)}) collective-permute-start(f32[8]{0:T(128)S(1)} %copy-done.5), channel_id=1, source_target_pairs={{0,1},{1,0},{2,3},{3,2},{4,5},{5,4},{6,7},{7,6},{8,9},{9,8},{10,11... | collective-permute-start | bytes 104 | tf_op jit(solution)/shard_map/ppermute | solution.py:402
  33.1 14.6 %all-to-all-start = ((f32[8,64,128]{2,1,0:T(8,128)}), f32[8,64,128]{2,1,0:T(8,128)S(1)}, u32[]{:S(2)}, u32[]{:S(2)}) async-start(f32[8,64,128]{2,1,0:T(8,128)} %get-tuple-element.55), calls=%async_computation | async-start | bytes 524288 | tf_op jit(solution)/shard_map/all_to_all | solution.py:515
  36.5 11.2 %collective-permute-start.16 = (bf16[864,128]{1,0:T(8,128)(2,1)S(1)}, bf16[864,128]{1,0:T(8,128)(2,1)S(1)}, u32[]{:S(2)}, u32[]{:S(2)}) collective-permute-start(bf16[864,128]{1,0:T(8,128)(2,1)S(1)} %collective-permute-done.15.refs_12_), channel_id=1, source_target_pairs={{0,2},{2,0},{4,6},{6,4},{8,10},{10,8},{12,14},{14,12},{1,3},{3,1},... | collective-permute-start | bytes 663560 | tf_op jit(solution)/shard_map/ppermute | solution.py:491
  41.2 0.6 copy-start.2
  41.8 2.5 %collective-permute-start.3 = (f32[200,128]{1,0:T(8,128)S(1)}, f32[200,128]{1,0:T(8,128)S(1)}, u32[]{:S(2)}, u32[]{:S(2)}) collective-permute-start(f32[200,128]{1,0:T(8,128)S(1)} %get-tuple-element.60.pack_m), channel_id=1, source_target_pairs={{0,1},{1,0},{2,3},{3,2},{4,5},{5,4},{6,7},{7,6},{8,9},{9,8},{10,11... | collective-permute-start | bytes 307208 | tf_op jit(solution)/shard_map/ppermute | solution.py:402
  41.8 6.8 %collective-permute-start.5 = (bf16[864,128]{1,0:T(8,128)(2,1)S(1)}, bf16[864,128]{1,0:T(8,128)(2,1)S(1)}, u32[]{:S(2)}, u32[]{:S(2)}) collective-permute-start(bf16[864,128]{1,0:T(8,128)(2,1)S(1)} %copy-done), channel_id=1, source_target_pairs={{0,1},{1,0},{2,3},{3,2},{4,5},{5,4},{6,7},{7,6},{8,9},{9,8},{10,11... | collective-permute-start | bytes 663560 | tf_op jit(solution)/shard_map/ppermute | solution.py:402
  42.3 10.1 %collective-permute-start.9 = (bf16[864,128]{1,0:T(8,128)(2,1)S(1)}, bf16[864,128]{1,0:T(8,128)(2,1)S(1)}, u32[]{:S(2)}, u32[]{:S(2)}) collective-permute-start(bf16[864,128]{1,0:T(8,128)(2,1)S(1)} %collective-permute-done.7.refs_4_), channel_id=1, source_target_pairs={{0,2},{2,0},{4,6},{6,4},{8,10},{10,8},{12,14},{14,12},{1,3},{3,1},... | collective-permute-start | bytes 663560 | tf_op jit(solution)/shard_map/ppermute | solution.py:491
  42.5 14.1 %collective-permute-start.12 = (bf16[864,128]{1,0:T(8,128)(2,1)S(1)}, bf16[864,128]{1,0:T(8,128)(2,1)}, u32[]{:S(2)}, u32[]{:S(2)}) collective-permute-start(bf16[864,128]{1,0:T(8,128)(2,1)S(1)} %collective-permute-done.8.refs_8_), channel_id=1, source_target_pairs={{0,2},{2,0},{4,6},{6,4},{8,10},{10,8},{12,14},{14,12},{1,3},{3,1},... | collective-permute-start | bytes 663560 | tf_op jit(solution)/shard_map/ppermute | solution.py:491
  44.4 12.2 %collective-permute-start.6 = (bf16[864,128]{1,0:T(8,128)(2,1)S(1)}, bf16[864,128]{1,0:T(8,128)(2,1)}, u32[]{:S(2)}, u32[]{:S(2)}) collective-permute-start(bf16[864,128]{1,0:T(8,128)(2,1)S(1)} %collective-permute-done.4.refs_1_), channel_id=1, source_target_pairs={{0,1},{1,0},{2,3},{3,2},{4,5},{5,4},{6,7},{7,6},{8,9},{9,8},{10,11... | collective-permute-start | bytes 663560 | tf_op jit(solution)/shard_map/ppermute | solution.py:402
  47.7 9.4 %collective-permute-start.10 = (bf16[864,128]{1,0:T(8,128)(2,1)S(1)}, bf16[864,128]{1,0:T(8,128)(2,1)}, u32[]{:S(2)}, u32[]{:S(2)}) collective-permute-start(bf16[864,128]{1,0:T(8,128)(2,1)S(1)} %collective-permute-done.7.refs_4_), channel_id=1, source_target_pairs={{0,1},{1,0},{2,3},{3,2},{4,5},{5,4},{6,7},{7,6},{8,9},{9,8},{10,11... | collective-permute-start | bytes 663560 | tf_op jit(solution)/shard_map/ppermute | solution.py:402
  48.6 13.1 %collective-permute-start.13 = (bf16[864,128]{1,0:T(8,128)(2,1)S(1)}, bf16[864,128]{1,0:T(8,128)(2,1)}, u32[]{:S(2)}, u32[]{:S(2)}) collective-permute-start(bf16[864,128]{1,0:T(8,128)(2,1)S(1)} %collective-permute-done.8.refs_8_), channel_id=1, source_target_pairs={{0,1},{1,0},{2,3},{3,2},{4,5},{5,4},{6,7},{7,6},{8,9},{9,8},{10,11... | collective-permute-start | bytes 663560 | tf_op jit(solution)/shard_map/ppermute | solution.py:402
  52.5 9.3 %collective-permute-start.11 = (bf16[864,128]{1,0:T(8,128)(2,1)S(1)}, bf16[864,128]{1,0:T(8,128)(2,1)}, u32[]{:S(2)}, u32[]{:S(2)}) collective-permute-start(bf16[864,128]{1,0:T(8,128)(2,1)S(1)} %collective-permute-done.9.refs_5_), channel_id=1, source_target_pairs={{0,1},{1,0},{2,3},{3,2},{4,5},{5,4},{6,7},{7,6},{8,9},{9,8},{10,11... | collective-permute-start | bytes 663560 | tf_op jit(solution)/shard_map/ppermute | solution.py:402
  56.6 5.2 %collective-permute-start.14 = (bf16[864,128]{1,0:T(8,128)(2,1)}, bf16[864,128]{1,0:T(8,128)(2,1)}, u32[]{:S(2)}, u32[]{:S(2)}) collective-permute-start(bf16[864,128]{1,0:T(8,128)(2,1)} %collective-permute-done.12.refs_9_), channel_id=1, source_target_pairs={{0,1},{1,0},{2,3},{3,2},{4,5},{5,4},{6,7},{7,6},{8,9},{9,8},{10,11... | collective-permute-start | bytes 663560 | tf_op jit(solution)/shard_map/ppermute | solution.py:402
  56.6 5.2 %collective-permute-start.17 = (bf16[864,128]{1,0:T(8,128)(2,1)S(1)}, bf16[864,128]{1,0:T(8,128)(2,1)}, u32[]{:S(2)}, u32[]{:S(2)}) collective-permute-start(bf16[864,128]{1,0:T(8,128)(2,1)S(1)} %collective-permute-done.15.refs_12_), channel_id=1, source_target_pairs={{0,1},{1,0},{2,3},{3,2},{4,5},{5,4},{6,7},{7,6},{8,9},{9,8},{10,11... | collective-permute-start | bytes 663560 | tf_op jit(solution)/shard_map/ppermute | solution.py:402
  57.1 4.7 %collective-permute-start.18 = (bf16[864,128]{1,0:T(8,128)(2,1)S(1)}, bf16[864,128]{1,0:T(8,128)(2,1)}, u32[]{:S(2)}, u32[]{:S(2)}) collective-permute-start(bf16[864,128]{1,0:T(8,128)(2,1)S(1)} %collective-permute-done.16.refs_13_), channel_id=1, source_target_pairs={{0,1},{1,0},{2,3},{3,2},{4,5},{5,4},{6,7},{7,6},{8,9},{9,8},{10,11... | collective-permute-start | bytes 663560 | tf_op jit(solution)/shard_map/ppermute | solution.py:402
  57.1 12.2 %all-to-all-start.1 = ((bf16[8,64,128]{2,1,0:T(8,128)(2,1)}), bf16[8,64,128]{2,1,0:T(8,128)(2,1)S(1)}, u32[]{:S(2)}, u32[]{:S(2)}) async-start(bf16[8,64,128]{2,1,0:T(8,128)(2,1)} %get-tuple-element.62), calls=%async_computation.1 | async-start | bytes 262144 | tf_op jit(solution)/shard_map/all_to_all | solution.py:537
  67.8 1.5 %collective-permute-start.19 = (f32[64,256]{1,0:T(8,128)S(1)}, f32[64,256]{1,0:T(8,128)S(1)}, u32[]{:S(2)}, u32[]{:S(2)}) collective-permute-start(f32[64,256]{1,0:T(8,128)S(1)} %get-tuple-element.69.flow_s), channel_id=1, source_target_pairs={{0,1},{1,0},{2,3},{3,2},{4,5},{5,4},{6,7},{7,6},{8,9},{9,8},{10,11... | collective-permute-start | bytes 196616 | tf_op jit(solution)/shard_map/ppermute | solution.py:402
  70.7 15.0 %all-to-all-start.2 = ((f32[8,64,128]{2,1,0:T(8,128)}), f32[8,64,128]{2,1,0:T(8,128)S(1)}, u32[]{:S(2)}, u32[]{:S(2)}) async-start(f32[8,64,128]{2,1,0:T(8,128)} %get-tuple-element.72), calls=%async_computation.2 | async-start | bytes 524288 | tf_op jit(solution)/shard_map/all_to_all | solution.py:555
  76.5 1.4 %collective-permute-start.21 = (f32[72,256]{1,0:T(8,128)S(1)}, f32[72,256]{1,0:T(8,128)S(1)}, u32[]{:S(2)}, u32[]{:S(2)}) collective-permute-start(f32[72,256]{1,0:T(8,128)S(1)} %get-tuple-element.76), channel_id=1, source_target_pairs={{0,1},{1,0},{2,3},{3,2},{4,5},{5,4},{6,7},{7,6},{8,9},{9,8},{10,11... | collective-permute-start | bytes 221192 | tf_op jit(solution)/shard_map/ppermute | solution.py:402
  76.5 1.4 %collective-permute-start.20 = (f32[2,64,128]{2,1,0:T(8,128)S(1)}, f32[2,64,128]{2,1,0:T(8,128)S(1)}, u32[]{:S(2)}, u32[]{:S(2)}) collective-permute-start(f32[2,64,128]{2,1,0:T(8,128)S(1)} %get-tuple-element.80.state_m.state), channel_id=1, source_target_pairs={{0,1},{1,0},{2,3},{3,2},{4,5},{5,4},{6,7},{7,6},{8,9},{9,8},{10,11... | collective-permute-start | bytes 196616 | tf_op jit(solution)/shard_map/ppermute | solution.py:402
  77.9 0.9 copy-start.3
  97.4 2.2 %collective-permute-start.23 = (bf16[8,64,128]{2,1,0:T(8,128)(2,1)S(1)}, bf16[8,64,128]{2,1,0:T(8,128)(2,1)S(1)}, u32[]{:S(2)}, u32[]{:S(2)}) collective-permute-start(bf16[8,64,128]{2,1,0:T(8,128)(2,1)S(1)} %all_to_all.20.bars_m), channel_id=1, source_target_pairs={{0,1},{1,0},{2,3},{3,2},{4,5},{5,4},{6,7},{7,6},{8,9},{9,8},{10,11... | collective-permute-start | bytes 393224 | tf_op jit(solution)/shard_map/ppermute | solution.py:402
  97.4 1.4 %collective-permute-start.22 = (f32[64,128]{1,0:T(8,128)S(1)}, f32[64,128]{1,0:T(8,128)S(1)}, u32[]{:S(2)}, u32[]{:S(2)}) collective-permute-start(f32[64,128]{1,0:T(8,128)S(1)} %get-tuple-element.81.gen_m), channel_id=1, source_target_pairs={{0,1},{1,0},{2,3},{3,2},{4,5},{5,4},{6,7},{7,6},{8,9},{9,8},{10,11... | collective-permute-start | bytes 98312 | tf_op jit(solution)/shard_map/ppermute | solution.py:402
